TPU v7x, 128 devices: a whole 4x4x4 slice. The times are simulated.
128 devices in a mesh: ctx: 32 (over z, x, core), tp: 4 (over y).
Axes of the slice: x: 4, y: 4, z: 4, core: 2. Of those that a mesh axis runs over, the one named last changes fastest.
Arguments:
- tokens: bfloat16 [4096, 4096], P('ctx', 'tp'), may hold values from -6 to 6
- in_weight: bfloat16 [4096, 3, 4096], P('ctx', None, 'tp'), may hold values from -0.09375 to 0.09375
- conv_taps: float32 [3, 3, 4096], P(None, None, 'tp'), may hold values from -2.5 to 2.5
- decay_rate: float32 [16, 4096], P(None, 'tp'), may hold values from 0 to 0.034, as said below
- residue: float32 [16, 4096], P(None, 'tp'), may hold values from -1 to 1
- skip: float32 [4096], P('tp'), may hold values from -1 to 1
Outputs:
- mixed: bfloat16 [4096, 4096], P('ctx', 'tp')
Inputs may be any that keep to these rules, and one draw needn't show every extreme that they name: `decay_rate`: positive decay rates of the poles.
All inputs are finite; a program needn't handle non-finite values.
Results may differ from a plain program's by a relative error of at most 0.0063.
Values may be sent and summed in bfloat16 or wider, within the bound.
A program may use at most 128 MiB of HBM per device.

v0:
```python
import math

import jax
import jax.numpy as jnp
from jax import lax
from jax.sharding import PartitionSpec as P


def passed_along(array, axis, by):
    peers = lax.axis_size(axis)
    pairs = [(i, i + by) for i in range(peers) if 0 <= i + by < peers]
    return lax.ppermute(array, axis, pairs)


def entering(array, axis, combine, identity):
    peers, here = (lax.axis_size(axis), lax.axis_index(axis))
    everything = jax.tree.map(lambda part: lax.all_gather(part, axis), array)
    start = jax.tree.map(
        lambda part, zero: jnp.broadcast_to(jnp.asarray(zero, part.dtype), part.shape),
        array,
        identity,
    )

    def turn(k, before):
        reached = k < here
        new = combine(before, jax.tree.map(lambda part: part[k], everything))
        return jax.tree.map(lambda a, b: jnp.where(reached, a, b), new, before)

    return lax.fori_loop(0, peers, turn, start)


def link(earlier, later):
    return (earlier[0] * later[0], later[0] * earlier[1] + later[1])


def per_device(tokens, in_weight, conv_taps, decay_rate, residue, skip):
    rows = tokens.shape[0]
    chans = in_weight.shape[2]
    whole = lax.all_gather(tokens, "tp", axis=1, tiled=True)
    piece = lax.all_gather(in_weight, "ctx", axis=0, tiled=True)
    sums = tuple(
        (jnp.dot(whole, piece[:, g, :], preferred_element_type=jnp.float32) for g in range(3))
    )
    projected = jnp.stack([total.astype(jnp.bfloat16) for total in sums], axis=0)
    edge_out = passed_along(projected[:, rows - 2 :, :], "ctx", 1)
    extended = jnp.concatenate([edge_out, projected], axis=1)
    values = lax.optimization_barrier(extended).astype(jnp.float32)
    filtered = (
        conv_taps[0][:, None, :] * values[:, 2:, :]
        + conv_taps[1][:, None, :] * values[:, 1:-1, :]
        + conv_taps[2][:, None, :] * values[:, :-2, :]
    )
    query = filtered[0]
    gated = filtered[1] * filtered[2]
    span = math.gcd(rows, 32)
    blocks = rows // span
    offsets = jnp.arange(span, dtype=jnp.float32)
    powers = jnp.exp(-decay_rate[None] * offsets[:, None, None])
    response = jnp.sum(residue[None] * powers, axis=1)
    lags = jnp.arange(span)[:, None] - jnp.arange(span)[None, :]
    toeplitz = jnp.where((lags >= 0)[:, :, None], response[jnp.clip(lags, 0, span - 1)], 0.0)
    blocked = gated.reshape(blocks, span, chans)
    inside = jnp.einsum("tsc,bsc->btc", toeplitz, blocked, precision=lax.Precision.HIGHEST)
    tails = jnp.exp(-decay_rate[None] * (span - 1.0 - offsets)[:, None, None])
    ends = jnp.einsum("spc,bsc->bpc", tails, blocked, precision=lax.Precision.HIGHEST)
    block_decay = jnp.broadcast_to(jnp.exp(-decay_rate * span)[None], ends.shape)
    after = lax.associative_scan(link, (block_decay, ends), axis=0)[1]
    final = after[blocks - 1]
    starts = jnp.concatenate([jnp.zeros_like(after[:1]), after[: blocks - 1]], axis=0)
    segment = jnp.exp(-decay_rate * rows)
    carried = entering(
        (segment, final), "ctx", link, (jnp.ones_like(final), jnp.zeros_like(final))
    )[1]
    block_starts = (span * jnp.arange(blocks, dtype=jnp.float32))[:, None, None]
    begin = starts + jnp.exp(-decay_rate[None] * block_starts) * carried[None]
    leading = residue[None] * jnp.exp(-decay_rate[None] * (offsets + 1.0)[:, None, None])
    convolved = inside + jnp.einsum("tpc,bpc->btc", leading, begin, precision=lax.Precision.HIGHEST)
    convolved = convolved.reshape(rows, chans)
    return (query * (convolved + skip[None, :] * gated)).astype(jnp.bfloat16)


def solution(mesh):
    placed = (
        P("ctx", "tp"),
        P("ctx", None, "tp"),
        P(None, None, "tp"),
        P(None, "tp"),
        P(None, "tp"),
        P("tp"),
    )
    return jax.shard_map(
        per_device, mesh=mesh, in_specs=placed, out_specs=P("ctx", "tp"), check_vma=False
    )
```

profile of v0, /device:TPU:0, one launch (start us, length us, event | category | flops | bytes accessed | tf_op | source)
XLA Modules:
  0.0 290.5 jit_solution(15202066247814389937)
XLA Ops:
  8.1 1.5 multiply_exponential_fusion
  10.4 25.1 %all-gather.6.cloned.1.call-done = bf16[128,4096]{1,0:T(8,128)(2,1)} async-done(((bf16[128,1024]{1,0:T(8,128)(2,1)}), bf16[128,4096]{1,0:T(8,128)(2,1)}) %all-gather.6.cloned.1.call-update) | async-done | bytes 1048592 | tf_op jit(solution)/shard_map/all_gather | solution.py:39
  35.5 94.9 %all-gather.8.cloned.1.call-done = bf16[4096,3,1024]{2,0,1:T(8,128)(2,1)} async-done(((bf16[128,3,1024]{2,0,1:T(8,128)(2,1)}), bf16[4096,3,1024]{2,0,1:T(8,128)(2,1)}) %all-gather.8.cloned.1.call-update) | async-done | bytes 25165840 | tf_op jit(solution)/shard_map/all_gather | solution.py:40
  130.4 5.0 %fusion.27 = bf16[1,128,1024]{2,1,0:T(8,128)(2,1)S(1)} fusion(bf16[128,4096]{1,0:T(8,128)(2,1)} %all-gather.6.cloned.1.call-done, bf16[4096,3,1024]{2,0,1:T(8,128)(2,1)} %all-gather.8.cloned.1.call-done), kind=kOutput, calls=%fused_computation.36 | convolution fusion | flops 1073872896 | bytes 9699328 | tf_op jit(solution)/shard_map/dot_general | solution.py:42
  135.4 4.6 %fusion.28 = bf16[1,128,1024]{2,1,0:T(8,128)(2,1)S(1)} fusion(bf16[128,4096]{1,0:T(8,128)(2,1)S(1)} %copy-done.15, bf16[4096,3,1024]{2,0,1:T(8,128)(2,1)} %all-gather.8.cloned.1.call-done), kind=kOutput, calls=%fused_computation.37 | convolution fusion | flops 1073872896 | bytes 9699328 | tf_op jit(solution)/shard_map/dot_general | solution.py:42
  140.0 4.7 %fusion.29 = bf16[1,128,1024]{2,1,0:T(8,128)(2,1)S(1)} fusion(bf16[128,4096]{1,0:T(8,128)(2,1)S(1)} %copy-done.15, bf16[4096,3,1024]{2,0,1:T(8,128)(2,1)} %all-gather.8.cloned.1.call-done), kind=kOutput, calls=%fused_computation.38 | convolution fusion | flops 1073872896 | bytes 9699328 | tf_op jit(solution)/shard_map/dot_general | solution.py:42
  144.8 2.3 collective-permute-start
  148.7 1.1 copy-done
  150.6 14.8 %fusion.10 = f32[1024,4,16]{2,1,0:T(4,128)} fusion(f32[4,32,1024]{1,0,2:T(4,128)S(1)} %copy.65, f32[32]{0:T(128)S(1)} %iota_subtract_fusion, f32[16,1024]{0,1:T(8,128)S(1)} %copy.62), kind=kOutput, calls=%fused_computation.16 | convolution fusion | flops 25690112 | bytes 852096 | tf_op jit(solution)/shard_map/spc,bsc->bpc/dot_general | solution.py:65
  165.5 1.9 copy.67
  168.2 1.0 copy.61
  169.3 15.3 %multiply_reduce_fusion = f32[32,1024]{0,1:T(8,128)S(1)} fusion(f32[16,1024]{0,1:T(8,128)S(1)} %copy.62, f32[16,1024]{0,1:T(8,128)} %copy.61), kind=kLoop, calls=%fused_computation.20 | loop fusion | flops 1540096 | bytes 262144 | tf_op jit(solution)/shard_map/reduce_sum | solution.py:59
  184.8 5.4 %gather_fusion = f32[1024,1024]{1,0:T(8,128)} fusion(f32[32,1024]{1,0:T(8,128)S(1)} %copy.63, s32[1024]{0:T(1024)S(1)} %broadcast_clamp_fusion), kind=kCustom, calls=%fused_computation | custom fusion | bytes 8392704 | tf_op jit(solution)/shard_map/gather | solution.py:61
  190.3 14.4 %copy.64 = f32[32,32,1024]{1,0,2:T(8,128)} copy(f32[32,32,1024]{2,1,0:T(8,128)} %bitcast.79) | data formatting | bytes 8388608 | tf_op jit(solution)/shard_map/gather | solution.py:61
  205.5 29.7 %fusion.1 = f32[1024,4,32]{2,1,0:T(4,128)} fusion(f32[4,32,1024]{1,0,2:T(4,128)S(1)} %copy.65, f32[32,32,1024]{1,0,2:T(8,128)} %copy.64, pred[32,32]{1,0:T(8,128)(4,1)S(1)} %subtract_compare_fusion), kind=kOutput, calls=%fused_computation.4 | convolution fusion | flops 51380224 | bytes 5243904 | tf_op jit(solution)/shard_map/tsc,bsc->btc/dot_general | solution.py:63
  235.2 30.1 %while.14 = (s32[]{:T(128)}, f32[16,1024]{1,0:T(8,128)S(1)}, s32[]{:T(128)}, f32[32,16,1024]{2,1,0:T(8,128)}, f32[32,16,1024]{2,1,0:T(8,128)}, /*index=5*/s32[]{:T(128)}, s32[]{:T(128)}) while((s32[]{:T(128)}, f32[16,1024]{1,0:T(8,128)S(1)}, s32[]{:T(128)}, f32[32,16,1024]{2,1,0:T(8,128)}, f32[32,16,1024]{2,1,0:T(8,128)}, ...), condition=%wide.region_2.3_spmd.clone, body=%wide.region_1.2_spmd.clone.sunk | while | flops 65540 | bytes 262253 | solution.py:29
  235.3 1.1 fusion.45
  236.4 0.9 fusion.45
  237.3 0.9 fusion.45
  238.2 0.9 fusion.45
  239.2 0.9 fusion.45
  240.1 0.9 fusion.45
  241.0 0.9 fusion.45
  242.0 0.9 fusion.45
  242.9 0.9 fusion.45
  250.4 0.9 fusion.45
  258.8 0.9 fusion.45
  259.8 0.9 fusion.45
  265.4 1.0 multiply_add_fusion
  266.4 1.7 copy.68
  268.2 12.9 %add_bitcast_fusion = f32[4,32,1024]{1,0,2:T(4,128)} fusion(f32[1024,4,32]{2,1,0:T(4,128)S(1)} %copy-done.2, f32[4,16,1024]{1,0,2:T(4,128)} %copy.68, f32[32]{0:T(128)S(1)} %iota_add_fusion, f32[16,1024]{0,1:T(8,128)S(1)} %copy.62, f32[16,1024]{0,1:T(8,128)S(1)} %copy-done.3), kind=kOutput, calls=%fused_computation.27 | convolution fusion | flops 26345472 | bytes 1441920 | tf_op jit(solution)/shard_map/tpc,bpc->btc/dot_general | solution.py:77
  281.1 2.0 copy.69
  (90 shorter events, 25.8 us)
Async XLA Ops:
  6.5 29.0 %all-gather.6.cloned.1.call-start = ((), (), s32[]{:S(2)}) async-start(), calls=%async_computation | async-start | bytes 1310720 | tf_op jit(solution)/shard_map/all_gather | solution.py:39
  7.3 123.1 %all-gather.8.cloned.1.call-start = ((), (), s32[]{:S(2)}) async-start(), calls=%async_computation.1 | async-start | bytes 25952256 | tf_op jit(solution)/shard_map/all_gather | solution.py:40
  8.0 227.2 %all-gather.12.cloned.1.call-start = ((), (), s32[]{:S(2)}) async-start(), calls=%async_computation.3 | async-start | bytes 2162688 | tf_op jit(solution)/shard_map/all_gather | solution.py:17
  9.5 137.6 %copy-start.11 = (f32[16,1024]{1,0:T(8,128)}, f32[16,1024]{1,0:T(8,128)S(1)}, u32[]{:S(2)}) copy-start(f32[16,1024]{1,0:T(8,128)S(1)} %get-tuple-element.144) | copy-start | bytes 196612
  9.6 225.7 %all-gather.10.cloned.1.call-start = ((), (), s32[]{:S(2)}) async-start(), calls=%async_computation.2 | async-start | bytes 2162688 | tf_op jit(solution)/shard_map/all_gather | solution.py:17
  35.5 99.9 %copy-start.15 = (bf16[128,4096]{1,0:T(8,128)(2,1)S(1)}, bf16[128,4096]{1,0:T(8,128)(2,1)}, u32[]{:S(2)}) copy-start(bf16[128,4096]{1,0:T(8,128)(2,1)} %all-gather.6.cloned.1.call-done) | copy-start | bytes 3145732
  144.8 3.0 %collective-permute-start = (bf16[3,2,1024]{2,1,0:T(2,128)(2,1)S(1)}, bf16[3,2,1024]{2,1,0:T(2,128)(2,1)S(1)}, u32[]{:S(2)}, u32[]{:S(2)}) collective-permute-start(bf16[3,2,1024]{2,1,0:T(2,128)(2,1)S(1)} %pad_maximum_fusion.1), channel_id=1, source_target_pairs={{0,4},{4,8},{8,12},{12,16},{16,20},{20,24},{24,28},{28,32},{32,36}... | collective-permute-start | bytes 36872 | tf_op jit(solution)/shard_map/ppermute | solution.py:12
  148.7 1.1 copy-start
  165.5 1.9 copy-start.6
  165.5 2.7 copy-start.13
  167.4 0.8 copy-start.4
  167.5 0.7 copy-start.7
  167.5 0.8 copy-start.9
  190.2 14.5 %copy-start.5 = (f32[1024,4,16]{0,2,1:T(8,128)S(1)}, f32[1024,4,16]{0,2,1:T(8,128)}, u32[]{:S(2)}) copy-start(f32[1024,4,16]{0,2,1:T(8,128)} %copy-done.4) | copy-start | bytes 786436
  190.3 14.5 %copy-start.8 = (f32[1,16,1024]{2,1,0:T(8,128)S(1)}, f32[1,16,1024]{2,1,0:T(8,128)}, u32[]{:S(2)}) copy-start(f32[1,16,1024]{2,1,0:T(8,128)} %copy-done.7) | copy-start | bytes 196612
  190.3 14.5 %copy-start.10 = (f32[1,16,1024]{2,1,0:T(8,128)S(1)}, f32[1,16,1024]{2,1,0:T(8,128)}, u32[]{:S(2)}) copy-start(f32[1,16,1024]{2,1,0:T(8,128)} %copy-done.9) | copy-start | bytes 196612
  205.5 59.8 %copy-start.12 = (f32[16,1024]{1,0:T(8,128)S(1)}, f32[16,1024]{1,0:T(8,128)}, u32[]{:S(2)}) copy-start(f32[16,1024]{1,0:T(8,128)} %copy-done.11) | copy-start | bytes 196612
  235.2 32.9 %copy-start.2 = (f32[1024,4,32]{2,1,0:T(4,128)S(1)}, f32[1024,4,32]{2,1,0:T(4,128)}, u32[]{:S(2)}) copy-start(f32[1024,4,32]{2,1,0:T(4,128)} %fusion.1) | copy-start | bytes 1572868
  235.2 32.9 %copy-start.3 = (f32[16,1024]{0,1:T(8,128)S(1)}, f32[16,1024]{0,1:T(8,128)}, u32[]{:S(2)}) copy-start(f32[16,1024]{0,1:T(8,128)} %copy.61) | copy-start | bytes 196612
  281.1 2.0 copy-start.1
  281.1 2.0 copy-start.14
Sparse Core Ops, SparseCore 0:
  9.0 26.4 all-gather.5
  37.8 92.5 all-gather.7
  132.7 43.2 all-gather.11
  178.1 43.2 all-gather.9
where the time goes:
time: 295 us; the launch traced here: 290 us
  waiting for transfers between devices  122 us (41%)
  matrix products  71.7 us (24%)
  other arithmetic  49.9 us (17%)
  local copies, waits for them, and re-layouts  30.4 us (10%)
  between operations  13.5 us (5%)
    all_gather x1, waiting for transfers between devices, per_device(): piece = lax.all_gather(in_weight, 'ctx', axis=0, tiled=True)  94.9 us
    dot_general x1, matrix products, per_device(): jnp.einsum('tsc,bsc->btc', toeplitz, blocked, precision=lax.Precision.HIG...  29.7 us
    select_n x32, other arithmetic, turn(): return jax.tree.map(lambda a, b: jnp.where(reached, a, b), new, before)  29.4 us
    all_gather x1, waiting for transfers between devices, per_device(): whole = lax.all_gather(tokens, 'tp', axis=1, tiled=True)  25.1 us
    gather x2, local copies, waits for them, and re-layouts, per_device(): response[jnp.clip(lags, 0, span - 1)]  19.8 us
    reduce_sum x1, other arithmetic, per_device(): response = jnp.sum(residue[None] * powers, axis=1)  15.3 us
    dot_general x1, matrix products, per_device(): jnp.einsum('spc,bsc->bpc', tails, blocked, precision=lax.Precision.HIGHEST)  14.8 us
    dot_general x3, matrix products, per_device(): jnp.dot(whole, piece[:, g, :], preferred_element_type=jnp.float32)  14.3 us
  transfers between devices with their start and end apart: 5, of which 3 were waited for; matrix products, arithmetic and copies ran while one was open for 35% of the time, Pallas kernels for 0%

commit v1 on v0

v1 whole, which is shorter than its diff:
```python
import jax
import jax.numpy as jnp
from jax import lax
from jax.experimental import pallas as pl
from jax.experimental.pallas import tpu as pltpu
from jax.sharding import PartitionSpec as P

LANES = 128


def passed_along(array, axis, by):
    peers = lax.axis_size(axis)
    pairs = [(i, i + by) for i in range(peers) if 0 <= i + by < peers]
    return lax.ppermute(array, axis, pairs)


def filtered_at(x_ref, taps_ref, g, t):
    return (
        taps_ref[0, g] * x_ref[g, t + 2]
        + taps_ref[1, g] * x_ref[g, t + 1]
        + taps_ref[2, g] * x_ref[g, t]
    )


def local_end_kernel(x_ref, taps_ref, decay_ref, end_ref):
    rows = x_ref.shape[1] - 2

    def step(t, state):
        gated = filtered_at(x_ref, taps_ref, 1, t) * filtered_at(x_ref, taps_ref, 2, t)
        return decay_ref[...] * state + gated[None]

    end_ref[...] = lax.fori_loop(
        0, rows, step, jnp.zeros(end_ref.shape, jnp.float32), unroll=8
    )


def mixed_kernel(
    x_ref, taps_ref, decay_ref, resid_ref, skip_ref, ends_ref, span_ref, here_ref, out_ref
):
    rows = x_ref.shape[1] - 2
    here = here_ref[0]

    def gather_carry(k, carry):
        later = span_ref[...] * carry + ends_ref[k]
        return jnp.where(k < here, later, carry)

    start = lax.fori_loop(
        0, ends_ref.shape[0], gather_carry, jnp.zeros(decay_ref.shape, jnp.float32)
    )

    def step(t, state):
        query = filtered_at(x_ref, taps_ref, 0, t)
        gated = filtered_at(x_ref, taps_ref, 1, t) * filtered_at(x_ref, taps_ref, 2, t)
        state = decay_ref[...] * state + gated[None]
        convolved = jnp.sum(resid_ref[...] * state, axis=0)
        out_ref[t] = query * (convolved + skip_ref[...] * gated)
        return state

    lax.fori_loop(0, rows, step, start, unroll=8)


def vmem_specs(n):
    return [pl.BlockSpec(memory_space=pltpu.VMEM)] * n


def per_device(tokens, in_weight, conv_taps, decay_rate, residue, skip):
    rows = tokens.shape[0]
    chans = in_weight.shape[2]
    poles = decay_rate.shape[0]
    subl = chans // LANES
    whole = lax.all_gather(tokens, "tp", axis=1, tiled=True)
    piece = lax.all_gather(in_weight, "ctx", axis=0, tiled=True)
    sums = tuple(
        (jnp.dot(whole, piece[:, g, :], preferred_element_type=jnp.float32) for g in range(3))
    )
    projected = jnp.stack([total.astype(jnp.bfloat16) for total in sums], axis=0)
    edge_out = passed_along(projected[:, rows - 2 :, :], "ctx", 1)
    extended = jnp.concatenate([edge_out, projected], axis=1)
    values = lax.optimization_barrier(extended).astype(jnp.float32)
    x = values.reshape(3, rows + 2, subl, LANES)
    taps = conv_taps.reshape(3, 3, subl, LANES)
    decay = jnp.exp(-decay_rate).reshape(poles, subl, LANES)
    span = jnp.exp(-decay_rate * float(rows)).reshape(poles, subl, LANES)
    resid = residue.reshape(poles, subl, LANES)
    direct = skip.reshape(subl, LANES)

    end = pl.pallas_call(
        local_end_kernel,
        out_shape=jax.ShapeDtypeStruct((poles, subl, LANES), jnp.float32),
        in_specs=vmem_specs(3),
        out_specs=pl.BlockSpec(memory_space=pltpu.VMEM),
    )(x, taps, decay)
    ends = lax.all_gather(end, "ctx", axis=0)
    here = lax.axis_index("ctx").astype(jnp.int32).reshape(1)
    out = pl.pallas_call(
        mixed_kernel,
        out_shape=jax.ShapeDtypeStruct((rows, subl, LANES), jnp.float32),
        in_specs=vmem_specs(7) + [pl.BlockSpec(memory_space=pltpu.SMEM)],
        out_specs=pl.BlockSpec(memory_space=pltpu.VMEM),
    )(x, taps, decay, resid, direct, ends, span, here)
    return out.reshape(rows, chans).astype(jnp.bfloat16)


def solution(mesh):
    placed = (
        P("ctx", "tp"),
        P("ctx", None, "tp"),
        P(None, None, "tp"),
        P(None, "tp"),
        P(None, "tp"),
        P("tp"),
    )
    return jax.shard_map(
        per_device, mesh=mesh, in_specs=placed, out_specs=P("ctx", "tp"), check_vma=False
    )
```

time: 295 us -> 213 us (0.72); the launches traced: 290 us -> 212 us
  matrix products: 71.7 us -> 14.3 us
  other arithmetic: 49.9 us -> 1.32 us
  waiting for transfers between devices: 122 us -> 168 us
  local copies, waits for them, and re-layouts: 30.4 us -> 4.83 us
  Pallas kernels: 0 us -> 7.75 us
    dot_general x3 -> x0, matrix products: 57.4 us -> none  [the longest x1 29.7 us: per_device(): jnp.einsum('tsc,bsc->btc', toeplitz, blocked, precision=lax.Precision.HIG...]
    all_gather x2 -> x1, waiting for transfers between devices: 0.01 us -> 44.5 us  [per_device(): ends = lax.all_gather(end, 'ctx', axis=0)]
    select_n x33 -> x0, other arithmetic: 29.5 us -> none  [the longest x32 29.4 us: turn(): return jax.tree.map(lambda a, b: jnp.where(reached, a, b), new, before)]
    gather x2 -> x0, local copies, waits for them, and re-layouts: 19.8 us -> none  [per_device(): response[jnp.clip(lags, 0, span - 1)]]
    reduce_sum x1 -> x0, other arithmetic: 15.3 us -> none  [per_device(): response = jnp.sum(residue[None] * powers, axis=1)]
    pallas_call x0 -> x2, Pallas kernels: none -> 7.75 us  [the longest x1 4.88 us: per_device(): pl.pallas_call(mixed_kernel, out_shape=jax.ShapeDtypeStruct((rows, subl,...]
    add x2 -> x0, local copies, waits for them, and re-layouts: 3.69 us -> none  [the longest x1 1.96 us: per_device(): inside + jnp.einsum('tpc,bpc->btc', leading, begin, precision=lax.Precisi...]
  transfers between devices with their start and end apart: 5 -> 4, of which waited for: 3 -> 3; matrix products, arithmetic and copies ran while one was open for 35% -> 1% of each run, Pallas kernels for 0% -> 0%
where the time goes in v1:
time: 213 us; the launch traced here: 212 us
  waiting for transfers between devices  168 us (79%)
  matrix products  14.3 us (7%)
  between operations  13.2 us (6%)
  Pallas kernels  7.75 us (4%)
  local copies, waits for them, and re-layouts  4.83 us (2%)
  starting transfers between devices  2.24 us (1%)
    all_gather x1, waiting for transfers between devices, per_device(): piece = lax.all_gather(in_weight, 'ctx', axis=0, tiled=True)  94.9 us
    all_gather x1, waiting for transfers between devices, per_device(): ends = lax.all_gather(end, 'ctx', axis=0)  44.5 us
    all_gather x1, waiting for transfers between devices, per_device(): whole = lax.all_gather(tokens, 'tp', axis=1, tiled=True)  27.4 us
    dot_general x3, matrix products, per_device(): jnp.dot(whole, piece[:, g, :], preferred_element_type=jnp.float32)  14.3 us
    pallas_call x1, Pallas kernels, per_device(): pl.pallas_call(mixed_kernel, out_shape=jax.ShapeDtypeStruct((rows, subl,...  4.88 us
  transfers between devices with their start and end apart: 4, of which 3 were waited for; matrix products, arithmetic and copies ran while one was open for 1% of the time, Pallas kernels for 0%

profile of v1, /device:TPU:0, one launch (start us, length us, event | category | flops | bytes accessed | tf_op | source)
XLA Modules:
  0.0 211.9 jit_solution(8602979145075272299)
XLA Ops:
  6.5 0.0 all-gather.5.cloned.1.call-start
  6.5 0.7 all-gather.5.cloned.1.call-update
  7.3 0.0 all-gather.7.cloned.1.call-start
  7.3 0.7 all-gather.7.cloned.1.call-update
  8.0 0.0 all-gather.9.cloned.1.call-start
  8.1 27.4 %all-gather.5.cloned.1.call-done = bf16[128,4096]{1,0:T(8,128)(2,1)} async-done(((bf16[128,1024]{1,0:T(8,128)(2,1)}), bf16[128,4096]{1,0:T(8,128)(2,1)}) %all-gather.5.cloned.1.call-update) | async-done | bytes 1048592 | tf_op jit(solution)/shard_map/all_gather | solution.py:71
  35.5 0.0 copy-start.3
  35.5 94.9 %all-gather.7.cloned.1.call-done = bf16[4096,3,1024]{2,0,1:T(8,128)(2,1)} async-done(((bf16[128,3,1024]{2,0,1:T(8,128)(2,1)}), bf16[4096,3,1024]{2,0,1:T(8,128)(2,1)}) %all-gather.7.cloned.1.call-update) | async-done | bytes 25165840 | tf_op jit(solution)/shard_map/all_gather | solution.py:72
  130.4 5.0 %fusion.6 = bf16[1,128,1024]{2,1,0:T(8,128)(2,1)S(1)} fusion(bf16[128,4096]{1,0:T(8,128)(2,1)} %all-gather.5.cloned.1.call-done, bf16[4096,3,1024]{2,0,1:T(8,128)(2,1)} %all-gather.7.cloned.1.call-done), kind=kOutput, calls=%fused_computation.9 | convolution fusion | flops 1073872896 | bytes 9699328 | tf_op jit(solution)/shard_map/dot_general | solution.py:74
  135.4 0.0 copy-done.3
  135.4 4.6 %fusion.7 = bf16[1,128,1024]{2,1,0:T(8,128)(2,1)S(1)} fusion(bf16[128,4096]{1,0:T(8,128)(2,1)S(1)} %copy-done.3, bf16[4096,3,1024]{2,0,1:T(8,128)(2,1)} %all-gather.7.cloned.1.call-done), kind=kOutput, calls=%fused_computation.10 | convolution fusion | flops 1073872896 | bytes 9699328 | tf_op jit(solution)/shard_map/dot_general | solution.py:74
  140.0 0.0 copy-start
  140.0 0.0 copy-start.2
  140.1 0.0 copy-start.1
  140.1 4.7 %fusion.8 = bf16[1,128,1024]{2,1,0:T(8,128)(2,1)S(1)} fusion(bf16[128,4096]{1,0:T(8,128)(2,1)S(1)} %copy-done.3, bf16[4096,3,1024]{2,0,1:T(8,128)(2,1)} %all-gather.7.cloned.1.call-done), kind=kOutput, calls=%fused_computation.11 | convolution fusion | flops 1073872896 | bytes 9699328 | tf_op jit(solution)/shard_map/dot_general | solution.py:74
  144.8 2.2 %collective-permute-start = (bf16[3,2,1024]{2,1,0:T(2,128)(2,1)S(1)}, bf16[3,2,1024]{2,1,0:T(2,128)(2,1)S(1)}, u32[]{:S(2)}, u32[]{:S(2)}) collective-permute-start(bf16[3,2,1024]{2,1,0:T(2,128)(2,1)S(1)} %pad_maximum_fusion), channel_id=1, source_target_pairs={{0,4},{4,8},{8,12},{12,16},{16,20},{20,24},{24,28},{28,32},{32,36}... | collective-permute-start | bytes 36872 | tf_op jit(solution)/shard_map/ppermute | solution.py:14
  147.0 0.0 copy-done
  147.0 0.6 copy.7
  147.6 0.0 copy-done.2
  147.6 0.6 reshape.27.taps_ref
  148.3 0.0 collective-permute-done
  148.3 0.2 maximum_maximum_fusion
  148.5 1.5 reshape.34.x_ref
  150.0 2.9 %shard_map.64 = f32[16,8,128]{2,1,0:T(8,128)} custom-call(f32[3,130,8,128]{3,2,1,0:T(8,128)} %reshape.34.x_ref, f32[3,3,8,128]{3,2,1,0:T(8,128)} %reshape.27.taps_ref, f32[16,8,128]{2,1,0:T(8,128)} %bitcast.47), custom_call_target="tpu_custom_call" | custom-call | tf_op jit(solution)/shard_map/pallas_call | solution.py:87
  152.9 0.0 all-gather.9.cloned.1.call-update
  152.9 0.6 copy.9
  153.5 0.0 copy-done.1
  153.6 0.6 copy.8
  154.2 44.5 %all-gather.9.cloned.1.call-done = f32[512,8,128]{2,1,0:T(8,128)} async-done(((f32[16,8,128]{2,1,0:T(8,128)}), f32[512,8,128]{2,1,0:T(8,128)}) %all-gather.9.cloned.1.call-update) | async-done | bytes 2097168 | tf_op jit(solution)/shard_map/all_gather | solution.py:93
  198.7 4.9 %shard_map.65 = f32[128,8,128]{2,1,0:T(8,128)} custom-call(f32[3,130,8,128]{3,2,1,0:T(8,128)} %reshape.34.x_ref, f32[3,3,8,128]{3,2,1,0:T(8,128)} %reshape.27.taps_ref, f32[16,8,128]{2,1,0:T(8,128)} %bitcast.48, f32[16,8,128]{2,1,0:T(8,128)} %bitcast.50, f32[8,128]{1,0:T(8,128)} %bitcast.52, f32[32,16,8,128]{3,2,1,0:T(8,128)} %bitcast.45, ...), custom_call_target="tpu_custom_call" | custom-call | tf_op jit(solution)/shard_map/pallas_call | solution.py:95
  203.6 1.1 convert_element_type.19
  204.6 0.8 copy.12
  (2 shorter events, 0.0 us)
Async XLA Ops:
  6.5 29.0 %all-gather.5.cloned.1.call-start = ((), (), s32[]{:S(2)}) async-start(), calls=%async_computation | async-start | bytes 1310720 | tf_op jit(solution)/shard_map/all_gather | solution.py:71
  7.3 123.1 %all-gather.7.cloned.1.call-start = ((), (), s32[]{:S(2)}) async-start(), calls=%async_computation.1 | async-start | bytes 25952256 | tf_op jit(solution)/shard_map/all_gather | solution.py:72
  8.0 190.7 %all-gather.9.cloned.1.call-start = ((), (), s32[]{:S(2)}) async-start(), calls=%async_computation.2 | async-start | bytes 2162688 | tf_op jit(solution)/shard_map/all_gather | solution.py:93
  35.5 99.9 %copy-start.3 = (bf16[128,4096]{1,0:T(8,128)(2,1)S(1)}, bf16[128,4096]{1,0:T(8,128)(2,1)}, u32[]{:S(2)}) copy-start(bf16[128,4096]{1,0:T(8,128)(2,1)} %all-gather.5.cloned.1.call-done) | copy-start | bytes 3145732
  140.0 6.9 %copy-start = (f32[16,1024]{1,0:T(8,128)S(1)}, f32[16,1024]{1,0:T(8,128)}, u32[]{:S(2)}) copy-start(f32[16,1024]{1,0:T(8,128)} %param.9) | copy-start | bytes 196612
  140.0 7.6 %copy-start.2 = (f32[3,3,1024]{2,1,0:T(4,128)S(1)}, f32[3,3,1024]{2,1,0:T(4,128)}, u32[]{:S(2)}) copy-start(f32[3,3,1024]{2,1,0:T(4,128)} %param.8) | copy-start | bytes 110596
  140.1 13.5 %copy-start.1 = (f32[16,1024]{1,0:T(8,128)S(1)}, f32[16,1024]{1,0:T(8,128)}, u32[]{:S(2)}) copy-start(f32[16,1024]{1,0:T(8,128)} %param.10) | copy-start | bytes 196612
  144.8 3.5 %collective-permute-start = (bf16[3,2,1024]{2,1,0:T(2,128)(2,1)S(1)}, bf16[3,2,1024]{2,1,0:T(2,128)(2,1)S(1)}, u32[]{:S(2)}, u32[]{:S(2)}) collective-permute-start(bf16[3,2,1024]{2,1,0:T(2,128)(2,1)S(1)} %pad_maximum_fusion), channel_id=1, source_target_pairs={{0,4},{4,8},{8,12},{12,16},{16,20},{20,24},{24,28},{28,32},{32,36}... | collective-permute-start | bytes 36872 | tf_op jit(solution)/shard_map/ppermute | solution.py:14
Sparse Core Ops, SparseCore 0:
  9.0 26.4 all-gather.4
  37.8 92.5 all-gather.6
  153.0 45.6 all-gather.8

commit v2 on v1

v2 whole, which is shorter than its diff:
```python
import jax
import jax.numpy as jnp
from jax import lax
from jax.experimental import pallas as pl
from jax.experimental.pallas import tpu as pltpu
from jax.sharding import PartitionSpec as P

LANES = 128


def filtered_at(x_ref, taps_ref, g, t):
    return (
        taps_ref[0, g] * x_ref[g, t + 2]
        + taps_ref[1, g] * x_ref[g, t + 1]
        + taps_ref[2, g] * x_ref[g, t]
    )


def local_end_kernel(x_ref, taps_ref, decay_ref, end_ref):
    rows = x_ref.shape[1] - 2

    def step(t, state):
        gated = filtered_at(x_ref, taps_ref, 1, t) * filtered_at(x_ref, taps_ref, 2, t)
        return decay_ref[...] * state + gated[None]

    end_ref[...] = lax.fori_loop(
        0, rows, step, jnp.zeros(end_ref.shape, jnp.float32), unroll=8
    )


def mixed_kernel(x_ref, taps_ref, decay_ref, resid_ref, skip_ref, start_ref, out_ref):
    rows = x_ref.shape[1] - 2

    def step(t, state):
        query = filtered_at(x_ref, taps_ref, 0, t)
        gated = filtered_at(x_ref, taps_ref, 1, t) * filtered_at(x_ref, taps_ref, 2, t)
        state = decay_ref[...] * state + gated[None]
        convolved = jnp.sum(resid_ref[...] * state, axis=0)
        out_ref[t] = query * (convolved + skip_ref[...] * gated)
        return state

    lax.fori_loop(0, rows, step, start_ref[...], unroll=8)


def vmem_specs(n):
    return [pl.BlockSpec(memory_space=pltpu.VMEM)] * n


def shifted(array, axes, by):
    peers = 1
    for axis in axes:
        peers *= lax.axis_size(axis)
    pairs = [(i, i + by) for i in range(peers) if i + by < peers]
    return lax.ppermute(array, axes, pairs)


def swapped(array, axis):
    return lax.ppermute(array, axis, [(0, 1), (1, 0)])


def gathered_tp(tokens):
    peers, here = lax.axis_size("tp"), lax.axis_index("tp")
    blocks = [tokens]
    for by in range(1, peers):
        blocks.append(lax.ppermute(tokens, "tp", [(i, (i + by) % peers) for i in range(peers)]))
    stacked = jnp.stack(blocks, axis=0)
    order = (here - jnp.arange(peers)) % peers
    placed = jnp.take(stacked, jnp.argsort(order), axis=0)
    return jnp.transpose(placed, (1, 0, 2)).reshape(tokens.shape[0], -1)


def per_device(tokens, in_weight, conv_taps, decay_rate, residue, skip):
    ctx = ("cx", "core")
    rows = tokens.shape[0]
    chans = in_weight.shape[2]
    poles = decay_rate.shape[0]
    subl = chans // LANES
    core = lax.axis_index("core")
    piece = lax.all_gather(in_weight, "cx", axis=0, tiled=True)
    whole = gathered_tp(tokens)
    split = whole.reshape(rows, -1, 2, in_weight.shape[0])
    mine = jnp.where(core == 0, split[:, :, 0], split[:, :, 1]).reshape(rows, -1)
    theirs = jnp.where(core == 0, split[:, :, 1], split[:, :, 0]).reshape(rows, -1)
    both = jnp.concatenate([mine, swapped(theirs, "core")], axis=0)
    partial = jnp.stack(
        [jnp.dot(both, piece[:, g, :], preferred_element_type=jnp.float32) for g in range(3)],
        axis=0,
    )
    sums = partial[:, :rows] + swapped(partial[:, rows:], "core")
    projected = sums.astype(jnp.bfloat16)
    edge_out = shifted(projected[:, rows - 2 :, :], ctx, 1)
    extended = jnp.concatenate([edge_out, projected], axis=1)
    values = lax.optimization_barrier(extended).astype(jnp.float32)
    x = values.reshape(3, rows + 2, subl, LANES)
    taps = conv_taps.reshape(3, 3, subl, LANES)
    decay = jnp.exp(-decay_rate).reshape(poles, subl, LANES)
    resid = residue.reshape(poles, subl, LANES)
    direct = skip.reshape(subl, LANES)

    end = pl.pallas_call(
        local_end_kernel,
        out_shape=jax.ShapeDtypeStruct((poles, subl, LANES), jnp.float32),
        in_specs=vmem_specs(3),
        out_specs=pl.BlockSpec(memory_space=pltpu.VMEM),
    )(x, taps, decay)
    start = shifted(end, ctx, 1)
    peers = lax.axis_size("cx") * lax.axis_size("core")
    by = 1
    while by < peers:
        span = jnp.exp(-decay_rate * float(rows * by)).reshape(poles, subl, LANES)
        start = start + span * shifted(start, ctx, by)
        by *= 2
    out = pl.pallas_call(
        mixed_kernel,
        out_shape=jax.ShapeDtypeStruct((rows, subl, LANES), jnp.float32),
        in_specs=vmem_specs(6),
        out_specs=pl.BlockSpec(memory_space=pltpu.VMEM),
    )(x, taps, decay, resid, direct, start)
    return out.reshape(rows, chans).astype(jnp.bfloat16)


def solution(mesh):
    ctx, tp = mesh.shape["ctx"], mesh.shape["tp"]
    split = jax.sharding.Mesh(mesh.devices.reshape(ctx // 2, 2, tp), ("cx", "core", "tp"))
    c = ("cx", "core")
    placed = (
        P(c, "tp"),
        P(c, None, "tp"),
        P(None, None, "tp"),
        P(None, "tp"),
        P(None, "tp"),
        P("tp"),
    )
    return jax.shard_map(
        per_device, mesh=split, in_specs=placed, out_specs=P(c, "tp"), check_vma=False
    )
```

time: 213 us -> 188 us (0.88)
  waiting for transfers between devices: 168 us -> 98.7 us
  starting transfers between devices: 2.24 us -> 47.4 us
  matrix products: 14.3 us -> 10.4 us
  other arithmetic: 1.32 us -> 4.87 us
    all_gather x3 -> x1, waiting for transfers between devices: 167 us -> 73.8 us  [per_device(): piece = lax.all_gather(in_weight, 'cx', axis=0, tiled=True)]
    ppermute x1 -> x12, starting transfers between devices: 2.16 us -> 47.4 us  [the longest x7 41.3 us: shifted(): return lax.ppermute(array, axes, pairs)]
    ppermute x1 -> x12, waiting for transfers between devices: 0.01 us -> 24.2 us  [the longest x3 9.71 us: gathered_tp(): lax.ppermute(tokens, 'tp', [(i, (i + by) % peers) for i in range(peers)])]
    dot_general x3, matrix products: 14.3 us -> 10.4 us  [per_device(): jnp.dot(both, piece[:, g, :], preferred_element_type=jnp.float32)]
  transfers between devices with their start and end apart: 4 -> 13, of which waited for: 3 -> 11; matrix products, arithmetic and copies ran while one was open for 1% -> 3% of each run, Pallas kernels for 0% -> 0%
where the time goes in v2:
time: 188 us
  waiting for transfers between devices  98.7 us (52%)
  starting transfers between devices  47.4 us (25%)
  between operations  13.7 us (7%)
  matrix products  10.4 us (6%)
  Pallas kernels  6.79 us (4%)
  local copies, waits for them, and re-layouts  5.73 us (3%)
  other arithmetic  4.87 us (3%)
    all_gather x1, waiting for transfers between devices, per_device(): piece = lax.all_gather(in_weight, 'cx', axis=0, tiled=True)  73.8 us
    ppermute x7, starting transfers between devices, shifted(): return lax.ppermute(array, axes, pairs)  41.3 us
    dot_general x3, matrix products, per_device(): jnp.dot(both, piece[:, g, :], preferred_element_type=jnp.float32)  10.4 us
    ppermute x3, waiting for transfers between devices, gathered_tp(): lax.ppermute(tokens, 'tp', [(i, (i + by) % peers) for i in range(peers)])  9.71 us
    ppermute x7, waiting for transfers between devices, shifted(): return lax.ppermute(array, axes, pairs)  9.21 us
    ppermute x3, starting transfers between devices, gathered_tp(): lax.ppermute(tokens, 'tp', [(i, (i + by) % peers) for i in range(peers)])  5.98 us
    ppermute x2, waiting for transfers between devices, swapped(): return lax.ppermute(array, axis, [(0, 1), (1, 0)])  5.29 us
    pallas_call x1, Pallas kernels, per_device(): pl.pallas_call(mixed_kernel, out_shape=jax.ShapeDtypeStruct((rows, subl,...  3.9 us
  transfers between devices with their start and end apart: 13, of which 11 were waited for; matrix products, arithmetic and copies ran while one was open for 3% of the time, Pallas kernels for 0%

profile of v2, /device:TPU:0, one launch (start us, length us, event | category | flops | bytes accessed | tf_op | source)
XLA Modules:
  0.0 187.6 jit_solution(15734455623509639714)
XLA Ops:
  6.5 0.7 all-gather.2.cloned.1.call-update
  7.3 1.7 collective-permute-start
  9.0 2.9 %collective-permute-start.1 = (bf16[128,1024]{1,0:T(8,128)(2,1)}, bf16[128,1024]{1,0:T(8,128)(2,1)S(1)}, u32[]{:S(2)}, u32[]{:S(2)}) collective-permute-start(bf16[128,1024]{1,0:T(8,128)(2,1)} %param.6), channel_id=1, source_target_pairs={{0,2},{1,3},{2,0},{3,1},{4,6},{5,7},{6,4},{7,5},{8,10},{9,11},{10,... | collective-permute-start | bytes 786440 | tf_op jit(solution)/shard_map/ppermute | solution.py:65
  11.9 1.3 collective-permute-start.2
  13.2 0.7 sort.17
  14.0 2.9 %collective-permute-done = bf16[128,1024]{1,0:T(8,128)(2,1)S(1)} collective-permute-done((bf16[128,1024]{1,0:T(8,128)(2,1)}, bf16[128,1024]{1,0:T(8,128)(2,1)S(1)}, u32[]{:S(2)}, u32[]{:S(2)}) %collective-permute-start) | collective-permute-done | bytes 262176 | tf_op jit(solution)/shard_map/ppermute | solution.py:65
  16.9 6.8 %collective-permute-done.1 = bf16[128,1024]{1,0:T(8,128)(2,1)S(1)} collective-permute-done((bf16[128,1024]{1,0:T(8,128)(2,1)}, bf16[128,1024]{1,0:T(8,128)(2,1)S(1)}, u32[]{:S(2)}, u32[]{:S(2)}) %collective-permute-start.1) | collective-permute-done | bytes 262176 | tf_op jit(solution)/shard_map/ppermute | solution.py:65
  23.7 1.1 pad_maximum_fusion.1
  26.5 1.9 %collective-permute-done.3 = bf16[128,2048]{0,1:T(8,128)(2,1)S(1)} collective-permute-done((bf16[128,2048]{0,1:T(8,128)(2,1)S(1)}, bf16[128,2048]{0,1:T(8,128)(2,1)S(1)}, u32[]{:S(2)}, u32[]{:S(2)}) %collective-permute-start.3) | collective-permute-done | bytes 524320 | tf_op jit(solution)/shard_map/ppermute | solution.py:58
  28.4 73.8 %all-gather.2.cloned.1.call-done = bf16[2048,3,1024]{2,0,1:T(8,128)(2,1)} async-done(((bf16[128,3,1024]{2,0,1:T(8,128)(2,1)}), bf16[2048,3,1024]{2,0,1:T(8,128)(2,1)}) %all-gather.2.cloned.1.call-update) | async-done | bytes 12582928 | tf_op jit(solution)/shard_map/all_gather | solution.py:79
  102.2 3.5 %fusion.4 = f32[1,256,1024]{2,1,0:T(8,128)S(1)} fusion(bf16[2048,3,1024]{2,0,1:T(8,128)(2,1)} %all-gather.2.cloned.1.call-done, bf16[128,2048]{0,1:T(8,128)(2,1)S(1)} %collective-permute-done.3, bf16[128,2048]{0,1:T(8,128)(2,1)S(1)} %bitcast.74), kind=kOutput, calls=%fused_computation.10 | convolution fusion | flops 1075838976 | bytes 6291456 | tf_op jit(solution)/shard_map/dot_general | solution.py:86
  105.6 3.5 %fusion.5 = f32[1,256,1024]{2,1,0:T(8,128)S(1)} fusion(bf16[2048,3,1024]{2,0,1:T(8,128)(2,1)} %all-gather.2.cloned.1.call-done, bf16[128,2048]{0,1:T(8,128)(2,1)S(1)} %collective-permute-done.3, bf16[128,2048]{0,1:T(8,128)(2,1)S(1)} %bitcast.75), kind=kOutput, calls=%fused_computation.11 | convolution fusion | flops 1075838976 | bytes 6291456 | tf_op jit(solution)/shard_map/dot_general | solution.py:86
  109.1 3.5 %fusion.6 = f32[1,256,1024]{2,1,0:T(8,128)S(1)} fusion(bf16[2048,3,1024]{2,0,1:T(8,128)(2,1)} %all-gather.2.cloned.1.call-done, bf16[128,2048]{0,1:T(8,128)(2,1)S(1)} %collective-permute-done.3, bf16[128,2048]{0,1:T(8,128)(2,1)S(1)} %bitcast.76), kind=kOutput, calls=%fused_computation.12 | convolution fusion | flops 1075838976 | bytes 6291456 | tf_op jit(solution)/shard_map/dot_general | solution.py:86
  113.3 3.4 %collective-permute-done.4 = f32[3,128,1024]{2,1,0:T(8,128)S(1)} collective-permute-done((f32[3,128,1024]{2,1,0:T(8,128)S(1)}, f32[3,128,1024]{2,1,0:T(8,128)S(1)}, u32[]{:S(2)}, u32[]{:S(2)}) %collective-permute-start.4) | collective-permute-done | bytes 1572896 | tf_op jit(solution)/shard_map/ppermute | solution.py:58
  117.0 2.0 %collective-permute-start.5 = (bf16[3,2,1024]{2,1,0:T(2,128)(2,1)S(1)}, bf16[3,2,1024]{2,1,0:T(2,128)(2,1)S(1)}, u32[]{:S(2)}, u32[]{:S(2)}) collective-permute-start(bf16[3,2,1024]{2,1,0:T(2,128)(2,1)S(1)} %slice.43), channel_id=1, source_target_pairs={{0,4},{4,8},{8,12},{12,16},{16,20},{20,24},{24,28},{28,32},{32,36}... | collective-permute-start | bytes 36872 | tf_op jit(solution)/shard_map/ppermute | solution.py:54
  120.7 1.5 reshape.61.x_ref
  122.2 2.9 %shard_map.64 = f32[16,8,128]{2,1,0:T(8,128)} custom-call(f32[3,130,8,128]{3,2,1,0:T(8,128)} %reshape.61.x_ref, f32[3,3,8,128]{3,2,1,0:T(8,128)} %reshape.51.taps_ref, f32[16,8,128]{2,1,0:T(8,128)} %bitcast.72), custom_call_target="tpu_custom_call" | custom-call | tf_op jit(solution)/shard_map/pallas_call | solution.py:100
  125.1 3.3 %collective-permute-start.6 = (f32[16,8,128]{2,1,0:T(8,128)}, f32[16,8,128]{2,1,0:T(8,128)S(1)}, u32[]{:S(2)}, u32[]{:S(2)}) collective-permute-start(f32[16,8,128]{2,1,0:T(8,128)} %shard_map.64), channel_id=1, source_target_pairs={{0,4},{4,8},{8,12},{12,16},{16,20},{20,24},{24,28},{28,32},{32,36}... | collective-permute-start | bytes 196616 | tf_op jit(solution)/shard_map/ppermute | solution.py:54
  128.4 1.1 collective-permute-done.6
  129.5 4.2 %collective-permute-start.7 = (f32[16,8,128]{2,1,0:T(8,128)S(1)}, f32[16,8,128]{2,1,0:T(8,128)S(1)}, u32[]{:S(2)}, u32[]{:S(2)}) collective-permute-start(f32[16,8,128]{2,1,0:T(8,128)S(1)} %collective-permute-done.6), channel_id=1, source_target_pairs={{0,4},{4,8},{8,12},{12,16},{16,20},{20,24},{24,28},{28,32},{32,36}... | collective-permute-start | bytes 196616 | tf_op jit(solution)/shard_map/ppermute | solution.py:54
  133.7 0.9 collective-permute-done.7
  134.6 6.8 %collective-permute-start.8 = (f32[16,8,128]{2,1,0:T(8,128)S(1)}, f32[16,8,128]{2,1,0:T(8,128)S(1)}, u32[]{:S(2)}, u32[]{:S(2)}) collective-permute-start(f32[16,8,128]{2,1,0:T(8,128)S(1)} %fusion.11), channel_id=1, source_target_pairs={{0,8},{4,12},{8,16},{12,20},{16,24},{20,28},{24,32},{28,36},{32,40... | collective-permute-start | bytes 196616 | tf_op jit(solution)/shard_map/ppermute | solution.py:54
  141.4 1.9 collective-permute-done.8
  143.3 5.8 %collective-permute-start.9 = (f32[16,8,128]{2,1,0:T(8,128)S(1)}, f32[16,8,128]{2,1,0:T(8,128)S(1)}, u32[]{:S(2)}, u32[]{:S(2)}) collective-permute-start(f32[16,8,128]{2,1,0:T(8,128)S(1)} %fusion.10), channel_id=1, source_target_pairs={{0,16},{4,20},{8,24},{12,28},{16,32},{20,36},{24,40},{28,44},{32,4... | collective-permute-start | bytes 196616 | tf_op jit(solution)/shard_map/ppermute | solution.py:54
  149.1 2.2 %collective-permute-done.9 = f32[16,8,128]{2,1,0:T(8,128)S(1)} collective-permute-done((f32[16,8,128]{2,1,0:T(8,128)S(1)}, f32[16,8,128]{2,1,0:T(8,128)S(1)}, u32[]{:S(2)}, u32[]{:S(2)}) %collective-permute-start.9) | collective-permute-done | bytes 65568 | tf_op jit(solution)/shard_map/ppermute | solution.py:54
  151.3 13.2 %collective-permute-start.10 = (f32[16,8,128]{2,1,0:T(8,128)S(1)}, f32[16,8,128]{2,1,0:T(8,128)S(1)}, u32[]{:S(2)}, u32[]{:S(2)}) collective-permute-start(f32[16,8,128]{2,1,0:T(8,128)S(1)} %fusion.9), channel_id=1, source_target_pairs={{0,32},{4,36},{8,40},{12,44},{16,48},{20,52},{24,56},{28,60},{32,6... | collective-permute-start | bytes 196616 | tf_op jit(solution)/shard_map/ppermute | solution.py:54
  164.5 2.0 %collective-permute-done.10 = f32[16,8,128]{2,1,0:T(8,128)S(1)} collective-permute-done((f32[16,8,128]{2,1,0:T(8,128)S(1)}, f32[16,8,128]{2,1,0:T(8,128)S(1)}, u32[]{:S(2)}, u32[]{:S(2)}) %collective-permute-start.10) | collective-permute-done | bytes 65568 | tf_op jit(solution)/shard_map/ppermute | solution.py:54
  166.5 6.0 %collective-permute-start.11 = (f32[16,8,128]{2,1,0:T(8,128)S(1)}, f32[16,8,128]{2,1,0:T(8,128)S(1)}, u32[]{:S(2)}, u32[]{:S(2)}) collective-permute-start(f32[16,8,128]{2,1,0:T(8,128)S(1)} %fusion.8), channel_id=1, source_target_pairs={{0,64},{4,68},{8,72},{12,76},{16,80},{20,84},{24,88},{28,92},{32,9... | collective-permute-start | bytes 196616 | tf_op jit(solution)/shard_map/ppermute | solution.py:54
  173.2 1.2 collective-permute-done.11
  175.0 3.9 %shard_map.65 = f32[128,8,128]{2,1,0:T(8,128)} custom-call(f32[3,130,8,128]{3,2,1,0:T(8,128)} %reshape.61.x_ref, f32[3,3,8,128]{3,2,1,0:T(8,128)} %reshape.51.taps_ref, f32[16,8,128]{2,1,0:T(8,128)} %bitcast.73, f32[16,8,128]{2,1,0:T(8,128)} %bitcast.78, f32[8,128]{1,0:T(8,128)} %bitcast.84, f32[16,8,128]{2,1,0:T(8,128)} %fusion.7.start_ref), custom_call_target="tpu_custom_call" | custom-call | tf_op jit(solution)/shard_map/pallas_call | solution.py:113
  178.9 1.1 convert_element_type.11
  180.0 0.8 copy.17
  (39 shorter events, 5.6 us)
Async XLA Ops:
  6.5 95.6 %all-gather.2.cloned.1.call-start = ((), (), s32[]{:S(2)}) async-start(), calls=%async_computation | async-start | bytes 13369344 | tf_op jit(solution)/shard_map/all_gather | solution.py:79
  7.3 9.7 %collective-permute-start = (bf16[128,1024]{1,0:T(8,128)(2,1)}, bf16[128,1024]{1,0:T(8,128)(2,1)S(1)}, u32[]{:S(2)}, u32[]{:S(2)}) collective-permute-start(bf16[128,1024]{1,0:T(8,128)(2,1)} %param.6), channel_id=1, source_target_pairs={{0,1},{1,2},{2,3},{3,0},{4,5},{5,6},{6,7},{7,4},{8,9},{9,10},{10,1... | collective-permute-start | bytes 786440 | tf_op jit(solution)/shard_map/ppermute | solution.py:65
  9.0 14.7 %collective-permute-start.1 = (bf16[128,1024]{1,0:T(8,128)(2,1)}, bf16[128,1024]{1,0:T(8,128)(2,1)S(1)}, u32[]{:S(2)}, u32[]{:S(2)}) collective-permute-start(bf16[128,1024]{1,0:T(8,128)(2,1)} %param.6), channel_id=1, source_target_pairs={{0,2},{1,3},{2,0},{3,1},{4,6},{5,7},{6,4},{7,5},{8,10},{9,11},{10,... | collective-permute-start | bytes 786440 | tf_op jit(solution)/shard_map/ppermute | solution.py:65
  11.9 11.9 %collective-permute-start.2 = (bf16[128,1024]{1,0:T(8,128)(2,1)}, bf16[128,1024]{1,0:T(8,128)(2,1)S(1)}, u32[]{:S(2)}, u32[]{:S(2)}) collective-permute-start(bf16[128,1024]{1,0:T(8,128)(2,1)} %param.6), channel_id=1, source_target_pairs={{0,3},{1,0},{2,1},{3,2},{4,7},{5,4},{6,5},{7,6},{8,11},{9,8},{10,9... | collective-permute-start | bytes 786440 | tf_op jit(solution)/shard_map/ppermute | solution.py:65
  26.4 2.0 %collective-permute-start.3 = (bf16[128,2048]{0,1:T(8,128)(2,1)S(1)}, bf16[128,2048]{0,1:T(8,128)(2,1)S(1)}, u32[]{:S(2)}, u32[]{:S(2)}) collective-permute-start(bf16[128,2048]{0,1:T(8,128)(2,1)S(1)} %bitcast.77), channel_id=1, source_target_pairs={{0,4},{4,0},{1,5},{5,1},{2,6},{6,2},{3,7},{7,3},{8,12},{12,8},{9,1... | collective-permute-start | bytes 1572872 | tf_op jit(solution)/shard_map/ppermute | solution.py:58
  113.0 6.1 %copy-start = (f32[16,1024]{1,0:T(8,128)S(1)}, f32[16,1024]{1,0:T(8,128)}, u32[]{:S(2)}) copy-start(f32[16,1024]{1,0:T(8,128)} %param.9) | copy-start | bytes 196612
  113.0 6.8 %copy-start.2 = (f32[3,3,1024]{2,1,0:T(4,128)S(1)}, f32[3,3,1024]{2,1,0:T(4,128)}, u32[]{:S(2)}) copy-start(f32[3,3,1024]{2,1,0:T(4,128)} %param.8) | copy-start | bytes 110596
  113.2 3.5 %collective-permute-start.4 = (f32[3,128,1024]{2,1,0:T(8,128)S(1)}, f32[3,128,1024]{2,1,0:T(8,128)S(1)}, u32[]{:S(2)}, u32[]{:S(2)}) collective-permute-start(f32[3,128,1024]{2,1,0:T(8,128)S(1)} %slice.42), channel_id=1, source_target_pairs={{0,4},{4,0},{1,5},{5,1},{2,6},{6,2},{3,7},{7,3},{8,12},{12,8},{9,1... | collective-permute-start | bytes 4718600 | tf_op jit(solution)/shard_map/ppermute | solution.py:58
  117.0 3.4 %collective-permute-start.5 = (bf16[3,2,1024]{2,1,0:T(2,128)(2,1)S(1)}, bf16[3,2,1024]{2,1,0:T(2,128)(2,1)S(1)}, u32[]{:S(2)}, u32[]{:S(2)}) collective-permute-start(bf16[3,2,1024]{2,1,0:T(2,128)(2,1)S(1)} %slice.43), channel_id=1, source_target_pairs={{0,4},{4,8},{8,12},{12,16},{16,20},{20,24},{24,28},{28,32},{32,36}... | collective-permute-start | bytes 36872 | tf_op jit(solution)/shard_map/ppermute | solution.py:54
  120.7 51.9 %copy-start.1 = (f32[16,1024]{1,0:T(8,128)S(1)}, f32[16,1024]{1,0:T(8,128)}, u32[]{:S(2)}) copy-start(f32[16,1024]{1,0:T(8,128)} %param.10) | copy-start | bytes 196612
  125.1 4.4 %collective-permute-start.6 = (f32[16,8,128]{2,1,0:T(8,128)}, f32[16,8,128]{2,1,0:T(8,128)S(1)}, u32[]{:S(2)}, u32[]{:S(2)}) collective-permute-start(f32[16,8,128]{2,1,0:T(8,128)} %shard_map.64), channel_id=1, source_target_pairs={{0,4},{4,8},{8,12},{12,16},{16,20},{20,24},{24,28},{28,32},{32,36}... | collective-permute-start | bytes 196616 | tf_op jit(solution)/shard_map/ppermute | solution.py:54
  129.5 5.1 %collective-permute-start.7 = (f32[16,8,128]{2,1,0:T(8,128)S(1)}, f32[16,8,128]{2,1,0:T(8,128)S(1)}, u32[]{:S(2)}, u32[]{:S(2)}) collective-permute-start(f32[16,8,128]{2,1,0:T(8,128)S(1)} %collective-permute-done.6), channel_id=1, source_target_pairs={{0,4},{4,8},{8,12},{12,16},{16,20},{20,24},{24,28},{28,32},{32,36}... | collective-permute-start | bytes 196616 | tf_op jit(solution)/shard_map/ppermute | solution.py:54
  134.6 8.7 %collective-permute-start.8 = (f32[16,8,128]{2,1,0:T(8,128)S(1)}, f32[16,8,128]{2,1,0:T(8,128)S(1)}, u32[]{:S(2)}, u32[]{:S(2)}) collective-permute-start(f32[16,8,128]{2,1,0:T(8,128)S(1)} %fusion.11), channel_id=1, source_target_pairs={{0,8},{4,12},{8,16},{12,20},{16,24},{20,28},{24,32},{28,36},{32,40... | collective-permute-start | bytes 196616 | tf_op jit(solution)/shard_map/ppermute | solution.py:54
  143.3 8.0 %collective-permute-start.9 = (f32[16,8,128]{2,1,0:T(8,128)S(1)}, f32[16,8,128]{2,1,0:T(8,128)S(1)}, u32[]{:S(2)}, u32[]{:S(2)}) collective-permute-start(f32[16,8,128]{2,1,0:T(8,128)S(1)} %fusion.10), channel_id=1, source_target_pairs={{0,16},{4,20},{8,24},{12,28},{16,32},{20,36},{24,40},{28,44},{32,4... | collective-permute-start | bytes 196616 | tf_op jit(solution)/shard_map/ppermute | solution.py:54
  151.3 15.2 %collective-permute-start.10 = (f32[16,8,128]{2,1,0:T(8,128)S(1)}, f32[16,8,128]{2,1,0:T(8,128)S(1)}, u32[]{:S(2)}, u32[]{:S(2)}) collective-permute-start(f32[16,8,128]{2,1,0:T(8,128)S(1)} %fusion.9), channel_id=1, source_target_pairs={{0,32},{4,36},{8,40},{12,44},{16,48},{20,52},{24,56},{28,60},{32,6... | collective-permute-start | bytes 196616 | tf_op jit(solution)/shard_map/ppermute | solution.py:54
  166.5 7.9 %collective-permute-start.11 = (f32[16,8,128]{2,1,0:T(8,128)S(1)}, f32[16,8,128]{2,1,0:T(8,128)S(1)}, u32[]{:S(2)}, u32[]{:S(2)}) collective-permute-start(f32[16,8,128]{2,1,0:T(8,128)S(1)} %fusion.8), channel_id=1, source_target_pairs={{0,64},{4,68},{8,72},{12,76},{16,80},{20,84},{24,88},{28,92},{32,9... | collective-permute-start | bytes 196616 | tf_op jit(solution)/shard_map/ppermute | solution.py:54
Sparse Core Ops, SparseCore 0:
  9.5 92.6 all-gather.1

commit v3 on v2

--- a/solution.py
+++ b/solution.py
@@ -1,9 +1,13 @@
+import functools
+
 import jax
 import jax.numpy as jnp
 from jax import lax
 from jax.experimental import pallas as pl
 from jax.experimental.pallas import tpu as pltpu
 from jax.sharding import PartitionSpec as P
+
+MESH = pl.DeviceIdType.MESH
 
 LANES = 128
 
@@ -40,6 +44,43 @@
         return state
 
     lax.fori_loop(0, rows, step, start_ref[...], unroll=8)
+
+
+def carry_kernel(peers, end_ref, lift_ref, keep_ref, start_ref, held, slots, send_sem, recv_sem):
+    rounds = lift_ref.shape[0]
+    me = lax.axis_index("cx") * 2 + lax.axis_index("core")
+    tp = lax.axis_index("tp")
+
+    def device(i):
+        return (i // 2, i % 2, tp)
+
+    barrier = pltpu.get_barrier_semaphore()
+    for r in range(rounds):
+        for peer in ((me + 2**r) % peers, (me + peers - 2**r) % peers):
+            pl.semaphore_signal(barrier, inc=1, device_id=device(peer), device_id_type=MESH)
+    pl.semaphore_wait(barrier, 2 * rounds)
+
+    held[0] = end_ref[...]
+    start_ref[...] = jnp.zeros(start_ref.shape, jnp.float32)
+    copies = []
+    for r in range(rounds):
+        copy = pltpu.make_async_remote_copy(
+            src_ref=held.at[r],
+            dst_ref=slots.at[r],
+            send_sem=send_sem.at[r],
+            recv_sem=recv_sem.at[r],
+            device_id=device((me + 2**r) % peers),
+            device_id_type=MESH,
+        )
+        copy.start()
+        copies.append(copy)
+        copy.wait_recv()
+        got = jnp.where(me >= 2**r, slots[r], 0.0)
+        start_ref[...] += lift_ref[r] * got
+        if r + 1 < rounds:
+            held[r + 1] = held[r] + keep_ref[r] * got
+    for copy in copies:
+        copy.wait_send()
 
 
 def vmem_specs(n):
@@ -103,13 +144,25 @@
         in_specs=vmem_specs(3),
         out_specs=pl.BlockSpec(memory_space=pltpu.VMEM),
     )(x, taps, decay)
-    start = shifted(end, ctx, 1)
     peers = lax.axis_size("cx") * lax.axis_size("core")
-    by = 1
-    while by < peers:
-        span = jnp.exp(-decay_rate * float(rows * by)).reshape(poles, subl, LANES)
-        start = start + span * shifted(start, ctx, by)
-        by *= 2
+    rounds = max(1, (peers - 1).bit_length())
+    widths = jnp.asarray([2.0**r for r in range(rounds)], jnp.float32)[:, None, None]
+    lift = jnp.exp(-decay_rate[None] * (rows * (widths - 1.0))).reshape(rounds, poles, subl, LANES)
+    keep = jnp.exp(-decay_rate[None] * (rows * widths)).reshape(rounds, poles, subl, LANES)
+    state_shape = (poles, subl, LANES)
+    start = pl.pallas_call(
+        functools.partial(carry_kernel, peers),
+        out_shape=jax.ShapeDtypeStruct(state_shape, jnp.float32),
+        in_specs=vmem_specs(3),
+        out_specs=pl.BlockSpec(memory_space=pltpu.VMEM),
+        scratch_shapes=[
+            pltpu.VMEM((rounds,) + state_shape, jnp.float32),
+            pltpu.VMEM((rounds,) + state_shape, jnp.float32),
+            pltpu.SemaphoreType.DMA((rounds,)),
+            pltpu.SemaphoreType.DMA((rounds,)),
+        ],
+        compiler_params=pltpu.CompilerParams(collective_id=0, has_side_effects=True),
+    )(end, lift, keep)
     out = pl.pallas_call(
         mixed_kernel,
         out_shape=jax.ShapeDtypeStruct((rows, subl, LANES), jnp.float32),

time: 188 us -> 165 us (0.88)
  starting transfers between devices: 47.4 us -> 8.19 us
  Pallas kernels: 6.79 us -> 31.7 us
  waiting for transfers between devices: 98.7 us -> 88.9 us
    ppermute x7 -> x1, starting transfers between devices: 41.3 us -> 2.04 us  [shifted(): return lax.ppermute(array, axes, pairs)]
    pallas_call x0 -> x1, Pallas kernels: none -> 24.9 us  [per_device(): pl.pallas_call(functools.partial(carry_kernel, peers), out_shape=jax.Shap...]
    ppermute x7 -> x1, waiting for transfers between devices: 9.21 us -> 0.01 us  [shifted(): return lax.ppermute(array, axes, pairs)]
  transfers between devices with their start and end apart: 13 -> 7, of which waited for: 11 -> 5; matrix products, arithmetic and copies ran while one was open for 3% -> 4% of each run, Pallas kernels for 0% -> 0%
where the time goes in v3:
time: 165 us; the launch traced here: 164 us
  waiting for transfers between devices  88.9 us (54%)
  Pallas kernels  31.7 us (19%)
  between operations  13.6 us (8%)
  matrix products  10.4 us (6%)
  starting transfers between devices  8.19 us (5%)
  local copies, waits for them, and re-layouts  6.16 us (4%)
  other arithmetic  5.15 us (3%)
    all_gather x1, waiting for transfers between devices, per_device(): piece = lax.all_gather(in_weight, 'cx', axis=0, tiled=True)  73.8 us
    pallas_call x1, Pallas kernels, per_device(): pl.pallas_call(functools.partial(carry_kernel, peers), out_shape=jax.Shap...  24.9 us
    dot_general x3, matrix products, per_device(): jnp.dot(both, piece[:, g, :], preferred_element_type=jnp.float32)  10.4 us
    ppermute x3, waiting for transfers between devices, gathered_tp(): lax.ppermute(tokens, 'tp', [(i, (i + by) % peers) for i in range(peers)])  9.71 us
    ppermute x3, starting transfers between devices, gathered_tp(): lax.ppermute(tokens, 'tp', [(i, (i + by) % peers) for i in range(peers)])  5.98 us
    ppermute x2, waiting for transfers between devices, swapped(): return lax.ppermute(array, axis, [(0, 1), (1, 0)])  4.67 us
    pallas_call x1, Pallas kernels, per_device(): pl.pallas_call(mixed_kernel, out_shape=jax.ShapeDtypeStruct((rows, subl,...  3.9 us
  transfers between devices with their start and end apart: 7, of which 5 were waited for; matrix products, arithmetic and copies ran while one was open for 4% of the time, Pallas kernels for 0%

profile of v3, /device:TPU:0, one launch (start us, length us, event | category | flops | bytes accessed | tf_op | source)
XLA Modules:
  0.0 164.0 jit_solution(5925973713229004642)
XLA Ops:
  6.5 0.7 all-gather.2.cloned.1.call-update
  7.3 1.7 %collective-permute-start = (bf16[128,1024]{1,0:T(8,128)(2,1)}, bf16[128,1024]{1,0:T(8,128)(2,1)S(1)}, u32[]{:S(2)}, u32[]{:S(2)}) collective-permute-start(bf16[128,1024]{1,0:T(8,128)(2,1)} %param.7), channel_id=1, source_target_pairs={{0,1},{1,2},{2,3},{3,0},{4,5},{5,6},{6,7},{7,4},{8,9},{9,10},{10,1... | collective-permute-start | bytes 786440 | tf_op jit(solution)/shard_map/ppermute | solution.py:106
  9.0 2.9 %collective-permute-start.1 = (bf16[128,1024]{1,0:T(8,128)(2,1)}, bf16[128,1024]{1,0:T(8,128)(2,1)S(1)}, u32[]{:S(2)}, u32[]{:S(2)}) collective-permute-start(bf16[128,1024]{1,0:T(8,128)(2,1)} %param.7), channel_id=1, source_target_pairs={{0,2},{1,3},{2,0},{3,1},{4,6},{5,7},{6,4},{7,5},{8,10},{9,11},{10,... | collective-permute-start | bytes 786440 | tf_op jit(solution)/shard_map/ppermute | solution.py:106
  11.9 1.3 collective-permute-start.2
  13.2 0.7 sort.17
  14.0 2.9 %collective-permute-done = bf16[128,1024]{1,0:T(8,128)(2,1)S(1)} collective-permute-done((bf16[128,1024]{1,0:T(8,128)(2,1)}, bf16[128,1024]{1,0:T(8,128)(2,1)S(1)}, u32[]{:S(2)}, u32[]{:S(2)}) %collective-permute-start) | collective-permute-done | bytes 262176 | tf_op jit(solution)/shard_map/ppermute | solution.py:106
  16.9 6.8 %collective-permute-done.1 = bf16[128,1024]{1,0:T(8,128)(2,1)S(1)} collective-permute-done((bf16[128,1024]{1,0:T(8,128)(2,1)}, bf16[128,1024]{1,0:T(8,128)(2,1)S(1)}, u32[]{:S(2)}, u32[]{:S(2)}) %collective-permute-start.1) | collective-permute-done | bytes 262176 | tf_op jit(solution)/shard_map/ppermute | solution.py:106
  23.7 1.1 pad_maximum_fusion.1
  24.8 0.6 gather_fusion
  25.4 0.2 select_bitcast_fusion
  25.6 0.7 copy.8
  26.5 1.9 %collective-permute-done.3 = bf16[128,2048]{0,1:T(8,128)(2,1)S(1)} collective-permute-done((bf16[128,2048]{0,1:T(8,128)(2,1)S(1)}, bf16[128,2048]{0,1:T(8,128)(2,1)S(1)}, u32[]{:S(2)}, u32[]{:S(2)}) %collective-permute-start.3) | collective-permute-done | bytes 524320 | tf_op jit(solution)/shard_map/ppermute | solution.py:99
  28.4 73.8 %all-gather.2.cloned.1.call-done = bf16[2048,3,1024]{2,0,1:T(8,128)(2,1)} async-done(((bf16[128,3,1024]{2,0,1:T(8,128)(2,1)}), bf16[2048,3,1024]{2,0,1:T(8,128)(2,1)}) %all-gather.2.cloned.1.call-update) | async-done | bytes 12582928 | tf_op jit(solution)/shard_map/all_gather | solution.py:120
  102.2 3.5 %fusion.4 = f32[1,256,1024]{2,1,0:T(8,128)S(1)} fusion(bf16[2048,3,1024]{2,0,1:T(8,128)(2,1)} %all-gather.2.cloned.1.call-done, bf16[128,2048]{0,1:T(8,128)(2,1)S(1)} %collective-permute-done.3, bf16[128,2048]{0,1:T(8,128)(2,1)S(1)} %bitcast.47), kind=kOutput, calls=%fused_computation.10 | convolution fusion | flops 1075838976 | bytes 6291456 | tf_op jit(solution)/shard_map/dot_general | solution.py:127
  105.6 3.5 %fusion.5 = f32[1,256,1024]{2,1,0:T(8,128)S(1)} fusion(bf16[2048,3,1024]{2,0,1:T(8,128)(2,1)} %all-gather.2.cloned.1.call-done, bf16[128,2048]{0,1:T(8,128)(2,1)S(1)} %collective-permute-done.3, bf16[128,2048]{0,1:T(8,128)(2,1)S(1)} %bitcast.48), kind=kOutput, calls=%fused_computation.11 | convolution fusion | flops 1075838976 | bytes 6291456 | tf_op jit(solution)/shard_map/dot_general | solution.py:127
  109.1 3.5 %fusion.6 = f32[1,256,1024]{2,1,0:T(8,128)S(1)} fusion(bf16[2048,3,1024]{2,0,1:T(8,128)(2,1)} %all-gather.2.cloned.1.call-done, bf16[128,2048]{0,1:T(8,128)(2,1)S(1)} %collective-permute-done.3, bf16[128,2048]{0,1:T(8,128)(2,1)S(1)} %bitcast.49), kind=kOutput, calls=%fused_computation.12 | convolution fusion | flops 1075838976 | bytes 6291456 | tf_op jit(solution)/shard_map/dot_general | solution.py:127
  112.6 0.4 pad_maximum_fusion
  113.2 0.6 copy-done
  113.9 2.8 %collective-permute-done.4 = f32[3,128,1024]{2,1,0:T(8,128)S(1)} collective-permute-done((f32[3,128,1024]{2,1,0:T(8,128)S(1)}, f32[3,128,1024]{2,1,0:T(8,128)S(1)}, u32[]{:S(2)}, u32[]{:S(2)}) %collective-permute-start.4) | collective-permute-done | bytes 1572896 | tf_op jit(solution)/shard_map/ppermute | solution.py:99
  116.6 0.3 fusion.3
  117.0 2.0 %collective-permute-start.5 = (bf16[3,2,1024]{2,1,0:T(2,128)(2,1)S(1)}, bf16[3,2,1024]{2,1,0:T(2,128)(2,1)S(1)}, u32[]{:S(2)}, u32[]{:S(2)}) collective-permute-start(bf16[3,2,1024]{2,1,0:T(2,128)(2,1)S(1)} %slice.43), channel_id=1, source_target_pairs={{0,4},{4,8},{8,12},{12,16},{16,20},{20,24},{24,28},{28,32},{32,36}... | collective-permute-start | bytes 36872 | tf_op jit(solution)/shard_map/ppermute | solution.py:95
  119.1 1.0 multiply_exponential_fusion
  120.1 0.6 copy.9
  120.7 0.6 reshape.48.taps_ref
  121.4 0.6 copy.10
  122.0 0.2 pad_maximum_fusion.3
  122.2 1.5 reshape.53.x_ref
  123.7 2.9 %shard_map.73.end_ref = f32[16,8,128]{2,1,0:T(8,128)} custom-call(f32[3,130,8,128]{3,2,1,0:T(8,128)} %reshape.53.x_ref, f32[3,3,8,128]{3,2,1,0:T(8,128)} %reshape.48.taps_ref, f32[16,8,128]{2,1,0:T(8,128)} %bitcast.45), custom_call_target="tpu_custom_call" | custom-call | tf_op jit(solution)/shard_map/pallas_call | solution.py:141
  126.6 24.9 %shard_map.74.start_ref = f32[16,8,128]{2,1,0:T(8,128)} custom-call(f32[16,8,128]{2,1,0:T(8,128)} %shard_map.73.end_ref, f32[5,16,8,128]{3,2,1,0:T(8,128)} %get-tuple-element.10.lift_ref, f32[5,16,8,128]{3,2,1,0:T(8,128)} %get-tuple-element.9.keep_ref), custom_call_target="tpu_custom_call" | custom-call | tf_op jit(solution)/shard_map/pallas_call | solution.py:153
  151.5 3.9 %shard_map.75 = f32[128,8,128]{2,1,0:T(8,128)} custom-call(f32[3,130,8,128]{3,2,1,0:T(8,128)} %reshape.53.x_ref, f32[3,3,8,128]{3,2,1,0:T(8,128)} %reshape.48.taps_ref, f32[16,8,128]{2,1,0:T(8,128)} %bitcast.46, f32[16,8,128]{2,1,0:T(8,128)} %bitcast.51, f32[8,128]{1,0:T(8,128)} %bitcast.58, f32[16,8,128]{2,1,0:T(8,128)} %shard_map.74.start_ref), custom_call_target="tpu_custom_call" | custom-call | tf_op jit(solution)/shard_map/pallas_call | solution.py:166
  155.4 1.1 convert_element_type.11
  156.4 0.8 copy.14
  (24 shorter events, 0.5 us)
Async XLA Ops:
  6.5 95.6 %all-gather.2.cloned.1.call-start = ((), (), s32[]{:S(2)}) async-start(), calls=%async_computation | async-start | bytes 13369344 | tf_op jit(solution)/shard_map/all_gather | solution.py:120
  7.3 9.7 %collective-permute-start = (bf16[128,1024]{1,0:T(8,128)(2,1)}, bf16[128,1024]{1,0:T(8,128)(2,1)S(1)}, u32[]{:S(2)}, u32[]{:S(2)}) collective-permute-start(bf16[128,1024]{1,0:T(8,128)(2,1)} %param.7), channel_id=1, source_target_pairs={{0,1},{1,2},{2,3},{3,0},{4,5},{5,6},{6,7},{7,4},{8,9},{9,10},{10,1... | collective-permute-start | bytes 786440 | tf_op jit(solution)/shard_map/ppermute | solution.py:106
  9.0 14.7 %collective-permute-start.1 = (bf16[128,1024]{1,0:T(8,128)(2,1)}, bf16[128,1024]{1,0:T(8,128)(2,1)S(1)}, u32[]{:S(2)}, u32[]{:S(2)}) collective-permute-start(bf16[128,1024]{1,0:T(8,128)(2,1)} %param.7), channel_id=1, source_target_pairs={{0,2},{1,3},{2,0},{3,1},{4,6},{5,7},{6,4},{7,5},{8,10},{9,11},{10,... | collective-permute-start | bytes 786440 | tf_op jit(solution)/shard_map/ppermute | solution.py:106
  11.9 11.9 %collective-permute-start.2 = (bf16[128,1024]{1,0:T(8,128)(2,1)}, bf16[128,1024]{1,0:T(8,128)(2,1)S(1)}, u32[]{:S(2)}, u32[]{:S(2)}) collective-permute-start(bf16[128,1024]{1,0:T(8,128)(2,1)} %param.7), channel_id=1, source_target_pairs={{0,3},{1,0},{2,1},{3,2},{4,7},{5,4},{6,5},{7,6},{8,11},{9,8},{10,9... | collective-permute-start | bytes 786440 | tf_op jit(solution)/shard_map/ppermute | solution.py:106
  26.4 2.0 %collective-permute-start.3 = (bf16[128,2048]{0,1:T(8,128)(2,1)S(1)}, bf16[128,2048]{0,1:T(8,128)(2,1)S(1)}, u32[]{:S(2)}, u32[]{:S(2)}) collective-permute-start(bf16[128,2048]{0,1:T(8,128)(2,1)S(1)} %bitcast.50), channel_id=1, source_target_pairs={{0,4},{4,0},{1,5},{5,1},{2,6},{6,2},{3,7},{7,3},{8,12},{12,8},{9,1... | collective-permute-start | bytes 1572872 | tf_op jit(solution)/shard_map/ppermute | solution.py:99
  113.0 0.8 copy-start
  113.0 6.1 %copy-start.3 = (f32[5]{0:T(128)S(1)}, f32[5]{0:T(128)}, u32[]{:S(2)}) copy-start(f32[5]{0:T(128)} %constant.47) | copy-start | bytes 64
  113.0 6.1 %copy-start.4 = (f32[5]{0:T(128)S(1)}, f32[5]{0:T(128)}, u32[]{:S(2)}) copy-start(f32[5]{0:T(128)} %constant.48) | copy-start | bytes 64
  113.1 7.6 %copy-start.2 = (f32[3,3,1024]{2,1,0:T(4,128)S(1)}, f32[3,3,1024]{2,1,0:T(4,128)}, u32[]{:S(2)}) copy-start(f32[3,3,1024]{2,1,0:T(4,128)} %param.9) | copy-start | bytes 110596
  113.1 8.2 %copy-start.1 = (f32[16,1024]{1,0:T(8,128)S(1)}, f32[16,1024]{1,0:T(8,128)}, u32[]{:S(2)}) copy-start(f32[16,1024]{1,0:T(8,128)} %param.11) | copy-start | bytes 196612
  113.1 3.5 %collective-permute-start.4 = (f32[3,128,1024]{2,1,0:T(8,128)S(1)}, f32[3,128,1024]{2,1,0:T(8,128)S(1)}, u32[]{:S(2)}, u32[]{:S(2)}) collective-permute-start(f32[3,128,1024]{2,1,0:T(8,128)S(1)} %slice.42), channel_id=1, source_target_pairs={{0,4},{4,0},{1,5},{5,1},{2,6},{6,2},{3,7},{7,3},{8,12},{12,8},{9,1... | collective-permute-start | bytes 4718600 | tf_op jit(solution)/shard_map/ppermute | solution.py:99
  117.0 5.0 %collective-permute-start.5 = (bf16[3,2,1024]{2,1,0:T(2,128)(2,1)S(1)}, bf16[3,2,1024]{2,1,0:T(2,128)(2,1)S(1)}, u32[]{:S(2)}, u32[]{:S(2)}) collective-permute-start(bf16[3,2,1024]{2,1,0:T(2,128)(2,1)S(1)} %slice.43), channel_id=1, source_target_pairs={{0,4},{4,8},{8,12},{12,16},{16,20},{20,24},{24,28},{28,32},{32,36}... | collective-permute-start | bytes 36872 | tf_op jit(solution)/shard_map/ppermute | solution.py:95
Sparse Core Ops, SparseCore 0:
  9.5 92.6 all-gather.1

commit v4 on v2

--- a/solution.py
+++ b/solution.py
@@ -1,9 +1,13 @@
+import functools
+
 import jax
 import jax.numpy as jnp
 from jax import lax
 from jax.experimental import pallas as pl
 from jax.experimental.pallas import tpu as pltpu
 from jax.sharding import PartitionSpec as P
+
+MESH = pl.DeviceIdType.MESH
 
 LANES = 128
 
@@ -40,6 +44,62 @@
         return state
 
     lax.fori_loop(0, rows, step, start_ref[...], unroll=8)
+
+
+def carry_kernel(peers, digits, end_ref, lift_ref, keep_ref, start_ref, held, slots, send_sem, recv_sem):
+    me = lax.axis_index("cx") * 2 + lax.axis_index("core")
+    tp = lax.axis_index("tp")
+
+    def device(i):
+        return (i // 2, i % 2, tp)
+
+    steps = []
+    width = 1
+    for r, digit in enumerate(digits):
+        steps.extend((r, d * width) for d in range(1, digit))
+        width *= digit
+
+    barrier = pltpu.get_barrier_semaphore()
+    for _, by in steps:
+        for peer in ((me + by) % peers, (me + peers - by) % peers):
+            pl.semaphore_signal(barrier, inc=1, device_id=device(peer), device_id_type=MESH)
+    pl.semaphore_wait(barrier, 2 * len(steps))
+
+    held[0] = end_ref[...]
+    start_ref[...] = jnp.zeros(start_ref.shape, jnp.float32)
+    copies = []
+    for r in range(len(digits)):
+        mine = [(n, by) for n, (q, by) in enumerate(steps) if q == r]
+        for n, by in mine:
+            copy = pltpu.make_async_remote_copy(
+                src_ref=held.at[r],
+                dst_ref=slots.at[n],
+                send_sem=send_sem.at[n],
+                recv_sem=recv_sem.at[n],
+                device_id=device((me + by) % peers),
+                device_id_type=MESH,
+            )
+            copy.start()
+            copies.append(copy)
+        grown = held[r]
+        for n, by in mine:
+            copies[n].wait_recv()
+            got = jnp.where(me >= by, slots[n], 0.0)
+            start_ref[...] += lift_ref[n] * got
+            grown = grown + keep_ref[n] * got
+        if r + 1 < len(digits):
+            held[r + 1] = grown
+    for copy in copies:
+        copy.wait_send()
+
+
+def scan_digits(peers):
+    digits = []
+    while peers > 1:
+        digit = 4 if peers % 4 == 0 and peers != 8 else 2
+        digits.append(digit)
+        peers //= digit
+    return digits or [2]
 
 
 def vmem_specs(n):
@@ -103,13 +163,30 @@
         in_specs=vmem_specs(3),
         out_specs=pl.BlockSpec(memory_space=pltpu.VMEM),
     )(x, taps, decay)
-    start = shifted(end, ctx, 1)
     peers = lax.axis_size("cx") * lax.axis_size("core")
-    by = 1
-    while by < peers:
-        span = jnp.exp(-decay_rate * float(rows * by)).reshape(poles, subl, LANES)
-        start = start + span * shifted(start, ctx, by)
-        by *= 2
+    digits = scan_digits(peers)
+    strides, width = [], 1
+    for digit in digits:
+        strides.extend(d * width for d in range(1, digit))
+        width *= digit
+    copies = len(strides)
+    widths = jnp.asarray(strides, jnp.float32)[:, None, None]
+    lift = jnp.exp(-decay_rate[None] * (rows * (widths - 1.0))).reshape(copies, poles, subl, LANES)
+    keep = jnp.exp(-decay_rate[None] * (rows * widths)).reshape(copies, poles, subl, LANES)
+    state_shape = (poles, subl, LANES)
+    start = pl.pallas_call(
+        functools.partial(carry_kernel, peers, digits),
+        out_shape=jax.ShapeDtypeStruct(state_shape, jnp.float32),
+        in_specs=vmem_specs(3),
+        out_specs=pl.BlockSpec(memory_space=pltpu.VMEM),
+        scratch_shapes=[
+            pltpu.VMEM((len(digits),) + state_shape, jnp.float32),
+            pltpu.VMEM((copies,) + state_shape, jnp.float32),
+            pltpu.SemaphoreType.DMA((copies,)),
+            pltpu.SemaphoreType.DMA((copies,)),
+        ],
+        compiler_params=pltpu.CompilerParams(collective_id=0, has_side_effects=True),
+    )(end, lift, keep)
     out = pl.pallas_call(
         mixed_kernel,
         out_shape=jax.ShapeDtypeStruct((rows, subl, LANES), jnp.float32),

time: 188 us -> 162 us (0.86)
  starting transfers between devices: 47.4 us -> 8.19 us
  Pallas kernels: 6.79 us -> 28.7 us
  waiting for transfers between devices: 98.7 us -> 88.9 us
    ppermute x7 -> x1, starting transfers between devices: 41.3 us -> 2.04 us  [shifted(): return lax.ppermute(array, axes, pairs)]
    pallas_call x0 -> x1, Pallas kernels: none -> 21.9 us  [per_device(): pl.pallas_call(functools.partial(carry_kernel, peers, digits), out_shape=...]
    ppermute x7 -> x1, waiting for transfers between devices: 9.21 us -> 0.01 us  [shifted(): return lax.ppermute(array, axes, pairs)]
  transfers between devices with their start and end apart: 13 -> 7, of which waited for: 11 -> 5; matrix products, arithmetic and copies ran while one was open for 3% -> 4% of each run, Pallas kernels for 0% -> 0%
where the time goes in v4:
time: 162 us; the launch traced here: 161 us
  waiting for transfers between devices  88.9 us (55%)
  Pallas kernels  28.7 us (18%)
  between operations  13.6 us (8%)
  matrix products  10.4 us (6%)
  starting transfers between devices  8.19 us (5%)
  local copies, waits for them, and re-layouts  6.16 us (4%)
  other arithmetic  5.24 us (3%)
    all_gather x1, waiting for transfers between devices, per_device(): piece = lax.all_gather(in_weight, 'cx', axis=0, tiled=True)  73.8 us
    pallas_call x1, Pallas kernels, per_device(): pl.pallas_call(functools.partial(carry_kernel, peers, digits), out_shape=...  21.9 us
    dot_general x3, matrix products, per_device(): jnp.dot(both, piece[:, g, :], preferred_element_type=jnp.float32)  10.4 us
    ppermute x3, waiting for transfers between devices, gathered_tp(): lax.ppermute(tokens, 'tp', [(i, (i + by) % peers) for i in range(peers)])  9.71 us
    ppermute x3, starting transfers between devices, gathered_tp(): lax.ppermute(tokens, 'tp', [(i, (i + by) % peers) for i in range(peers)])  5.98 us
    ppermute x2, waiting for transfers between devices, swapped(): return lax.ppermute(array, axis, [(0, 1), (1, 0)])  4.67 us
    pallas_call x1, Pallas kernels, per_device(): pl.pallas_call(mixed_kernel, out_shape=jax.ShapeDtypeStruct((rows, subl,...  3.9 us
  transfers between devices with their start and end apart: 7, of which 5 were waited for; matrix products, arithmetic and copies ran while one was open for 4% of the time, Pallas kernels for 0%

profile of v4, /device:TPU:0, one launch (start us, length us, event | category | flops | bytes accessed | tf_op | source)
XLA Modules:
  0.0 161.1 jit_solution(11294254977005505771)
XLA Ops:
  6.5 0.7 all-gather.2.cloned.1.call-update
  7.3 1.7 %collective-permute-start = (bf16[128,1024]{1,0:T(8,128)(2,1)}, bf16[128,1024]{1,0:T(8,128)(2,1)S(1)}, u32[]{:S(2)}, u32[]{:S(2)}) collective-permute-start(bf16[128,1024]{1,0:T(8,128)(2,1)} %param.7), channel_id=1, source_target_pairs={{0,1},{1,2},{2,3},{3,0},{4,5},{5,6},{6,7},{7,4},{8,9},{9,10},{10,1... | collective-permute-start | bytes 786440 | tf_op jit(solution)/shard_map/ppermute | solution.py:125
  9.0 2.9 %collective-permute-start.1 = (bf16[128,1024]{1,0:T(8,128)(2,1)}, bf16[128,1024]{1,0:T(8,128)(2,1)S(1)}, u32[]{:S(2)}, u32[]{:S(2)}) collective-permute-start(bf16[128,1024]{1,0:T(8,128)(2,1)} %param.7), channel_id=1, source_target_pairs={{0,2},{1,3},{2,0},{3,1},{4,6},{5,7},{6,4},{7,5},{8,10},{9,11},{10,... | collective-permute-start | bytes 786440 | tf_op jit(solution)/shard_map/ppermute | solution.py:125
  11.9 1.3 collective-permute-start.2
  13.2 0.7 sort.17
  14.0 2.9 %collective-permute-done = bf16[128,1024]{1,0:T(8,128)(2,1)S(1)} collective-permute-done((bf16[128,1024]{1,0:T(8,128)(2,1)}, bf16[128,1024]{1,0:T(8,128)(2,1)S(1)}, u32[]{:S(2)}, u32[]{:S(2)}) %collective-permute-start) | collective-permute-done | bytes 262176 | tf_op jit(solution)/shard_map/ppermute | solution.py:125
  16.9 6.8 %collective-permute-done.1 = bf16[128,1024]{1,0:T(8,128)(2,1)S(1)} collective-permute-done((bf16[128,1024]{1,0:T(8,128)(2,1)}, bf16[128,1024]{1,0:T(8,128)(2,1)S(1)}, u32[]{:S(2)}, u32[]{:S(2)}) %collective-permute-start.1) | collective-permute-done | bytes 262176 | tf_op jit(solution)/shard_map/ppermute | solution.py:125
  23.7 1.1 pad_maximum_fusion.1
  24.8 0.6 gather_fusion
  25.4 0.2 select_bitcast_fusion
  25.6 0.7 copy.8
  26.5 1.9 %collective-permute-done.3 = bf16[128,2048]{0,1:T(8,128)(2,1)S(1)} collective-permute-done((bf16[128,2048]{0,1:T(8,128)(2,1)S(1)}, bf16[128,2048]{0,1:T(8,128)(2,1)S(1)}, u32[]{:S(2)}, u32[]{:S(2)}) %collective-permute-start.3) | collective-permute-done | bytes 524320 | tf_op jit(solution)/shard_map/ppermute | solution.py:118
  28.4 73.8 %all-gather.2.cloned.1.call-done = bf16[2048,3,1024]{2,0,1:T(8,128)(2,1)} async-done(((bf16[128,3,1024]{2,0,1:T(8,128)(2,1)}), bf16[2048,3,1024]{2,0,1:T(8,128)(2,1)}) %all-gather.2.cloned.1.call-update) | async-done | bytes 12582928 | tf_op jit(solution)/shard_map/all_gather | solution.py:139
  102.2 3.5 %fusion.4 = f32[1,256,1024]{2,1,0:T(8,128)S(1)} fusion(bf16[2048,3,1024]{2,0,1:T(8,128)(2,1)} %all-gather.2.cloned.1.call-done, bf16[128,2048]{0,1:T(8,128)(2,1)S(1)} %collective-permute-done.3, bf16[128,2048]{0,1:T(8,128)(2,1)S(1)} %bitcast.47), kind=kOutput, calls=%fused_computation.10 | convolution fusion | flops 1075838976 | bytes 6291456 | tf_op jit(solution)/shard_map/dot_general | solution.py:146
  105.6 3.5 %fusion.5 = f32[1,256,1024]{2,1,0:T(8,128)S(1)} fusion(bf16[2048,3,1024]{2,0,1:T(8,128)(2,1)} %all-gather.2.cloned.1.call-done, bf16[128,2048]{0,1:T(8,128)(2,1)S(1)} %collective-permute-done.3, bf16[128,2048]{0,1:T(8,128)(2,1)S(1)} %bitcast.48), kind=kOutput, calls=%fused_computation.11 | convolution fusion | flops 1075838976 | bytes 6291456 | tf_op jit(solution)/shard_map/dot_general | solution.py:146
  109.1 3.5 %fusion.6 = f32[1,256,1024]{2,1,0:T(8,128)S(1)} fusion(bf16[2048,3,1024]{2,0,1:T(8,128)(2,1)} %all-gather.2.cloned.1.call-done, bf16[128,2048]{0,1:T(8,128)(2,1)S(1)} %collective-permute-done.3, bf16[128,2048]{0,1:T(8,128)(2,1)S(1)} %bitcast.49), kind=kOutput, calls=%fused_computation.12 | convolution fusion | flops 1075838976 | bytes 6291456 | tf_op jit(solution)/shard_map/dot_general | solution.py:146
  112.6 0.4 pad_maximum_fusion
  113.2 0.6 copy-done
  113.9 2.8 %collective-permute-done.4 = f32[3,128,1024]{2,1,0:T(8,128)S(1)} collective-permute-done((f32[3,128,1024]{2,1,0:T(8,128)S(1)}, f32[3,128,1024]{2,1,0:T(8,128)S(1)}, u32[]{:S(2)}, u32[]{:S(2)}) %collective-permute-start.4) | collective-permute-done | bytes 1572896 | tf_op jit(solution)/shard_map/ppermute | solution.py:118
  116.6 0.3 fusion.3
  117.0 2.0 %collective-permute-start.5 = (bf16[3,2,1024]{2,1,0:T(2,128)(2,1)S(1)}, bf16[3,2,1024]{2,1,0:T(2,128)(2,1)S(1)}, u32[]{:S(2)}, u32[]{:S(2)}) collective-permute-start(bf16[3,2,1024]{2,1,0:T(2,128)(2,1)S(1)} %slice.43), channel_id=1, source_target_pairs={{0,4},{4,8},{8,12},{12,16},{16,20},{20,24},{24,28},{28,32},{32,36}... | collective-permute-start | bytes 36872 | tf_op jit(solution)/shard_map/ppermute | solution.py:114
  119.1 1.1 multiply_exponential_fusion
  120.2 0.6 copy.9
  120.8 0.6 reshape.48.taps_ref
  121.5 0.6 copy.10
  122.1 0.2 pad_maximum_fusion.3
  122.3 1.5 reshape.53.x_ref
  123.8 2.9 %shard_map.73.end_ref = f32[16,8,128]{2,1,0:T(8,128)} custom-call(f32[3,130,8,128]{3,2,1,0:T(8,128)} %reshape.53.x_ref, f32[3,3,8,128]{3,2,1,0:T(8,128)} %reshape.48.taps_ref, f32[16,8,128]{2,1,0:T(8,128)} %bitcast.45), custom_call_target="tpu_custom_call" | custom-call | tf_op jit(solution)/shard_map/pallas_call | solution.py:160
  126.7 21.9 %shard_map.74.start_ref = f32[16,8,128]{2,1,0:T(8,128)} custom-call(f32[16,8,128]{2,1,0:T(8,128)} %shard_map.73.end_ref, f32[7,16,8,128]{3,2,1,0:T(8,128)} %get-tuple-element.10.lift_ref, f32[7,16,8,128]{3,2,1,0:T(8,128)} %get-tuple-element.9.keep_ref), custom_call_target="tpu_custom_call" | custom-call | tf_op jit(solution)/shard_map/pallas_call | solution.py:177
  148.6 3.9 %shard_map.75 = f32[128,8,128]{2,1,0:T(8,128)} custom-call(f32[3,130,8,128]{3,2,1,0:T(8,128)} %reshape.53.x_ref, f32[3,3,8,128]{3,2,1,0:T(8,128)} %reshape.48.taps_ref, f32[16,8,128]{2,1,0:T(8,128)} %bitcast.46, f32[16,8,128]{2,1,0:T(8,128)} %bitcast.52, f32[8,128]{1,0:T(8,128)} %bitcast.58, f32[16,8,128]{2,1,0:T(8,128)} %shard_map.74.start_ref), custom_call_target="tpu_custom_call" | custom-call | tf_op jit(solution)/shard_map/pallas_call | solution.py:190
  152.5 1.1 convert_element_type.11
  153.5 0.8 copy.14
  (24 shorter events, 0.5 us)
Async XLA Ops:
  6.5 95.6 %all-gather.2.cloned.1.call-start = ((), (), s32[]{:S(2)}) async-start(), calls=%async_computation | async-start | bytes 13369344 | tf_op jit(solution)/shard_map/all_gather | solution.py:139
  7.3 9.7 %collective-permute-start = (bf16[128,1024]{1,0:T(8,128)(2,1)}, bf16[128,1024]{1,0:T(8,128)(2,1)S(1)}, u32[]{:S(2)}, u32[]{:S(2)}) collective-permute-start(bf16[128,1024]{1,0:T(8,128)(2,1)} %param.7), channel_id=1, source_target_pairs={{0,1},{1,2},{2,3},{3,0},{4,5},{5,6},{6,7},{7,4},{8,9},{9,10},{10,1... | collective-permute-start | bytes 786440 | tf_op jit(solution)/shard_map/ppermute | solution.py:125
  9.0 14.7 %collective-permute-start.1 = (bf16[128,1024]{1,0:T(8,128)(2,1)}, bf16[128,1024]{1,0:T(8,128)(2,1)S(1)}, u32[]{:S(2)}, u32[]{:S(2)}) collective-permute-start(bf16[128,1024]{1,0:T(8,128)(2,1)} %param.7), channel_id=1, source_target_pairs={{0,2},{1,3},{2,0},{3,1},{4,6},{5,7},{6,4},{7,5},{8,10},{9,11},{10,... | collective-permute-start | bytes 786440 | tf_op jit(solution)/shard_map/ppermute | solution.py:125
  11.9 11.9 %collective-permute-start.2 = (bf16[128,1024]{1,0:T(8,128)(2,1)}, bf16[128,1024]{1,0:T(8,128)(2,1)S(1)}, u32[]{:S(2)}, u32[]{:S(2)}) collective-permute-start(bf16[128,1024]{1,0:T(8,128)(2,1)} %param.7), channel_id=1, source_target_pairs={{0,3},{1,0},{2,1},{3,2},{4,7},{5,4},{6,5},{7,6},{8,11},{9,8},{10,9... | collective-permute-start | bytes 786440 | tf_op jit(solution)/shard_map/ppermute | solution.py:125
  26.4 2.0 %collective-permute-start.3 = (bf16[128,2048]{0,1:T(8,128)(2,1)S(1)}, bf16[128,2048]{0,1:T(8,128)(2,1)S(1)}, u32[]{:S(2)}, u32[]{:S(2)}) collective-permute-start(bf16[128,2048]{0,1:T(8,128)(2,1)S(1)} %bitcast.50), channel_id=1, source_target_pairs={{0,4},{4,0},{1,5},{5,1},{2,6},{6,2},{3,7},{7,3},{8,12},{12,8},{9,1... | collective-permute-start | bytes 1572872 | tf_op jit(solution)/shard_map/ppermute | solution.py:118
  113.0 0.8 copy-start
  113.0 6.1 %copy-start.3 = (f32[7]{0:T(128)S(1)}, f32[7]{0:T(128)}, u32[]{:S(2)}) copy-start(f32[7]{0:T(128)} %constant.47) | copy-start | bytes 88
  113.0 6.1 %copy-start.4 = (f32[7]{0:T(128)S(1)}, f32[7]{0:T(128)}, u32[]{:S(2)}) copy-start(f32[7]{0:T(128)} %constant.48) | copy-start | bytes 88
  113.1 7.7 %copy-start.2 = (f32[3,3,1024]{2,1,0:T(4,128)S(1)}, f32[3,3,1024]{2,1,0:T(4,128)}, u32[]{:S(2)}) copy-start(f32[3,3,1024]{2,1,0:T(4,128)} %param.9) | copy-start | bytes 110596
  113.1 8.3 %copy-start.1 = (f32[16,1024]{1,0:T(8,128)S(1)}, f32[16,1024]{1,0:T(8,128)}, u32[]{:S(2)}) copy-start(f32[16,1024]{1,0:T(8,128)} %param.11) | copy-start | bytes 196612
  113.1 3.5 %collective-permute-start.4 = (f32[3,128,1024]{2,1,0:T(8,128)S(1)}, f32[3,128,1024]{2,1,0:T(8,128)S(1)}, u32[]{:S(2)}, u32[]{:S(2)}) collective-permute-start(f32[3,128,1024]{2,1,0:T(8,128)S(1)} %slice.42), channel_id=1, source_target_pairs={{0,4},{4,0},{1,5},{5,1},{2,6},{6,2},{3,7},{7,3},{8,12},{12,8},{9,1... | collective-permute-start | bytes 4718600 | tf_op jit(solution)/shard_map/ppermute | solution.py:118
  117.0 5.1 %collective-permute-start.5 = (bf16[3,2,1024]{2,1,0:T(2,128)(2,1)S(1)}, bf16[3,2,1024]{2,1,0:T(2,128)(2,1)S(1)}, u32[]{:S(2)}, u32[]{:S(2)}) collective-permute-start(bf16[3,2,1024]{2,1,0:T(2,128)(2,1)S(1)} %slice.43), channel_id=1, source_target_pairs={{0,4},{4,8},{8,12},{12,16},{16,20},{20,24},{24,28},{28,32},{32,36}... | collective-permute-start | bytes 36872 | tf_op jit(solution)/shard_map/ppermute | solution.py:114
Sparse Core Ops, SparseCore 0:
  9.5 92.6 all-gather.1

commit v5 on v4

--- a/solution.py
+++ b/solution.py
@@ -129,19 +129,11 @@
     return jnp.transpose(placed, (1, 0, 2)).reshape(tokens.shape[0], -1)
 
 
-def per_device(tokens, in_weight, conv_taps, decay_rate, residue, skip):
+def block_half(both, piece, conv_taps, decay_rate, residue, skip, rows, tag):
     ctx = ("cx", "core")
-    rows = tokens.shape[0]
-    chans = in_weight.shape[2]
+    chans = piece.shape[2]
     poles = decay_rate.shape[0]
     subl = chans // LANES
-    core = lax.axis_index("core")
-    piece = lax.all_gather(in_weight, "cx", axis=0, tiled=True)
-    whole = gathered_tp(tokens)
-    split = whole.reshape(rows, -1, 2, in_weight.shape[0])
-    mine = jnp.where(core == 0, split[:, :, 0], split[:, :, 1]).reshape(rows, -1)
-    theirs = jnp.where(core == 0, split[:, :, 1], split[:, :, 0]).reshape(rows, -1)
-    both = jnp.concatenate([mine, swapped(theirs, "core")], axis=0)
     partial = jnp.stack(
         [jnp.dot(both, piece[:, g, :], preferred_element_type=jnp.float32) for g in range(3)],
         axis=0,
@@ -162,6 +154,9 @@
         out_shape=jax.ShapeDtypeStruct((poles, subl, LANES), jnp.float32),
         in_specs=vmem_specs(3),
         out_specs=pl.BlockSpec(memory_space=pltpu.VMEM),
+        cost_estimate=pl.CostEstimate(
+            flops=40 * rows * poles * chans, transcendentals=0, bytes_accessed=x.size * 4
+        ),
     )(x, taps, decay)
     peers = lax.axis_size("cx") * lax.axis_size("core")
     digits = scan_digits(peers)
@@ -185,15 +180,49 @@
             pltpu.SemaphoreType.DMA((copies,)),
             pltpu.SemaphoreType.DMA((copies,)),
         ],
-        compiler_params=pltpu.CompilerParams(collective_id=0, has_side_effects=True),
+        compiler_params=pltpu.CompilerParams(collective_id=tag, has_side_effects=True),
+        cost_estimate=pl.CostEstimate(
+            flops=400 * rows * poles * chans, transcendentals=0, bytes_accessed=lift.size * 8
+        ),
     )(end, lift, keep)
     out = pl.pallas_call(
         mixed_kernel,
         out_shape=jax.ShapeDtypeStruct((rows, subl, LANES), jnp.float32),
         in_specs=vmem_specs(6),
         out_specs=pl.BlockSpec(memory_space=pltpu.VMEM),
+        cost_estimate=pl.CostEstimate(
+            flops=80 * rows * poles * chans, transcendentals=0, bytes_accessed=x.size * 4
+        ),
     )(x, taps, decay, resid, direct, start)
-    return out.reshape(rows, chans).astype(jnp.bfloat16)
+    return out.reshape(rows, chans)
+
+
+def per_device(tokens, in_weight, conv_taps, decay_rate, residue, skip):
+    rows = tokens.shape[0]
+    chans = in_weight.shape[2]
+    core = lax.axis_index("core")
+    whole = gathered_tp(tokens)
+    split = whole.reshape(rows, -1, 2, in_weight.shape[0])
+    mine = jnp.where(core == 0, split[:, :, 0], split[:, :, 1]).reshape(rows, -1)
+    theirs = jnp.where(core == 0, split[:, :, 1], split[:, :, 0]).reshape(rows, -1)
+    both = jnp.concatenate([mine, swapped(theirs, "core")], axis=0)
+    pieces = 2 if chans % (2 * LANES) == 0 else 1
+    width = chans // pieces
+    cuts = [slice(h * width, (h + 1) * width) for h in range(pieces)]
+    gathered_w = [lax.all_gather(in_weight[:, :, cut], "cx", axis=0, tiled=True) for cut in cuts]
+    outs = []
+    for h, cut in enumerate(cuts):
+        piece = gathered_w[h]
+        if outs:
+            piece, done = lax.optimization_barrier((piece, outs[-1]))
+            outs[-1] = done
+        outs.append(
+            block_half(
+                both, piece, conv_taps[:, :, cut], decay_rate[:, cut],
+                residue[:, cut], skip[cut], rows, h,
+            )
+        )
+    return jnp.concatenate(outs, axis=1).astype(jnp.bfloat16)
 
 
 def solution(mesh):

time: 162 us -> 186 us (1.15)
  Pallas kernels: 28.7 us -> 50 us
  waiting for transfers between devices: 88.9 us -> 80.4 us
  local copies, waits for them, and re-layouts: 6.16 us -> 11.8 us
  matrix products: 10.4 us -> 13.9 us
  starting transfers between devices: 8.19 us -> 10.4 us
    pallas_call x3 -> x6, Pallas kernels: 28.7 us -> 50 us  [the longest x2 37.2 us: block_half(): pl.pallas_call(functools.partial(carry_kernel, peers, digits), out_shape=...]
    all_gather x1 -> x2, waiting for transfers between devices: 73.8 us -> 65.5 us  [per_device(): lax.all_gather(in_weight[:, :, cut], 'cx', axis=0, tiled=True)]
    reshape x2 -> x8, local copies, waits for them, and re-layouts: 2.11 us -> 6.07 us  [the longest x2 2.35 us: block_half(): x = values.reshape(3, rows + 2, subl, LANES)]
    dot_general x3 -> x6, matrix products: 10.4 us -> 13.9 us  [block_half(): jnp.dot(both, piece[:, g, :], preferred_element_type=jnp.float32)]
    slice x2 -> x8, local copies, waits for them, and re-layouts: 0.12 us -> 2.88 us  [the longest x1 2.14 us: per_device(): in_weight[:, :, cut]]
    ppermute x1 -> x2, starting transfers between devices: 2.04 us -> 4.08 us  [shifted(): return lax.ppermute(array, axes, pairs)]
    ppermute x2 -> x3, waiting for transfers between devices: 4.67 us -> 4.68 us  [swapped(): return lax.ppermute(array, axis, [(0, 1), (1, 0)])]
  transfers between devices with their start and end apart: 7 -> 10, of which waited for: 5 -> 7; matrix products, arithmetic and copies ran while one was open for 4% -> 9% of each run, Pallas kernels for 0% -> 14%
where the time goes in v5:
time: 186 us; the launch traced here: 185 us
  waiting for transfers between devices  80.4 us (43%)
  Pallas kernels  50 us (27%)
  matrix products  13.9 us (7%)
  between operations  13.8 us (7%)
  local copies, waits for them, and re-layouts  11.8 us (6%)
  starting transfers between devices  10.4 us (6%)
  other arithmetic  4.83 us (3%)
    all_gather x2, waiting for transfers between devices, per_device(): lax.all_gather(in_weight[:, :, cut], 'cx', axis=0, tiled=True)  65.5 us
    pallas_call x2, Pallas kernels, block_half(): pl.pallas_call(functools.partial(carry_kernel, peers, digits), out_shape=...  37.2 us
    dot_general x6, matrix products, block_half(): jnp.dot(both, piece[:, g, :], preferred_element_type=jnp.float32)  13.9 us
    ppermute x3, waiting for transfers between devices, gathered_tp(): lax.ppermute(tokens, 'tp', [(i, (i + by) % peers) for i in range(peers)])  9.5 us
    pallas_call x2, Pallas kernels, block_half(): pl.pallas_call(mixed_kernel, out_shape=jax.ShapeDtypeStruct((rows, subl,...  7.53 us
    ppermute x3, starting transfers between devices, gathered_tp(): lax.ppermute(tokens, 'tp', [(i, (i + by) % peers) for i in range(peers)])  5.98 us
    pallas_call x2, Pallas kernels, block_half(): pl.pallas_call(local_end_kernel, out_shape=jax.ShapeDtypeStruct((poles, s...  5.27 us
    ppermute x3, waiting for transfers between devices, swapped(): return lax.ppermute(array, axis, [(0, 1), (1, 0)])  4.68 us
  transfers between devices with their start and end apart: 10, of which 7 were waited for; matrix products, arithmetic and copies ran while one was open for 9% of the time, Pallas kernels for 14%

profile of v5, /device:TPU:0, one launch (start us, length us, event | category | flops | bytes accessed | tf_op | source)
XLA Modules:
  0.0 185.0 jit_solution(6793535436543965393)
XLA Ops:
  6.5 2.1 %fusion.29 = (bf16[128,3,512]{2,0,1:T(8,128)(2,1)}, bf16[128,3,512]{2,0,1:T(8,128)(2,1)}) fusion(bf16[128,3,1024]{2,0,1:T(8,128)(2,1)} %param.9), kind=kLoop, calls=%fused_computation.55 | loop fusion | bytes 1572864 | tf_op jit(solution)/shard_map/slice | solution.py:212
  8.8 0.7 all-gather.3.cloned.1.call-update
  9.5 1.7 collective-permute-start
  11.2 2.9 %collective-permute-start.1 = (bf16[128,1024]{1,0:T(8,128)(2,1)S(1)}, bf16[128,1024]{1,0:T(8,128)(2,1)S(1)}, u32[]{:S(2)}, u32[]{:S(2)}) collective-permute-start(bf16[128,1024]{1,0:T(8,128)(2,1)S(1)} %copy-done.2), channel_id=1, source_target_pairs={{0,2},{1,3},{2,0},{3,1},{4,6},{5,7},{6,4},{7,5},{8,10},{9,11},{10,... | collective-permute-start | bytes 786440 | tf_op jit(solution)/shard_map/ppermute | solution.py:125
  14.1 1.3 collective-permute-start.2
  15.5 0.7 sort.17
  16.2 2.7 %collective-permute-done = bf16[128,1024]{1,0:T(8,128)(2,1)S(1)} collective-permute-done((bf16[128,1024]{1,0:T(8,128)(2,1)S(1)}, bf16[128,1024]{1,0:T(8,128)(2,1)S(1)}, u32[]{:S(2)}, u32[]{:S(2)}) %collective-permute-start) | collective-permute-done | bytes 262176 | tf_op jit(solution)/shard_map/ppermute | solution.py:125
  18.9 6.8 %collective-permute-done.1 = bf16[128,1024]{1,0:T(8,128)(2,1)S(1)} collective-permute-done((bf16[128,1024]{1,0:T(8,128)(2,1)S(1)}, bf16[128,1024]{1,0:T(8,128)(2,1)S(1)}, u32[]{:S(2)}, u32[]{:S(2)}) %collective-permute-start.1) | collective-permute-done | bytes 262176 | tf_op jit(solution)/shard_map/ppermute | solution.py:125
  27.5 1.9 %collective-permute-done.3 = bf16[128,2048]{0,1:T(8,128)(2,1)S(1)} collective-permute-done((bf16[128,2048]{0,1:T(8,128)(2,1)S(1)}, bf16[128,2048]{0,1:T(8,128)(2,1)S(1)}, u32[]{:S(2)}, u32[]{:S(2)}) %collective-permute-start.3) | collective-permute-done | bytes 524320 | tf_op jit(solution)/shard_map/ppermute | solution.py:118
  29.4 44.0 %all-gather.5.cloned.1.call-done = bf16[2048,3,512]{2,0,1:T(8,128)(2,1)} async-done(((bf16[128,3,512]{2,0,1:T(8,128)(2,1)}), bf16[2048,3,512]{2,0,1:T(8,128)(2,1)}) %all-gather.5.cloned.1.call-update) | async-done | bytes 6291472 | tf_op jit(solution)/shard_map/all_gather | solution.py:212
  73.4 2.3 %fusion.21 = f32[1,256,512]{2,1,0:T(8,128)S(1)} fusion(bf16[2048,3,512]{2,0,1:T(8,128)(2,1)} %all-gather.5.cloned.1.call-done, bf16[128,2048]{0,1:T(8,128)(2,1)S(1)} %collective-permute-done.3, bf16[128,2048]{0,1:T(8,128)(2,1)S(1)} %bitcast.65), kind=kOutput, calls=%fused_computation.21 | convolution fusion | flops 538968064 | bytes 3670016 | tf_op jit(solution)/shard_map/dot_general | solution.py:138
  75.7 2.3 %fusion.22 = f32[1,256,512]{2,1,0:T(8,128)S(1)} fusion(bf16[2048,3,512]{2,0,1:T(8,128)(2,1)} %all-gather.5.cloned.1.call-done, bf16[128,2048]{0,1:T(8,128)(2,1)S(1)} %collective-permute-done.3, bf16[128,2048]{0,1:T(8,128)(2,1)S(1)} %bitcast.66), kind=kOutput, calls=%fused_computation.22 | convolution fusion | flops 538968064 | bytes 3670016 | tf_op jit(solution)/shard_map/dot_general | solution.py:138
  78.1 2.3 %fusion.23 = f32[1,256,512]{2,1,0:T(8,128)S(1)} fusion(bf16[2048,3,512]{2,0,1:T(8,128)(2,1)} %all-gather.5.cloned.1.call-done, bf16[128,2048]{0,1:T(8,128)(2,1)S(1)} %collective-permute-done.3, bf16[128,2048]{0,1:T(8,128)(2,1)S(1)} %bitcast.67), kind=kOutput, calls=%fused_computation.23 | convolution fusion | flops 538968064 | bytes 3670016 | tf_op jit(solution)/shard_map/dot_general | solution.py:138
  81.4 1.1 multiply_exponential_fusion.2
  83.2 2.0 %collective-permute-start.5 = (bf16[3,2,512]{2,1,0:T(2,128)(2,1)S(1)}, bf16[3,2,512]{2,1,0:T(2,128)(2,1)S(1)}, u32[]{:S(2)}, u32[]{:S(2)}) collective-permute-start(bf16[3,2,512]{2,1,0:T(2,128)(2,1)S(1)} %slice.129), channel_id=1, source_target_pairs={{0,4},{4,8},{8,12},{12,16},{16,20},{20,24},{24,28},{28,32},{32,36}... | collective-permute-start | bytes 18440 | tf_op jit(solution)/shard_map/ppermute | solution.py:114
  87.8 1.2 reshape.105.x_ref
  89.0 2.7 %shard_map.82.end_ref = f32[16,4,128]{2,1,0:T(4,128)} custom-call(f32[3,130,4,128]{3,2,1,0:T(4,128)} %reshape.105.x_ref, f32[3,3,4,128]{3,2,1,0:T(4,128)} %reshape.94.taps_ref, f32[16,4,128]{2,1,0:T(4,128)} %reshape.95.decay_ref), custom_call_target="tpu_custom_call" | custom-call | flops 41943040 | bytes 798720 | tf_op jit(solution)/shard_map/pallas_call | solution.py:152
  91.7 18.6 %shard_map.83.start_ref = f32[16,4,128]{2,1,0:T(4,128)} custom-call(f32[16,4,128]{2,1,0:T(4,128)} %shard_map.82.end_ref, f32[7,16,4,128]{3,2,1,0:T(4,128)} %get-tuple-element.26.lift_ref, f32[7,16,4,128]{3,2,1,0:T(4,128)} %get-tuple-element.25.keep_ref), custom_call_target="tpu_custom_call" | custom-call | flops 419430400 | bytes 458752 | tf_op jit(solution)/shard_map/pallas_call | solution.py:172
  110.3 3.8 %shard_map.84 = f32[128,4,128]{2,1,0:T(4,128)} custom-call(f32[3,130,4,128]{3,2,1,0:T(4,128)} %reshape.105.x_ref, f32[3,3,4,128]{3,2,1,0:T(4,128)} %reshape.94.taps_ref, f32[16,4,128]{2,1,0:T(4,128)} %reshape.95.decay_ref, f32[16,4,128]{2,1,0:T(4,128)} %reshape.96.resid_ref, f32[4,128]{1,0:T(4,128)} %get-tuple-element.28.skip_ref, ...), custom_call_target="tpu_custom_call" | custom-call | flops 83886080 | bytes 798720 | tf_op jit(solution)/shard_map/pallas_call | solution.py:188
  114.1 1.0 copy.14
  115.1 21.5 %all-gather.3.cloned.1.call-done = bf16[2048,3,512]{2,0,1:T(8,128)(2,1)} async-done(((bf16[128,3,512]{2,0,1:T(8,128)(2,1)}), bf16[2048,3,512]{2,0,1:T(8,128)(2,1)}) %all-gather.3.cloned.1.call-update) | async-done | bytes 6291472 | tf_op jit(solution)/shard_map/all_gather | solution.py:212
  136.6 2.3 %fusion.12 = f32[1,256,512]{2,1,0:T(8,128)S(1)} fusion(bf16[2048,3,512]{2,0,1:T(8,128)(2,1)} %all-gather.3.cloned.1.call-done, bf16[128,2048]{0,1:T(8,128)(2,1)S(1)} %copy-done.10, bf16[128,2048]{0,1:T(8,128)(2,1)S(1)} %bitcast.68), kind=kOutput, calls=%fused_computation.18 | convolution fusion | flops 538968064 | bytes 3670016 | tf_op jit(solution)/shard_map/dot_general | solution.py:138
  138.9 2.3 %fusion.15 = f32[1,256,512]{2,1,0:T(8,128)S(1)} fusion(bf16[2048,3,512]{2,0,1:T(8,128)(2,1)} %all-gather.3.cloned.1.call-done, bf16[128,2048]{0,1:T(8,128)(2,1)S(1)} %copy-done.10, bf16[128,2048]{0,1:T(8,128)(2,1)S(1)} %bitcast.69), kind=kOutput, calls=%fused_computation.19 | convolution fusion | flops 538968064 | bytes 3670016 | tf_op jit(solution)/shard_map/dot_general | solution.py:138
  141.2 2.3 %fusion.18 = f32[1,256,512]{2,1,0:T(8,128)S(1)} fusion(bf16[2048,3,512]{2,0,1:T(8,128)(2,1)} %all-gather.3.cloned.1.call-done, bf16[128,2048]{0,1:T(8,128)(2,1)S(1)} %copy-done.10, bf16[128,2048]{0,1:T(8,128)(2,1)S(1)} %bitcast.70), kind=kOutput, calls=%fused_computation.20 | convolution fusion | flops 538968064 | bytes 3670016 | tf_op jit(solution)/shard_map/dot_general | solution.py:138
  143.8 2.3 %collective-permute-done.6 = f32[3,128,512]{2,1,0:T(8,128)S(1)} collective-permute-done((f32[3,128,512]{2,1,0:T(8,128)S(1)}, f32[3,128,512]{2,1,0:T(8,128)S(1)}, u32[]{:S(2)}, u32[]{:S(2)}) %collective-permute-start.6) | collective-permute-done | bytes 786464 | tf_op jit(solution)/shard_map/ppermute | solution.py:118
  146.3 2.0 %collective-permute-start.7 = (bf16[3,2,512]{2,1,0:T(2,128)(2,1)S(1)}, bf16[3,2,512]{2,1,0:T(2,128)(2,1)S(1)}, u32[]{:S(2)}, u32[]{:S(2)}) collective-permute-start(bf16[3,2,512]{2,1,0:T(2,128)(2,1)S(1)} %slice.132), channel_id=1, source_target_pairs={{0,4},{4,8},{8,12},{12,16},{16,20},{20,24},{24,28},{28,32},{32,36}... | collective-permute-start | bytes 18440 | tf_op jit(solution)/shard_map/ppermute | solution.py:114
  150.3 1.2 reshape.107.x_ref
  151.5 2.6 %shard_map.85.end_ref = f32[16,4,128]{2,1,0:T(4,128)} custom-call(f32[3,130,4,128]{3,2,1,0:T(4,128)} %reshape.107.x_ref, f32[3,3,4,128]{3,2,1,0:T(4,128)} %reshape.100.taps_ref, f32[16,4,128]{2,1,0:T(4,128)} %reshape.101.decay_ref), custom_call_target="tpu_custom_call" | custom-call | flops 41943040 | bytes 798720 | tf_op jit(solution)/shard_map/pallas_call | solution.py:152
  154.1 18.6 %shard_map.86.start_ref = f32[16,4,128]{2,1,0:T(4,128)} custom-call(f32[16,4,128]{2,1,0:T(4,128)} %shard_map.85.end_ref, f32[7,16,4,128]{3,2,1,0:T(4,128)} %get-tuple-element.29.lift_ref, f32[7,16,4,128]{3,2,1,0:T(4,128)} %get-tuple-element.30.keep_ref), custom_call_target="tpu_custom_call" | custom-call | flops 419430400 | bytes 458752 | tf_op jit(solution)/shard_map/pallas_call | solution.py:172
  172.7 3.8 %shard_map.87 = f32[128,4,128]{2,1,0:T(4,128)} custom-call(f32[3,130,4,128]{3,2,1,0:T(4,128)} %reshape.107.x_ref, f32[3,3,4,128]{3,2,1,0:T(4,128)} %reshape.100.taps_ref, f32[16,4,128]{2,1,0:T(4,128)} %reshape.101.decay_ref, f32[16,4,128]{2,1,0:T(4,128)} %reshape.102.resid_ref, f32[4,128]{1,0:T(4,128)} %get-tuple-element.27.skip_ref, ...), custom_call_target="tpu_custom_call" | custom-call | flops 83886080 | bytes 798720 | tf_op jit(solution)/shard_map/pallas_call | solution.py:188
  176.4 1.0 convert.10
  177.4 0.7 pad_maximum_fusion.6
  (65 shorter events, 8.4 us)
Async XLA Ops:
  6.5 2.9 %copy-start.2 = (bf16[128,1024]{1,0:T(8,128)(2,1)S(1)}, bf16[128,1024]{1,0:T(8,128)(2,1)}, u32[]{:S(2)}) copy-start(bf16[128,1024]{1,0:T(8,128)(2,1)} %param.8) | copy-start | bytes 786436
  6.5 66.9 %all-gather.5.cloned.1.call-start = ((), (), s32[]{:S(2)}) async-start(), calls=%async_computation.1 | async-start | bytes 6684672 | tf_op jit(solution)/shard_map/all_gather | solution.py:212
  8.7 127.9 %all-gather.3.cloned.1.call-start = ((), (), s32[]{:S(2)}) async-start(), calls=%async_computation | async-start | bytes 6684672 | tf_op jit(solution)/shard_map/all_gather | solution.py:212
  9.5 9.5 %collective-permute-start = (bf16[128,1024]{1,0:T(8,128)(2,1)S(1)}, bf16[128,1024]{1,0:T(8,128)(2,1)S(1)}, u32[]{:S(2)}, u32[]{:S(2)}) collective-permute-start(bf16[128,1024]{1,0:T(8,128)(2,1)S(1)} %copy-done.2), channel_id=1, source_target_pairs={{0,1},{1,2},{2,3},{3,0},{4,5},{5,6},{6,7},{7,4},{8,9},{9,10},{10,1... | collective-permute-start | bytes 786440 | tf_op jit(solution)/shard_map/ppermute | solution.py:125
  11.2 14.5 %collective-permute-start.1 = (bf16[128,1024]{1,0:T(8,128)(2,1)S(1)}, bf16[128,1024]{1,0:T(8,128)(2,1)S(1)}, u32[]{:S(2)}, u32[]{:S(2)}) collective-permute-start(bf16[128,1024]{1,0:T(8,128)(2,1)S(1)} %copy-done.2), channel_id=1, source_target_pairs={{0,2},{1,3},{2,0},{3,1},{4,6},{5,7},{6,4},{7,5},{8,10},{9,11},{10,... | collective-permute-start | bytes 786440 | tf_op jit(solution)/shard_map/ppermute | solution.py:125
  14.1 11.6 %collective-permute-start.2 = (bf16[128,1024]{1,0:T(8,128)(2,1)S(1)}, bf16[128,1024]{1,0:T(8,128)(2,1)S(1)}, u32[]{:S(2)}, u32[]{:S(2)}) collective-permute-start(bf16[128,1024]{1,0:T(8,128)(2,1)S(1)} %copy-done.2), channel_id=1, source_target_pairs={{0,3},{1,0},{2,1},{3,2},{4,7},{5,4},{6,5},{7,6},{8,11},{9,8},{10,9... | collective-permute-start | bytes 786440 | tf_op jit(solution)/shard_map/ppermute | solution.py:125
  27.4 50.6 %copy-start = (bf16[128,16,1,128]{0,3,2,1:T(8,128)(2,1)}, bf16[128,16,1,128]{0,3,2,1:T(8,128)(2,1)S(1)}, u32[]{:S(2)}) copy-start(bf16[128,16,1,128]{0,3,2,1:T(8,128)(2,1)S(1)} %get-tuple-element.11) | copy-start | bytes 1572868
  27.4 2.0 %collective-permute-start.3 = (bf16[128,2048]{0,1:T(8,128)(2,1)S(1)}, bf16[128,2048]{0,1:T(8,128)(2,1)S(1)}, u32[]{:S(2)}, u32[]{:S(2)}) collective-permute-start(bf16[128,2048]{0,1:T(8,128)(2,1)S(1)} %bitcast.71), channel_id=1, source_target_pairs={{0,4},{4,0},{1,5},{5,1},{2,6},{6,2},{3,7},{7,3},{8,12},{12,8},{9,1... | collective-permute-start | bytes 1572872 | tf_op jit(solution)/shard_map/ppermute | solution.py:118
  29.4 48.6 %copy-start.9 = (bf16[128,2048]{0,1:T(8,128)(2,1)}, bf16[128,2048]{0,1:T(8,128)(2,1)S(1)}, u32[]{:S(2)}) copy-start(bf16[128,2048]{0,1:T(8,128)(2,1)S(1)} %collective-permute-done.3) | copy-start | bytes 1572868
  80.4 0.8 copy-start.3
  80.4 0.9 copy-start.5
  80.4 0.9 copy-start.4
  80.4 0.9 copy-start.7
  80.4 0.9 copy-start.8
  80.6 4.6 %copy-start.6 = (f32[1024]{0:T(1024)S(1)}, f32[1024]{0:T(1024)}, u32[]{:S(2)}) copy-start(f32[1024]{0:T(1024)} %param.13) | copy-start | bytes 12292
  80.6 2.4 %collective-permute-start.4 = (f32[3,128,512]{2,1,0:T(8,128)S(1)}, f32[3,128,512]{2,1,0:T(8,128)S(1)}, u32[]{:S(2)}, u32[]{:S(2)}) collective-permute-start(f32[3,128,512]{2,1,0:T(8,128)S(1)} %slice.128), channel_id=1, source_target_pairs={{0,4},{4,0},{1,5},{5,1},{2,6},{6,2},{3,7},{7,3},{8,12},{12,8},{9,1... | collective-permute-start | bytes 2359304 | tf_op jit(solution)/shard_map/ppermute | solution.py:118
  83.2 4.5 %collective-permute-start.5 = (bf16[3,2,512]{2,1,0:T(2,128)(2,1)S(1)}, bf16[3,2,512]{2,1,0:T(2,128)(2,1)S(1)}, u32[]{:S(2)}, u32[]{:S(2)}) collective-permute-start(bf16[3,2,512]{2,1,0:T(2,128)(2,1)S(1)} %slice.129), channel_id=1, source_target_pairs={{0,4},{4,8},{8,12},{12,16},{16,20},{20,24},{24,28},{28,32},{32,36}... | collective-permute-start | bytes 18440 | tf_op jit(solution)/shard_map/ppermute | solution.py:114
  89.0 47.6 %copy-start.1 = (bf16[128,16,1,128]{0,3,2,1:T(8,128)(2,1)S(1)}, bf16[128,16,1,128]{0,3,2,1:T(8,128)(2,1)}, u32[]{:S(2)}) copy-start(bf16[128,16,1,128]{0,3,2,1:T(8,128)(2,1)} %copy-done) | copy-start | bytes 1572868
  89.0 47.6 %copy-start.10 = (bf16[128,2048]{0,1:T(8,128)(2,1)S(1)}, bf16[128,2048]{0,1:T(8,128)(2,1)}, u32[]{:S(2)}) copy-start(bf16[128,2048]{0,1:T(8,128)(2,1)} %copy-done.9) | copy-start | bytes 1572868
  143.7 2.4 %collective-permute-start.6 = (f32[3,128,512]{2,1,0:T(8,128)S(1)}, f32[3,128,512]{2,1,0:T(8,128)S(1)}, u32[]{:S(2)}, u32[]{:S(2)}) collective-permute-start(f32[3,128,512]{2,1,0:T(8,128)S(1)} %slice.131), channel_id=1, source_target_pairs={{0,4},{4,0},{1,5},{5,1},{2,6},{6,2},{3,7},{7,3},{8,12},{12,8},{9,1... | collective-permute-start | bytes 2359304 | tf_op jit(solution)/shard_map/ppermute | solution.py:118
  146.3 3.9 %collective-permute-start.7 = (bf16[3,2,512]{2,1,0:T(2,128)(2,1)S(1)}, bf16[3,2,512]{2,1,0:T(2,128)(2,1)S(1)}, u32[]{:S(2)}, u32[]{:S(2)}) collective-permute-start(bf16[3,2,512]{2,1,0:T(2,128)(2,1)S(1)} %slice.132), channel_id=1, source_target_pairs={{0,4},{4,8},{8,12},{12,16},{16,20},{20,24},{24,28},{28,32},{32,36}... | collective-permute-start | bytes 18440 | tf_op jit(solution)/shard_map/ppermute | solution.py:114
Sparse Core Ops, SparseCore 0:
  9.5 63.8 all-gather.4
  75.6 60.9 all-gather.2

commit v6 on v4

--- a/solution.py
+++ b/solution.py
@@ -46,7 +46,10 @@
     lax.fori_loop(0, rows, step, start_ref[...], unroll=8)
 
 
-def carry_kernel(peers, digits, end_ref, lift_ref, keep_ref, start_ref, held, slots, send_sem, recv_sem):
+def block_kernel(
+    peers, digits, x_ref, taps_ref, decay_ref, resid_ref, skip_ref, lift_ref, keep_ref, out_ref,
+    end_ref, start_ref, held, slots, send_sem, recv_sem,
+):
     me = lax.axis_index("cx") * 2 + lax.axis_index("core")
     tp = lax.axis_index("tp")
 
@@ -63,6 +66,7 @@
     for _, by in steps:
         for peer in ((me + by) % peers, (me + peers - by) % peers):
             pl.semaphore_signal(barrier, inc=1, device_id=device(peer), device_id_type=MESH)
+    local_end_kernel(x_ref, taps_ref, decay_ref, end_ref)
     pl.semaphore_wait(barrier, 2 * len(steps))
 
     held[0] = end_ref[...]
@@ -89,6 +93,7 @@
             grown = grown + keep_ref[n] * got
         if r + 1 < len(digits):
             held[r + 1] = grown
+    mixed_kernel(x_ref, taps_ref, decay_ref, resid_ref, skip_ref, start_ref, out_ref)
     for copy in copies:
         copy.wait_send()
 
@@ -157,12 +162,6 @@
     resid = residue.reshape(poles, subl, LANES)
     direct = skip.reshape(subl, LANES)
 
-    end = pl.pallas_call(
-        local_end_kernel,
-        out_shape=jax.ShapeDtypeStruct((poles, subl, LANES), jnp.float32),
-        in_specs=vmem_specs(3),
-        out_specs=pl.BlockSpec(memory_space=pltpu.VMEM),
-    )(x, taps, decay)
     peers = lax.axis_size("cx") * lax.axis_size("core")
     digits = scan_digits(peers)
     strides, width = [], 1
@@ -174,25 +173,21 @@
     lift = jnp.exp(-decay_rate[None] * (rows * (widths - 1.0))).reshape(copies, poles, subl, LANES)
     keep = jnp.exp(-decay_rate[None] * (rows * widths)).reshape(copies, poles, subl, LANES)
     state_shape = (poles, subl, LANES)
-    start = pl.pallas_call(
-        functools.partial(carry_kernel, peers, digits),
-        out_shape=jax.ShapeDtypeStruct(state_shape, jnp.float32),
-        in_specs=vmem_specs(3),
+    out = pl.pallas_call(
+        functools.partial(block_kernel, peers, digits),
+        out_shape=jax.ShapeDtypeStruct((rows, subl, LANES), jnp.float32),
+        in_specs=vmem_specs(7),
         out_specs=pl.BlockSpec(memory_space=pltpu.VMEM),
         scratch_shapes=[
+            pltpu.VMEM(state_shape, jnp.float32),
+            pltpu.VMEM(state_shape, jnp.float32),
             pltpu.VMEM((len(digits),) + state_shape, jnp.float32),
             pltpu.VMEM((copies,) + state_shape, jnp.float32),
             pltpu.SemaphoreType.DMA((copies,)),
             pltpu.SemaphoreType.DMA((copies,)),
         ],
         compiler_params=pltpu.CompilerParams(collective_id=0, has_side_effects=True),
-    )(end, lift, keep)
-    out = pl.pallas_call(
-        mixed_kernel,
-        out_shape=jax.ShapeDtypeStruct((rows, subl, LANES), jnp.float32),
-        in_specs=vmem_specs(6),
-        out_specs=pl.BlockSpec(memory_space=pltpu.VMEM),
-    )(x, taps, decay, resid, direct, start)
+    )(x, taps, decay, resid, direct, lift, keep)
     return out.reshape(rows, chans).astype(jnp.bfloat16)
 
 

time: 162 us -> 157 us (0.969)
  Pallas kernels: 28.7 us -> 24.2 us
    pallas_call x3 -> x1, Pallas kernels: 28.7 us -> 24.2 us  [per_device(): pl.pallas_call(functools.partial(block_kernel, peers, digits), out_shape=...]
where the time goes in v6:
time: 157 us
  waiting for transfers between devices  88.9 us (57%)
  Pallas kernels  24.2 us (15%)
  between operations  13.6 us (9%)
  matrix products  10.4 us (7%)
  starting transfers between devices  8.19 us (5%)
  local copies, waits for them, and re-layouts  6.16 us (4%)
  other arithmetic  5.31 us (3%)
    all_gather x1, waiting for transfers between devices, per_device(): piece = lax.all_gather(in_weight, 'cx', axis=0, tiled=True)  73.8 us
    pallas_call x1, Pallas kernels, per_device(): pl.pallas_call(functools.partial(block_kernel, peers, digits), out_shape=...  24.2 us
    dot_general x3, matrix products, per_device(): jnp.dot(both, piece[:, g, :], preferred_element_type=jnp.float32)  10.4 us
    ppermute x3, waiting for transfers between devices, gathered_tp(): lax.ppermute(tokens, 'tp', [(i, (i + by) % peers) for i in range(peers)])  9.71 us
    ppermute x3, starting transfers between devices, gathered_tp(): lax.ppermute(tokens, 'tp', [(i, (i + by) % peers) for i in range(peers)])  5.98 us
    ppermute x2, waiting for transfers between devices, swapped(): return lax.ppermute(array, axis, [(0, 1), (1, 0)])  4.67 us
  transfers between devices with their start and end apart: 7, of which 5 were waited for; matrix products, arithmetic and copies ran while one was open for 4% of the time, Pallas kernels for 0%

profile of v6, /device:TPU:0, one launch (start us, length us, event | category | flops | bytes accessed | tf_op | source)
XLA Modules:
  0.0 156.7 jit_solution(4362366454419793244)
XLA Ops:
  6.5 0.7 all-gather.2.cloned.1.call-update
  7.3 1.7 %collective-permute-start = (bf16[128,1024]{1,0:T(8,128)(2,1)}, bf16[128,1024]{1,0:T(8,128)(2,1)S(1)}, u32[]{:S(2)}, u32[]{:S(2)}) collective-permute-start(bf16[128,1024]{1,0:T(8,128)(2,1)} %param.7), channel_id=1, source_target_pairs={{0,1},{1,2},{2,3},{3,0},{4,5},{5,6},{6,7},{7,4},{8,9},{9,10},{10,1... | collective-permute-start | bytes 786440 | tf_op jit(solution)/shard_map/ppermute | solution.py:130
  9.0 2.9 %collective-permute-start.1 = (bf16[128,1024]{1,0:T(8,128)(2,1)}, bf16[128,1024]{1,0:T(8,128)(2,1)S(1)}, u32[]{:S(2)}, u32[]{:S(2)}) collective-permute-start(bf16[128,1024]{1,0:T(8,128)(2,1)} %param.7), channel_id=1, source_target_pairs={{0,2},{1,3},{2,0},{3,1},{4,6},{5,7},{6,4},{7,5},{8,10},{9,11},{10,... | collective-permute-start | bytes 786440 | tf_op jit(solution)/shard_map/ppermute | solution.py:130
  11.9 1.3 collective-permute-start.2
  13.2 0.7 sort.17
  14.0 2.9 %collective-permute-done = bf16[128,1024]{1,0:T(8,128)(2,1)S(1)} collective-permute-done((bf16[128,1024]{1,0:T(8,128)(2,1)}, bf16[128,1024]{1,0:T(8,128)(2,1)S(1)}, u32[]{:S(2)}, u32[]{:S(2)}) %collective-permute-start) | collective-permute-done | bytes 262176 | tf_op jit(solution)/shard_map/ppermute | solution.py:130
  16.9 6.8 %collective-permute-done.1 = bf16[128,1024]{1,0:T(8,128)(2,1)S(1)} collective-permute-done((bf16[128,1024]{1,0:T(8,128)(2,1)}, bf16[128,1024]{1,0:T(8,128)(2,1)S(1)}, u32[]{:S(2)}, u32[]{:S(2)}) %collective-permute-start.1) | collective-permute-done | bytes 262176 | tf_op jit(solution)/shard_map/ppermute | solution.py:130
  23.7 1.1 pad_maximum_fusion.1
  24.8 0.6 gather_fusion
  25.4 0.2 select_bitcast_fusion
  25.6 0.7 copy.8
  26.5 1.9 %collective-permute-done.3 = bf16[128,2048]{0,1:T(8,128)(2,1)S(1)} collective-permute-done((bf16[128,2048]{0,1:T(8,128)(2,1)S(1)}, bf16[128,2048]{0,1:T(8,128)(2,1)S(1)}, u32[]{:S(2)}, u32[]{:S(2)}) %collective-permute-start.3) | collective-permute-done | bytes 524320 | tf_op jit(solution)/shard_map/ppermute | solution.py:123
  28.4 73.8 %all-gather.2.cloned.1.call-done = bf16[2048,3,1024]{2,0,1:T(8,128)(2,1)} async-done(((bf16[128,3,1024]{2,0,1:T(8,128)(2,1)}), bf16[2048,3,1024]{2,0,1:T(8,128)(2,1)}) %all-gather.2.cloned.1.call-update) | async-done | bytes 12582928 | tf_op jit(solution)/shard_map/all_gather | solution.py:144
  102.2 3.5 %fusion.4 = f32[1,256,1024]{2,1,0:T(8,128)S(1)} fusion(bf16[2048,3,1024]{2,0,1:T(8,128)(2,1)} %all-gather.2.cloned.1.call-done, bf16[128,2048]{0,1:T(8,128)(2,1)S(1)} %collective-permute-done.3, bf16[128,2048]{0,1:T(8,128)(2,1)S(1)} %bitcast.45), kind=kOutput, calls=%fused_computation.10 | convolution fusion | flops 1075838976 | bytes 6291456 | tf_op jit(solution)/shard_map/dot_general | solution.py:151
  105.6 3.5 %fusion.5 = f32[1,256,1024]{2,1,0:T(8,128)S(1)} fusion(bf16[2048,3,1024]{2,0,1:T(8,128)(2,1)} %all-gather.2.cloned.1.call-done, bf16[128,2048]{0,1:T(8,128)(2,1)S(1)} %collective-permute-done.3, bf16[128,2048]{0,1:T(8,128)(2,1)S(1)} %bitcast.46), kind=kOutput, calls=%fused_computation.11 | convolution fusion | flops 1075838976 | bytes 6291456 | tf_op jit(solution)/shard_map/dot_general | solution.py:151
  109.1 3.5 %fusion.6 = f32[1,256,1024]{2,1,0:T(8,128)S(1)} fusion(bf16[2048,3,1024]{2,0,1:T(8,128)(2,1)} %all-gather.2.cloned.1.call-done, bf16[128,2048]{0,1:T(8,128)(2,1)S(1)} %collective-permute-done.3, bf16[128,2048]{0,1:T(8,128)(2,1)S(1)} %bitcast.47), kind=kOutput, calls=%fused_computation.12 | convolution fusion | flops 1075838976 | bytes 6291456 | tf_op jit(solution)/shard_map/dot_general | solution.py:151
  112.6 0.4 pad_maximum_fusion
  113.0 0.1 slice.42
  113.1 0.1 collective-permute-start.4
  113.2 0.6 copy-done
  113.9 2.8 %collective-permute-done.4 = f32[3,128,1024]{2,1,0:T(8,128)S(1)} collective-permute-done((f32[3,128,1024]{2,1,0:T(8,128)S(1)}, f32[3,128,1024]{2,1,0:T(8,128)S(1)}, u32[]{:S(2)}, u32[]{:S(2)}) %collective-permute-start.4) | collective-permute-done | bytes 1572896 | tf_op jit(solution)/shard_map/ppermute | solution.py:123
  116.6 0.3 fusion.3
  117.0 2.0 %collective-permute-start.5 = (bf16[3,2,1024]{2,1,0:T(2,128)(2,1)S(1)}, bf16[3,2,1024]{2,1,0:T(2,128)(2,1)S(1)}, u32[]{:S(2)}, u32[]{:S(2)}) collective-permute-start(bf16[3,2,1024]{2,1,0:T(2,128)(2,1)S(1)} %slice.43), channel_id=1, source_target_pairs={{0,4},{4,8},{8,12},{12,16},{16,20},{20,24},{24,28},{28,32},{32,36}... | collective-permute-start | bytes 36872 | tf_op jit(solution)/shard_map/ppermute | solution.py:119
  119.1 1.2 multiply_exponential_fusion
  120.2 0.6 copy.9
  120.9 0.6 copy.10
  121.5 0.6 reshape.48.taps_ref
  122.2 0.2 pad_maximum_fusion.3
  122.4 1.5 reshape.53.x_ref
  123.9 24.2 %shard_map.73 = f32[128,8,128]{2,1,0:T(8,128)} custom-call(f32[3,130,8,128]{3,2,1,0:T(8,128)} %reshape.53.x_ref, f32[3,3,8,128]{3,2,1,0:T(8,128)} %reshape.48.taps_ref, f32[16,8,128]{2,1,0:T(8,128)} %bitcast.50, f32[16,8,128]{2,1,0:T(8,128)} %bitcast.51, f32[8,128]{1,0:T(8,128)} %bitcast.57, f32[7,16,8,128]{3,2,1,0:T(8,128)} %get-tuple-element.10.lift_ref, ...), custom_call_target="tpu_custom_call" | custom-call | tf_op jit(solution)/shard_map/pallas_call | solution.py:176
  148.1 1.1 convert_element_type.11
  149.1 0.8 copy.14
  (22 shorter events, 0.3 us)
Async XLA Ops:
  6.5 95.6 %all-gather.2.cloned.1.call-start = ((), (), s32[]{:S(2)}) async-start(), calls=%async_computation | async-start | bytes 13369344 | tf_op jit(solution)/shard_map/all_gather | solution.py:144
  7.3 9.7 %collective-permute-start = (bf16[128,1024]{1,0:T(8,128)(2,1)}, bf16[128,1024]{1,0:T(8,128)(2,1)S(1)}, u32[]{:S(2)}, u32[]{:S(2)}) collective-permute-start(bf16[128,1024]{1,0:T(8,128)(2,1)} %param.7), channel_id=1, source_target_pairs={{0,1},{1,2},{2,3},{3,0},{4,5},{5,6},{6,7},{7,4},{8,9},{9,10},{10,1... | collective-permute-start | bytes 786440 | tf_op jit(solution)/shard_map/ppermute | solution.py:130
  9.0 14.7 %collective-permute-start.1 = (bf16[128,1024]{1,0:T(8,128)(2,1)}, bf16[128,1024]{1,0:T(8,128)(2,1)S(1)}, u32[]{:S(2)}, u32[]{:S(2)}) collective-permute-start(bf16[128,1024]{1,0:T(8,128)(2,1)} %param.7), channel_id=1, source_target_pairs={{0,2},{1,3},{2,0},{3,1},{4,6},{5,7},{6,4},{7,5},{8,10},{9,11},{10,... | collective-permute-start | bytes 786440 | tf_op jit(solution)/shard_map/ppermute | solution.py:130
  11.9 11.9 %collective-permute-start.2 = (bf16[128,1024]{1,0:T(8,128)(2,1)}, bf16[128,1024]{1,0:T(8,128)(2,1)S(1)}, u32[]{:S(2)}, u32[]{:S(2)}) collective-permute-start(bf16[128,1024]{1,0:T(8,128)(2,1)} %param.7), channel_id=1, source_target_pairs={{0,3},{1,0},{2,1},{3,2},{4,7},{5,4},{6,5},{7,6},{8,11},{9,8},{10,9... | collective-permute-start | bytes 786440 | tf_op jit(solution)/shard_map/ppermute | solution.py:130
  26.4 2.0 %collective-permute-start.3 = (bf16[128,2048]{0,1:T(8,128)(2,1)S(1)}, bf16[128,2048]{0,1:T(8,128)(2,1)S(1)}, u32[]{:S(2)}, u32[]{:S(2)}) collective-permute-start(bf16[128,2048]{0,1:T(8,128)(2,1)S(1)} %bitcast.48), channel_id=1, source_target_pairs={{0,4},{4,0},{1,5},{5,1},{2,6},{6,2},{3,7},{7,3},{8,12},{12,8},{9,1... | collective-permute-start | bytes 1572872 | tf_op jit(solution)/shard_map/ppermute | solution.py:123
  113.0 0.8 copy-start
  113.0 6.1 %copy-start.3 = (f32[7]{0:T(128)S(1)}, f32[7]{0:T(128)}, u32[]{:S(2)}) copy-start(f32[7]{0:T(128)} %constant.47) | copy-start | bytes 88
  113.0 6.1 %copy-start.4 = (f32[7]{0:T(128)S(1)}, f32[7]{0:T(128)}, u32[]{:S(2)}) copy-start(f32[7]{0:T(128)} %constant.48) | copy-start | bytes 88
  113.1 7.8 %copy-start.1 = (f32[16,1024]{1,0:T(8,128)S(1)}, f32[16,1024]{1,0:T(8,128)}, u32[]{:S(2)}) copy-start(f32[16,1024]{1,0:T(8,128)} %param.11) | copy-start | bytes 196612
  113.1 8.4 %copy-start.2 = (f32[3,3,1024]{2,1,0:T(4,128)S(1)}, f32[3,3,1024]{2,1,0:T(4,128)}, u32[]{:S(2)}) copy-start(f32[3,3,1024]{2,1,0:T(4,128)} %param.9) | copy-start | bytes 110596
  113.1 3.5 %collective-permute-start.4 = (f32[3,128,1024]{2,1,0:T(8,128)S(1)}, f32[3,128,1024]{2,1,0:T(8,128)S(1)}, u32[]{:S(2)}, u32[]{:S(2)}) collective-permute-start(f32[3,128,1024]{2,1,0:T(8,128)S(1)} %slice.42), channel_id=1, source_target_pairs={{0,4},{4,0},{1,5},{5,1},{2,6},{6,2},{3,7},{7,3},{8,12},{12,8},{9,1... | collective-permute-start | bytes 4718600 | tf_op jit(solution)/shard_map/ppermute | solution.py:123
  117.0 5.2 %collective-permute-start.5 = (bf16[3,2,1024]{2,1,0:T(2,128)(2,1)S(1)}, bf16[3,2,1024]{2,1,0:T(2,128)(2,1)S(1)}, u32[]{:S(2)}, u32[]{:S(2)}) collective-permute-start(bf16[3,2,1024]{2,1,0:T(2,128)(2,1)S(1)} %slice.43), channel_id=1, source_target_pairs={{0,4},{4,8},{8,12},{12,16},{16,20},{20,24},{24,28},{28,32},{32,36}... | collective-permute-start | bytes 36872 | tf_op jit(solution)/shard_map/ppermute | solution.py:119
Sparse Core Ops, SparseCore 0:
  9.5 92.6 all-gather.1

commit v7 on v6

--- a/solution.py
+++ b/solution.py
@@ -147,21 +147,10 @@
     mine = jnp.where(core == 0, split[:, :, 0], split[:, :, 1]).reshape(rows, -1)
     theirs = jnp.where(core == 0, split[:, :, 1], split[:, :, 0]).reshape(rows, -1)
     both = jnp.concatenate([mine, swapped(theirs, "core")], axis=0)
-    partial = jnp.stack(
-        [jnp.dot(both, piece[:, g, :], preferred_element_type=jnp.float32) for g in range(3)],
-        axis=0,
-    )
-    sums = partial[:, :rows] + swapped(partial[:, rows:], "core")
-    projected = sums.astype(jnp.bfloat16)
-    edge_out = shifted(projected[:, rows - 2 :, :], ctx, 1)
-    extended = jnp.concatenate([edge_out, projected], axis=1)
-    values = lax.optimization_barrier(extended).astype(jnp.float32)
-    x = values.reshape(3, rows + 2, subl, LANES)
     taps = conv_taps.reshape(3, 3, subl, LANES)
     decay = jnp.exp(-decay_rate).reshape(poles, subl, LANES)
     resid = residue.reshape(poles, subl, LANES)
     direct = skip.reshape(subl, LANES)
-
     peers = lax.axis_size("cx") * lax.axis_size("core")
     digits = scan_digits(peers)
     strides, width = [], 1
@@ -172,6 +161,19 @@
     widths = jnp.asarray(strides, jnp.float32)[:, None, None]
     lift = jnp.exp(-decay_rate[None] * (rows * (widths - 1.0))).reshape(copies, poles, subl, LANES)
     keep = jnp.exp(-decay_rate[None] * (rows * widths)).reshape(copies, poles, subl, LANES)
+    (taps, decay, resid, direct, lift, keep), both = lax.optimization_barrier(
+        ((taps, decay, resid, direct, lift, keep), both)
+    )
+    partial = jnp.stack(
+        [jnp.dot(both, piece[:, g, :], preferred_element_type=jnp.float32) for g in range(3)],
+        axis=0,
+    )
+    sums = partial[:, :rows] + swapped(partial[:, rows:], "core")
+    projected = sums.astype(jnp.bfloat16)
+    edge_out = shifted(projected[:, rows - 2 :, :], ctx, 1)
+    extended = jnp.concatenate([edge_out, projected], axis=1)
+    values = lax.optimization_barrier(extended).astype(jnp.float32)
+    x = values.reshape(3, rows + 2, subl, LANES)
     state_shape = (poles, subl, LANES)
     out = pl.pallas_call(
         functools.partial(block_kernel, peers, digits),

time: 157 us -> 157 us (level)
  Pallas kernels: 24.2 us -> 25.8 us
    pallas_call x1, Pallas kernels: 24.2 us -> 25.8 us  [per_device(): pl.pallas_call(functools.partial(block_kernel, peers, digits), out_shape=...]
  transfers between devices with their start and end apart: 7 -> 7, of which waited for: 5 -> 6; matrix products, arithmetic and copies ran while one was open for 4% -> 4% of each run, Pallas kernels for 0% -> 0%
where the time goes in v7:
time: 157 us; the launch traced here: 156 us
  waiting for transfers between devices  87.6 us (56%)
  Pallas kernels  25.8 us (16%)
  between operations  13.6 us (9%)
  matrix products  10.4 us (7%)
  starting transfers between devices  7.59 us (5%)
  local copies, waits for them, and re-layouts  5.59 us (4%)
  other arithmetic  5.43 us (3%)
    all_gather x1, waiting for transfers between devices, per_device(): piece = lax.all_gather(in_weight, 'cx', axis=0, tiled=True)  72.4 us
    pallas_call x1, Pallas kernels, per_device(): pl.pallas_call(functools.partial(block_kernel, peers, digits), out_shape=...  25.8 us
    dot_general x3, matrix products, per_device(): jnp.dot(both, piece[:, g, :], preferred_element_type=jnp.float32)  10.4 us
    ppermute x3, waiting for transfers between devices, gathered_tp(): lax.ppermute(tokens, 'tp', [(i, (i + by) % peers) for i in range(peers)])  10.3 us
    ppermute x3, starting transfers between devices, gathered_tp(): lax.ppermute(tokens, 'tp', [(i, (i + by) % peers) for i in range(peers)])  5.37 us
    ppermute x2, waiting for transfers between devices, swapped(): return lax.ppermute(array, axis, [(0, 1), (1, 0)])  3.4 us
  transfers between devices with their start and end apart: 7, of which 6 were waited for; matrix products, arithmetic and copies ran while one was open for 4% of the time, Pallas kernels for 0%

profile of v7, /device:TPU:0, one launch (start us, length us, event | category | flops | bytes accessed | tf_op | source)
XLA Modules:
  0.0 156.0 jit_solution(15276009897520016085)
XLA Ops:
  6.5 0.7 all-gather.2.cloned.1.call-update
  7.3 1.7 %collective-permute-start = (bf16[128,1024]{1,0:T(8,128)(2,1)}, bf16[128,1024]{1,0:T(8,128)(2,1)S(1)}, u32[]{:S(2)}, u32[]{:S(2)}) collective-permute-start(bf16[128,1024]{1,0:T(8,128)(2,1)} %param.7), channel_id=1, source_target_pairs={{0,1},{1,2},{2,3},{3,0},{4,5},{5,6},{6,7},{7,4},{8,9},{9,10},{10,1... | collective-permute-start | bytes 786440 | tf_op jit(solution)/shard_map/ppermute | solution.py:130
  9.0 1.6 %collective-permute-start.2 = (bf16[128,1024]{1,0:T(8,128)(2,1)}, bf16[128,1024]{1,0:T(8,128)(2,1)S(1)}, u32[]{:S(2)}, u32[]{:S(2)}) collective-permute-start(bf16[128,1024]{1,0:T(8,128)(2,1)} %param.7), channel_id=1, source_target_pairs={{0,3},{1,0},{2,1},{3,2},{4,7},{5,4},{6,5},{7,6},{8,11},{9,8},{10,9... | collective-permute-start | bytes 786440 | tf_op jit(solution)/shard_map/ppermute | solution.py:130
  10.6 2.1 %collective-permute-start.1 = (bf16[128,1024]{1,0:T(8,128)(2,1)}, bf16[128,1024]{1,0:T(8,128)(2,1)S(1)}, u32[]{:S(2)}, u32[]{:S(2)}) collective-permute-start(bf16[128,1024]{1,0:T(8,128)(2,1)} %param.7), channel_id=1, source_target_pairs={{0,2},{1,3},{2,0},{3,1},{4,6},{5,7},{6,4},{7,5},{8,10},{9,11},{10,... | collective-permute-start | bytes 786440 | tf_op jit(solution)/shard_map/ppermute | solution.py:130
  12.6 0.7 sort.17
  13.4 3.5 %collective-permute-done = bf16[128,1024]{1,0:T(8,128)(2,1)S(1)} collective-permute-done((bf16[128,1024]{1,0:T(8,128)(2,1)}, bf16[128,1024]{1,0:T(8,128)(2,1)S(1)}, u32[]{:S(2)}, u32[]{:S(2)}) %collective-permute-start) | collective-permute-done | bytes 262176 | tf_op jit(solution)/shard_map/ppermute | solution.py:130
  16.9 5.1 %collective-permute-done.2 = bf16[128,1024]{1,0:T(8,128)(2,1)S(1)} collective-permute-done((bf16[128,1024]{1,0:T(8,128)(2,1)}, bf16[128,1024]{1,0:T(8,128)(2,1)S(1)}, u32[]{:S(2)}, u32[]{:S(2)}) %collective-permute-start.2) | collective-permute-done | bytes 262176 | tf_op jit(solution)/shard_map/ppermute | solution.py:130
  22.0 1.7 %collective-permute-done.1 = bf16[128,1024]{1,0:T(8,128)(2,1)S(1)} collective-permute-done((bf16[128,1024]{1,0:T(8,128)(2,1)}, bf16[128,1024]{1,0:T(8,128)(2,1)S(1)}, u32[]{:S(2)}, u32[]{:S(2)}) %collective-permute-start.1) | collective-permute-done | bytes 262176 | tf_op jit(solution)/shard_map/ppermute | solution.py:130
  23.7 1.1 pad_maximum_fusion.1
  24.8 0.6 gather_fusion
  25.5 0.2 select_bitcast_fusion
  25.7 0.7 copy.8
  26.5 0.6 reshape.46.taps_ref
  27.2 0.6 copy.10
  27.8 0.6 copy.9
  28.5 1.1 multiply_exponential_fusion
  29.6 0.1 pad_maximum_fusion.2
  29.8 72.4 %all-gather.2.cloned.1.call-done = bf16[2048,3,1024]{2,0,1:T(8,128)(2,1)} async-done(((bf16[128,3,1024]{2,0,1:T(8,128)(2,1)}), bf16[2048,3,1024]{2,0,1:T(8,128)(2,1)}) %all-gather.2.cloned.1.call-update) | async-done | bytes 12582928 | tf_op jit(solution)/shard_map/all_gather | solution.py:144
  102.2 3.5 %fusion.6 = f32[1,256,1024]{2,1,0:T(8,128)S(1)} fusion(bf16[256,2048]{0,1:T(8,128)(2,1)S(1)} %pad_maximum_fusion.2, bf16[2048,3,1024]{2,0,1:T(8,128)(2,1)} %all-gather.2.cloned.1.call-done), kind=kOutput, calls=%fused_computation.12 | convolution fusion | flops 1073741824 | bytes 6291456 | tf_op jit(solution)/shard_map/dot_general | solution.py:168
  105.6 3.5 %fusion.5 = f32[1,256,1024]{2,1,0:T(8,128)S(1)} fusion(bf16[256,2048]{0,1:T(8,128)(2,1)S(1)} %pad_maximum_fusion.2, bf16[2048,3,1024]{2,0,1:T(8,128)(2,1)} %all-gather.2.cloned.1.call-done), kind=kOutput, calls=%fused_computation.11 | convolution fusion | flops 1073741824 | bytes 6291456 | tf_op jit(solution)/shard_map/dot_general | solution.py:168
  109.1 3.5 %fusion.4 = f32[1,256,1024]{2,1,0:T(8,128)S(1)} fusion(bf16[256,2048]{0,1:T(8,128)(2,1)S(1)} %pad_maximum_fusion.2, bf16[2048,3,1024]{2,0,1:T(8,128)(2,1)} %all-gather.2.cloned.1.call-done), kind=kOutput, calls=%fused_computation.10 | convolution fusion | flops 1073741824 | bytes 6291456 | tf_op jit(solution)/shard_map/dot_general | solution.py:168
  112.6 0.4 pad_maximum_fusion
  113.0 0.1 slice.42
  113.2 3.4 %collective-permute-done.4 = f32[3,128,1024]{2,1,0:T(8,128)S(1)} collective-permute-done((f32[3,128,1024]{2,1,0:T(8,128)S(1)}, f32[3,128,1024]{2,1,0:T(8,128)S(1)}, u32[]{:S(2)}, u32[]{:S(2)}) %collective-permute-start.4) | collective-permute-done | bytes 1572896 | tf_op jit(solution)/shard_map/ppermute | solution.py:123
  116.6 0.4 fusion.3
  117.0 2.0 %collective-permute-start.5 = (bf16[3,2,1024]{2,1,0:T(2,128)(2,1)S(1)}, bf16[3,2,1024]{2,1,0:T(2,128)(2,1)S(1)}, u32[]{:S(2)}, u32[]{:S(2)}) collective-permute-start(bf16[3,2,1024]{2,1,0:T(2,128)(2,1)S(1)} %slice.43), channel_id=1, source_target_pairs={{0,4},{4,8},{8,12},{12,16},{16,20},{20,24},{24,28},{28,32},{32,36}... | collective-permute-start | bytes 36872 | tf_op jit(solution)/shard_map/ppermute | solution.py:119
  119.0 0.8 collective-permute-done.5
  119.8 0.2 pad_maximum_fusion.3
  120.1 1.5 reshape.53.x_ref
  121.5 25.8 %shard_map.73 = f32[128,8,128]{2,1,0:T(8,128)} custom-call(f32[3,130,8,128]{3,2,1,0:T(8,128)} %reshape.53.x_ref, f32[3,3,8,128]{3,2,1,0:T(8,128)} %reshape.46.taps_ref, f32[16,8,128]{2,1,0:T(8,128)} %bitcast.51, f32[16,8,128]{2,1,0:T(8,128)} %bitcast.50, f32[8,128]{1,0:T(8,128)} %bitcast.58, f32[7,16,8,128]{3,2,1,0:T(8,128)} %get-tuple-element.19.lift_ref, ...), custom_call_target="tpu_custom_call" | custom-call | tf_op jit(solution)/shard_map/pallas_call | solution.py:178
  147.4 1.1 convert_element_type.11
  148.4 0.8 copy.14
  (23 shorter events, 0.4 us)
Async XLA Ops:
  6.5 95.6 %all-gather.2.cloned.1.call-start = ((), (), s32[]{:S(2)}) async-start(), calls=%async_computation | async-start | bytes 13369344 | tf_op jit(solution)/shard_map/all_gather | solution.py:144
  7.3 9.7 %collective-permute-start = (bf16[128,1024]{1,0:T(8,128)(2,1)}, bf16[128,1024]{1,0:T(8,128)(2,1)S(1)}, u32[]{:S(2)}, u32[]{:S(2)}) collective-permute-start(bf16[128,1024]{1,0:T(8,128)(2,1)} %param.7), channel_id=1, source_target_pairs={{0,1},{1,2},{2,3},{3,0},{4,5},{5,6},{6,7},{7,4},{8,9},{9,10},{10,1... | collective-permute-start | bytes 786440 | tf_op jit(solution)/shard_map/ppermute | solution.py:130
  9.0 13.1 %collective-permute-start.2 = (bf16[128,1024]{1,0:T(8,128)(2,1)}, bf16[128,1024]{1,0:T(8,128)(2,1)S(1)}, u32[]{:S(2)}, u32[]{:S(2)}) collective-permute-start(bf16[128,1024]{1,0:T(8,128)(2,1)} %param.7), channel_id=1, source_target_pairs={{0,3},{1,0},{2,1},{3,2},{4,7},{5,4},{6,5},{7,6},{8,11},{9,8},{10,9... | collective-permute-start | bytes 786440 | tf_op jit(solution)/shard_map/ppermute | solution.py:130
  10.6 13.2 %collective-permute-start.1 = (bf16[128,1024]{1,0:T(8,128)(2,1)}, bf16[128,1024]{1,0:T(8,128)(2,1)S(1)}, u32[]{:S(2)}, u32[]{:S(2)}) collective-permute-start(bf16[128,1024]{1,0:T(8,128)(2,1)} %param.7), channel_id=1, source_target_pairs={{0,2},{1,3},{2,0},{3,1},{4,6},{5,7},{6,4},{7,5},{8,10},{9,11},{10,... | collective-permute-start | bytes 786440 | tf_op jit(solution)/shard_map/ppermute | solution.py:130
  25.4 1.1 copy-start.2
  25.5 1.7 %copy-start.1 = (f32[16,1024]{1,0:T(8,128)S(1)}, f32[16,1024]{1,0:T(8,128)}, u32[]{:S(2)}) copy-start(f32[16,1024]{1,0:T(8,128)} %param.11) | copy-start | bytes 196612
  25.5 2.3 %copy-start = (f32[16,1024]{1,0:T(8,128)S(1)}, f32[16,1024]{1,0:T(8,128)}, u32[]{:S(2)}) copy-start(f32[16,1024]{1,0:T(8,128)} %param.10) | copy-start | bytes 196612
  25.5 3.0 %copy-start.3 = (f32[7]{0:T(128)S(1)}, f32[7]{0:T(128)}, u32[]{:S(2)}) copy-start(f32[7]{0:T(128)} %constant.48) | copy-start | bytes 88
  25.5 3.0 %copy-start.4 = (f32[7]{0:T(128)S(1)}, f32[7]{0:T(128)}, u32[]{:S(2)}) copy-start(f32[7]{0:T(128)} %constant.47) | copy-start | bytes 88
  26.4 3.2 %collective-permute-start.3 = (bf16[128,2048]{0,1:T(8,128)(2,1)S(1)}, bf16[128,2048]{0,1:T(8,128)(2,1)S(1)}, u32[]{:S(2)}, u32[]{:S(2)}) collective-permute-start(bf16[128,2048]{0,1:T(8,128)(2,1)S(1)} %bitcast.49), channel_id=1, source_target_pairs={{0,4},{4,0},{1,5},{5,1},{2,6},{6,2},{3,7},{7,3},{8,12},{12,8},{9,1... | collective-permute-start | bytes 1572872 | tf_op jit(solution)/shard_map/ppermute | solution.py:123
  113.1 3.5 %collective-permute-start.4 = (f32[3,128,1024]{2,1,0:T(8,128)S(1)}, f32[3,128,1024]{2,1,0:T(8,128)S(1)}, u32[]{:S(2)}, u32[]{:S(2)}) collective-permute-start(f32[3,128,1024]{2,1,0:T(8,128)S(1)} %slice.42), channel_id=1, source_target_pairs={{0,4},{4,0},{1,5},{5,1},{2,6},{6,2},{3,7},{7,3},{8,12},{12,8},{9,1... | collective-permute-start | bytes 4718600 | tf_op jit(solution)/shard_map/ppermute | solution.py:123
  117.0 2.9 %collective-permute-start.5 = (bf16[3,2,1024]{2,1,0:T(2,128)(2,1)S(1)}, bf16[3,2,1024]{2,1,0:T(2,128)(2,1)S(1)}, u32[]{:S(2)}, u32[]{:S(2)}) collective-permute-start(bf16[3,2,1024]{2,1,0:T(2,128)(2,1)S(1)} %slice.43), channel_id=1, source_target_pairs={{0,4},{4,8},{8,12},{12,16},{16,20},{20,24},{24,28},{28,32},{32,36}... | collective-permute-start | bytes 36872 | tf_op jit(solution)/shard_map/ppermute | solution.py:119
Sparse Core Ops, SparseCore 0:
  9.5 92.6 all-gather.1

commit v8 on v7

--- a/solution.py
+++ b/solution.py
@@ -101,7 +101,7 @@
 def scan_digits(peers):
     digits = []
     while peers > 1:
-        digit = 4 if peers % 4 == 0 and peers != 8 else 2
+        digit = 8 if peers % 8 == 0 and not digits else (4 if peers % 4 == 0 else 2)
         digits.append(digit)
         peers //= digit
     return digits or [2]

time: 157 us -> 159 us (1.013)
  Pallas kernels: 25.8 us -> 27.8 us
    pallas_call x1, Pallas kernels: 25.8 us -> 27.8 us  [per_device(): pl.pallas_call(functools.partial(block_kernel, peers, digits), out_shape=...]
where the time goes in v8:
time: 159 us; the launch traced here: 158 us
  waiting for transfers between devices  87.4 us (55%)
  Pallas kernels  27.8 us (17%)
  between operations  13.6 us (9%)
  matrix products  10.4 us (7%)
  starting transfers between devices  7.59 us (5%)
  other arithmetic  5.63 us (4%)
  local copies, waits for them, and re-layouts  5.59 us (4%)
    all_gather x1, waiting for transfers between devices, per_device(): piece = lax.all_gather(in_weight, 'cx', axis=0, tiled=True)  72.2 us
    pallas_call x1, Pallas kernels, per_device(): pl.pallas_call(functools.partial(block_kernel, peers, digits), out_shape=...  27.8 us
    dot_general x3, matrix products, per_device(): jnp.dot(both, piece[:, g, :], preferred_element_type=jnp.float32)  10.4 us
    ppermute x3, waiting for transfers between devices, gathered_tp(): lax.ppermute(tokens, 'tp', [(i, (i + by) % peers) for i in range(peers)])  10.3 us
    ppermute x3, starting transfers between devices, gathered_tp(): lax.ppermute(tokens, 'tp', [(i, (i + by) % peers) for i in range(peers)])  5.37 us
    ppermute x2, waiting for transfers between devices, swapped(): return lax.ppermute(array, axis, [(0, 1), (1, 0)])  3.4 us
  transfers between devices with their start and end apart: 7, of which 6 were waited for; matrix products, arithmetic and copies ran while one was open for 4% of the time, Pallas kernels for 0%

profile of v8, /device:TPU:0, one launch (start us, length us, event | category | flops | bytes accessed | tf_op | source)
XLA Modules:
  0.0 158.0 jit_solution(7213279647446750266)
XLA Ops:
  6.5 0.7 all-gather.2.cloned.1.call-update
  7.3 1.7 %collective-permute-start = (bf16[128,1024]{1,0:T(8,128)(2,1)}, bf16[128,1024]{1,0:T(8,128)(2,1)S(1)}, u32[]{:S(2)}, u32[]{:S(2)}) collective-permute-start(bf16[128,1024]{1,0:T(8,128)(2,1)} %param.7), channel_id=1, source_target_pairs={{0,1},{1,2},{2,3},{3,0},{4,5},{5,6},{6,7},{7,4},{8,9},{9,10},{10,1... | collective-permute-start | bytes 786440 | tf_op jit(solution)/shard_map/ppermute | solution.py:130
  9.0 1.6 collective-permute-start.2
  10.6 2.1 %collective-permute-start.1 = (bf16[128,1024]{1,0:T(8,128)(2,1)}, bf16[128,1024]{1,0:T(8,128)(2,1)S(1)}, u32[]{:S(2)}, u32[]{:S(2)}) collective-permute-start(bf16[128,1024]{1,0:T(8,128)(2,1)} %param.7), channel_id=1, source_target_pairs={{0,2},{1,3},{2,0},{3,1},{4,6},{5,7},{6,4},{7,5},{8,10},{9,11},{10,... | collective-permute-start | bytes 786440 | tf_op jit(solution)/shard_map/ppermute | solution.py:130
  12.6 0.7 sort.17
  13.4 3.5 %collective-permute-done = bf16[128,1024]{1,0:T(8,128)(2,1)S(1)} collective-permute-done((bf16[128,1024]{1,0:T(8,128)(2,1)}, bf16[128,1024]{1,0:T(8,128)(2,1)S(1)}, u32[]{:S(2)}, u32[]{:S(2)}) %collective-permute-start) | collective-permute-done | bytes 262176 | tf_op jit(solution)/shard_map/ppermute | solution.py:130
  16.9 5.1 %collective-permute-done.2 = bf16[128,1024]{1,0:T(8,128)(2,1)S(1)} collective-permute-done((bf16[128,1024]{1,0:T(8,128)(2,1)}, bf16[128,1024]{1,0:T(8,128)(2,1)S(1)}, u32[]{:S(2)}, u32[]{:S(2)}) %collective-permute-start.2) | collective-permute-done | bytes 262176 | tf_op jit(solution)/shard_map/ppermute | solution.py:130
  22.0 1.7 %collective-permute-done.1 = bf16[128,1024]{1,0:T(8,128)(2,1)S(1)} collective-permute-done((bf16[128,1024]{1,0:T(8,128)(2,1)}, bf16[128,1024]{1,0:T(8,128)(2,1)S(1)}, u32[]{:S(2)}, u32[]{:S(2)}) %collective-permute-start.1) | collective-permute-done | bytes 262176 | tf_op jit(solution)/shard_map/ppermute | solution.py:130
  23.7 1.1 pad_maximum_fusion.1
  24.8 0.6 gather_fusion
  25.5 0.2 select_bitcast_fusion
  25.7 0.7 copy.8
  26.5 0.6 reshape.46.taps_ref
  27.2 0.6 copy.10
  27.8 0.6 copy.9
  28.5 1.3 multiply_exponential_fusion
  29.8 0.1 pad_maximum_fusion.2
  29.9 72.2 %all-gather.2.cloned.1.call-done = bf16[2048,3,1024]{2,0,1:T(8,128)(2,1)} async-done(((bf16[128,3,1024]{2,0,1:T(8,128)(2,1)}), bf16[2048,3,1024]{2,0,1:T(8,128)(2,1)}) %all-gather.2.cloned.1.call-update) | async-done | bytes 12582928 | tf_op jit(solution)/shard_map/all_gather | solution.py:144
  102.2 3.5 %fusion.6 = f32[1,256,1024]{2,1,0:T(8,128)S(1)} fusion(bf16[256,2048]{0,1:T(8,128)(2,1)S(1)} %pad_maximum_fusion.2, bf16[2048,3,1024]{2,0,1:T(8,128)(2,1)} %all-gather.2.cloned.1.call-done), kind=kOutput, calls=%fused_computation.12 | convolution fusion | flops 1073741824 | bytes 6291456 | tf_op jit(solution)/shard_map/dot_general | solution.py:168
  105.6 3.5 %fusion.5 = f32[1,256,1024]{2,1,0:T(8,128)S(1)} fusion(bf16[256,2048]{0,1:T(8,128)(2,1)S(1)} %pad_maximum_fusion.2, bf16[2048,3,1024]{2,0,1:T(8,128)(2,1)} %all-gather.2.cloned.1.call-done), kind=kOutput, calls=%fused_computation.11 | convolution fusion | flops 1073741824 | bytes 6291456 | tf_op jit(solution)/shard_map/dot_general | solution.py:168
  109.1 3.5 %fusion.4 = f32[1,256,1024]{2,1,0:T(8,128)S(1)} fusion(bf16[256,2048]{0,1:T(8,128)(2,1)S(1)} %pad_maximum_fusion.2, bf16[2048,3,1024]{2,0,1:T(8,128)(2,1)} %all-gather.2.cloned.1.call-done), kind=kOutput, calls=%fused_computation.10 | convolution fusion | flops 1073741824 | bytes 6291456 | tf_op jit(solution)/shard_map/dot_general | solution.py:168
  112.6 0.4 pad_maximum_fusion
  113.0 0.1 slice.42
  113.2 3.4 %collective-permute-done.4 = f32[3,128,1024]{2,1,0:T(8,128)S(1)} collective-permute-done((f32[3,128,1024]{2,1,0:T(8,128)S(1)}, f32[3,128,1024]{2,1,0:T(8,128)S(1)}, u32[]{:S(2)}, u32[]{:S(2)}) %collective-permute-start.4) | collective-permute-done | bytes 1572896 | tf_op jit(solution)/shard_map/ppermute | solution.py:123
  116.6 0.4 fusion.3
  117.0 2.0 %collective-permute-start.5 = (bf16[3,2,1024]{2,1,0:T(2,128)(2,1)S(1)}, bf16[3,2,1024]{2,1,0:T(2,128)(2,1)S(1)}, u32[]{:S(2)}, u32[]{:S(2)}) collective-permute-start(bf16[3,2,1024]{2,1,0:T(2,128)(2,1)S(1)} %slice.43), channel_id=1, source_target_pairs={{0,4},{4,8},{8,12},{12,16},{16,20},{20,24},{24,28},{28,32},{32,36}... | collective-permute-start | bytes 36872 | tf_op jit(solution)/shard_map/ppermute | solution.py:119
  119.0 0.8 collective-permute-done.5
  119.8 0.2 pad_maximum_fusion.3
  120.1 1.5 reshape.53.x_ref
  121.5 27.8 %shard_map.73 = f32[128,8,128]{2,1,0:T(8,128)} custom-call(f32[3,130,8,128]{3,2,1,0:T(8,128)} %reshape.53.x_ref, f32[3,3,8,128]{3,2,1,0:T(8,128)} %reshape.46.taps_ref, f32[16,8,128]{2,1,0:T(8,128)} %bitcast.51, f32[16,8,128]{2,1,0:T(8,128)} %bitcast.50, f32[8,128]{1,0:T(8,128)} %bitcast.58, f32[10,16,8,128]{3,2,1,0:T(8,128)} %get-tuple-element.19.lift_ref, ...), custom_call_target="tpu_custom_call" | custom-call | tf_op jit(solution)/shard_map/pallas_call | solution.py:178
  149.3 1.1 convert_element_type.11
  150.4 0.8 copy.14
  (23 shorter events, 0.4 us)
Async XLA Ops:
  6.5 95.6 %all-gather.2.cloned.1.call-start = ((), (), s32[]{:S(2)}) async-start(), calls=%async_computation | async-start | bytes 13369344 | tf_op jit(solution)/shard_map/all_gather | solution.py:144
  7.3 9.7 %collective-permute-start = (bf16[128,1024]{1,0:T(8,128)(2,1)}, bf16[128,1024]{1,0:T(8,128)(2,1)S(1)}, u32[]{:S(2)}, u32[]{:S(2)}) collective-permute-start(bf16[128,1024]{1,0:T(8,128)(2,1)} %param.7), channel_id=1, source_target_pairs={{0,1},{1,2},{2,3},{3,0},{4,5},{5,6},{6,7},{7,4},{8,9},{9,10},{10,1... | collective-permute-start | bytes 786440 | tf_op jit(solution)/shard_map/ppermute | solution.py:130
  9.0 13.1 %collective-permute-start.2 = (bf16[128,1024]{1,0:T(8,128)(2,1)}, bf16[128,1024]{1,0:T(8,128)(2,1)S(1)}, u32[]{:S(2)}, u32[]{:S(2)}) collective-permute-start(bf16[128,1024]{1,0:T(8,128)(2,1)} %param.7), channel_id=1, source_target_pairs={{0,3},{1,0},{2,1},{3,2},{4,7},{5,4},{6,5},{7,6},{8,11},{9,8},{10,9... | collective-permute-start | bytes 786440 | tf_op jit(solution)/shard_map/ppermute | solution.py:130
  10.6 13.2 %collective-permute-start.1 = (bf16[128,1024]{1,0:T(8,128)(2,1)}, bf16[128,1024]{1,0:T(8,128)(2,1)S(1)}, u32[]{:S(2)}, u32[]{:S(2)}) collective-permute-start(bf16[128,1024]{1,0:T(8,128)(2,1)} %param.7), channel_id=1, source_target_pairs={{0,2},{1,3},{2,0},{3,1},{4,6},{5,7},{6,4},{7,5},{8,10},{9,11},{10,... | collective-permute-start | bytes 786440 | tf_op jit(solution)/shard_map/ppermute | solution.py:130
  25.4 1.1 copy-start.2
  25.5 1.7 %copy-start.1 = (f32[16,1024]{1,0:T(8,128)S(1)}, f32[16,1024]{1,0:T(8,128)}, u32[]{:S(2)}) copy-start(f32[16,1024]{1,0:T(8,128)} %param.11) | copy-start | bytes 196612
  25.5 2.3 %copy-start = (f32[16,1024]{1,0:T(8,128)S(1)}, f32[16,1024]{1,0:T(8,128)}, u32[]{:S(2)}) copy-start(f32[16,1024]{1,0:T(8,128)} %param.10) | copy-start | bytes 196612
  25.5 3.0 %copy-start.3 = (f32[10]{0:T(128)S(1)}, f32[10]{0:T(128)}, u32[]{:S(2)}) copy-start(f32[10]{0:T(128)} %constant.48) | copy-start | bytes 124
  25.5 3.0 %copy-start.4 = (f32[10]{0:T(128)S(1)}, f32[10]{0:T(128)}, u32[]{:S(2)}) copy-start(f32[10]{0:T(128)} %constant.47) | copy-start | bytes 124
  26.4 3.4 %collective-permute-start.3 = (bf16[128,2048]{0,1:T(8,128)(2,1)S(1)}, bf16[128,2048]{0,1:T(8,128)(2,1)S(1)}, u32[]{:S(2)}, u32[]{:S(2)}) collective-permute-start(bf16[128,2048]{0,1:T(8,128)(2,1)S(1)} %bitcast.49), channel_id=1, source_target_pairs={{0,4},{4,0},{1,5},{5,1},{2,6},{6,2},{3,7},{7,3},{8,12},{12,8},{9,1... | collective-permute-start | bytes 1572872 | tf_op jit(solution)/shard_map/ppermute | solution.py:123
  113.1 3.5 %collective-permute-start.4 = (f32[3,128,1024]{2,1,0:T(8,128)S(1)}, f32[3,128,1024]{2,1,0:T(8,128)S(1)}, u32[]{:S(2)}, u32[]{:S(2)}) collective-permute-start(f32[3,128,1024]{2,1,0:T(8,128)S(1)} %slice.42), channel_id=1, source_target_pairs={{0,4},{4,0},{1,5},{5,1},{2,6},{6,2},{3,7},{7,3},{8,12},{12,8},{9,1... | collective-permute-start | bytes 4718600 | tf_op jit(solution)/shard_map/ppermute | solution.py:123
  117.0 2.9 %collective-permute-start.5 = (bf16[3,2,1024]{2,1,0:T(2,128)(2,1)S(1)}, bf16[3,2,1024]{2,1,0:T(2,128)(2,1)S(1)}, u32[]{:S(2)}, u32[]{:S(2)}) collective-permute-start(bf16[3,2,1024]{2,1,0:T(2,128)(2,1)S(1)} %slice.43), channel_id=1, source_target_pairs={{0,4},{4,8},{8,12},{12,16},{16,20},{20,24},{24,28},{28,32},{32,36}... | collective-permute-start | bytes 36872 | tf_op jit(solution)/shard_map/ppermute | solution.py:119
Sparse Core Ops, SparseCore 0:
  9.5 92.6 all-gather.1

commit v9 on v7

--- a/solution.py
+++ b/solution.py
@@ -164,11 +164,16 @@
     (taps, decay, resid, direct, lift, keep), both = lax.optimization_barrier(
         ((taps, decay, resid, direct, lift, keep), both)
     )
-    partial = jnp.stack(
-        [jnp.dot(both, piece[:, g, :], preferred_element_type=jnp.float32) for g in range(3)],
+    theirs_part = jnp.stack(
+        [jnp.dot(both[rows:], piece[:, g, :], preferred_element_type=jnp.float32) for g in range(3)],
         axis=0,
     )
-    sums = partial[:, :rows] + swapped(partial[:, rows:], "core")
+    arrived = swapped(theirs_part, "core")
+    mine_part = jnp.stack(
+        [jnp.dot(both[:rows], piece[:, g, :], preferred_element_type=jnp.float32) for g in range(3)],
+        axis=0,
+    )
+    sums = mine_part + arrived
     projected = sums.astype(jnp.bfloat16)
     edge_out = shifted(projected[:, rows - 2 :, :], ctx, 1)
     extended = jnp.concatenate([edge_out, projected], axis=1)

time: 157 us -> 155 us (0.987)
  waiting for transfers between devices: 87.6 us -> 85.1 us
    ppermute x2, waiting for transfers between devices: 3.4 us -> 0.84 us  [swapped(): return lax.ppermute(array, axis, [(0, 1), (1, 0)])]
    dot_general x3 -> x6, matrix products: 10.4 us -> 11.7 us  [the longest x3 9.45 us: per_device(): jnp.dot(both[rows:], piece[:, g, :], preferred_element_type=jnp.float32)]
  transfers between devices with their start and end apart: 7 -> 7, of which waited for: 6 -> 6; matrix products, arithmetic and copies ran while one was open for 4% -> 6% of each run, Pallas kernels for 0% -> 0%
where the time goes in v9:
time: 155 us
  waiting for transfers between devices  85.1 us (55%)
  Pallas kernels  25.8 us (17%)
  between operations  13.6 us (9%)
  matrix products  11.7 us (8%)
  starting transfers between devices  7.59 us (5%)
  local copies, waits for them, and re-layouts  5.79 us (4%)
  other arithmetic  5.17 us (3%)
    all_gather x1, waiting for transfers between devices, per_device(): piece = lax.all_gather(in_weight, 'cx', axis=0, tiled=True)  72.4 us
    pallas_call x1, Pallas kernels, per_device(): pl.pallas_call(functools.partial(block_kernel, peers, digits), out_shape=...  25.8 us
    ppermute x3, waiting for transfers between devices, gathered_tp(): lax.ppermute(tokens, 'tp', [(i, (i + by) % peers) for i in range(peers)])  10.3 us
    dot_general x3, matrix products, per_device(): jnp.dot(both[rows:], piece[:, g, :], preferred_element_type=jnp.float32)  9.45 us
    ppermute x3, starting transfers between devices, gathered_tp(): lax.ppermute(tokens, 'tp', [(i, (i + by) % peers) for i in range(peers)])  5.37 us
  transfers between devices with their start and end apart: 7, of which 6 were waited for; matrix products, arithmetic and copies ran while one was open for 6% of the time, Pallas kernels for 0%

profile of v9, /device:TPU:0, one launch (start us, length us, event | category | flops | bytes accessed | tf_op | source)
XLA Modules:
  0.0 154.8 jit_solution(12301250553312252952)
XLA Ops:
  6.5 0.7 all-gather.2.cloned.1.call-update
  7.3 1.7 %collective-permute-start = (bf16[128,1024]{1,0:T(8,128)(2,1)}, bf16[128,1024]{1,0:T(8,128)(2,1)S(1)}, u32[]{:S(2)}, u32[]{:S(2)}) collective-permute-start(bf16[128,1024]{1,0:T(8,128)(2,1)} %param.7), channel_id=1, source_target_pairs={{0,1},{1,2},{2,3},{3,0},{4,5},{5,6},{6,7},{7,4},{8,9},{9,10},{10,1... | collective-permute-start | bytes 786440 | tf_op jit(solution)/shard_map/ppermute | solution.py:130
  9.0 1.6 %collective-permute-start.2 = (bf16[128,1024]{1,0:T(8,128)(2,1)}, bf16[128,1024]{1,0:T(8,128)(2,1)S(1)}, u32[]{:S(2)}, u32[]{:S(2)}) collective-permute-start(bf16[128,1024]{1,0:T(8,128)(2,1)} %param.7), channel_id=1, source_target_pairs={{0,3},{1,0},{2,1},{3,2},{4,7},{5,4},{6,5},{7,6},{8,11},{9,8},{10,9... | collective-permute-start | bytes 786440 | tf_op jit(solution)/shard_map/ppermute | solution.py:130
  10.6 2.1 %collective-permute-start.1 = (bf16[128,1024]{1,0:T(8,128)(2,1)}, bf16[128,1024]{1,0:T(8,128)(2,1)S(1)}, u32[]{:S(2)}, u32[]{:S(2)}) collective-permute-start(bf16[128,1024]{1,0:T(8,128)(2,1)} %param.7), channel_id=1, source_target_pairs={{0,2},{1,3},{2,0},{3,1},{4,6},{5,7},{6,4},{7,5},{8,10},{9,11},{10,... | collective-permute-start | bytes 786440 | tf_op jit(solution)/shard_map/ppermute | solution.py:130
  12.6 0.7 sort.17
  13.4 3.5 %collective-permute-done = bf16[128,1024]{1,0:T(8,128)(2,1)S(1)} collective-permute-done((bf16[128,1024]{1,0:T(8,128)(2,1)}, bf16[128,1024]{1,0:T(8,128)(2,1)S(1)}, u32[]{:S(2)}, u32[]{:S(2)}) %collective-permute-start) | collective-permute-done | bytes 262176 | tf_op jit(solution)/shard_map/ppermute | solution.py:130
  16.9 5.1 %collective-permute-done.2 = bf16[128,1024]{1,0:T(8,128)(2,1)S(1)} collective-permute-done((bf16[128,1024]{1,0:T(8,128)(2,1)}, bf16[128,1024]{1,0:T(8,128)(2,1)S(1)}, u32[]{:S(2)}, u32[]{:S(2)}) %collective-permute-start.2) | collective-permute-done | bytes 262176 | tf_op jit(solution)/shard_map/ppermute | solution.py:130
  22.0 1.7 %collective-permute-done.1 = bf16[128,1024]{1,0:T(8,128)(2,1)S(1)} collective-permute-done((bf16[128,1024]{1,0:T(8,128)(2,1)}, bf16[128,1024]{1,0:T(8,128)(2,1)S(1)}, u32[]{:S(2)}, u32[]{:S(2)}) %collective-permute-start.1) | collective-permute-done | bytes 262176 | tf_op jit(solution)/shard_map/ppermute | solution.py:130
  23.7 1.1 pad_maximum_fusion.1
  24.9 0.6 gather_fusion
  25.7 0.7 copy.8
  26.5 0.6 reshape.46.taps_ref
  27.2 0.6 copy.10
  27.8 0.6 copy.9
  28.5 1.1 multiply_exponential_fusion
  29.8 72.4 %all-gather.2.cloned.1.call-done = bf16[2048,3,1024]{2,0,1:T(8,128)(2,1)} async-done(((bf16[128,3,1024]{2,0,1:T(8,128)(2,1)}), bf16[2048,3,1024]{2,0,1:T(8,128)(2,1)}) %all-gather.2.cloned.1.call-update) | async-done | bytes 12582928 | tf_op jit(solution)/shard_map/all_gather | solution.py:144
  102.2 2.9 %fusion.10 = f32[1,128,1024]{2,1,0:T(8,128)S(1)} fusion(bf16[2048,3,1024]{2,0,1:T(8,128)(2,1)} %all-gather.2.cloned.1.call-done, bf16[256,2048]{0,1:T(8,128)(2,1)S(1)} %pad_maximum_fusion.2), kind=kOutput, calls=%fused_computation.16 | convolution fusion | flops 536870912 | bytes 5242880 | tf_op jit(solution)/shard_map/dot_general | solution.py:168
  105.1 3.1 %fusion.8 = f32[1,128,1024]{2,1,0:T(8,128)S(1)} fusion(bf16[2048,3,1024]{2,0,1:T(8,128)(2,1)} %all-gather.2.cloned.1.call-done, bf16[256,2048]{0,1:T(8,128)(2,1)S(1)} %pad_maximum_fusion.2), kind=kOutput, calls=%fused_computation.14 | convolution fusion | flops 536870912 | bytes 5242880 | tf_op jit(solution)/shard_map/dot_general | solution.py:168
  108.2 3.5 %fusion.12 = f32[1,128,1024]{2,1,0:T(8,128)S(1)} fusion(bf16[2048,3,1024]{2,0,1:T(8,128)(2,1)} %all-gather.2.cloned.1.call-done, bf16[256,2048]{0,1:T(8,128)(2,1)S(1)} %pad_maximum_fusion.2), kind=kOutput, calls=%fused_computation.18 | convolution fusion | flops 536870912 | bytes 5242880 | tf_op jit(solution)/shard_map/dot_general | solution.py:168
  111.9 0.3 copy-done.5
  112.2 0.7 fusion.9
  112.9 0.8 fusion.7
  113.7 0.8 fusion.11
  114.5 0.8 collective-permute-done.4
  115.3 0.3 fusion.6
  115.7 2.0 %collective-permute-start.5 = (bf16[3,2,1024]{2,1,0:T(2,128)(2,1)S(1)}, bf16[3,2,1024]{2,1,0:T(2,128)(2,1)S(1)}, u32[]{:S(2)}, u32[]{:S(2)}) collective-permute-start(bf16[3,2,1024]{2,1,0:T(2,128)(2,1)S(1)} %slice.48), channel_id=1, source_target_pairs={{0,4},{4,8},{8,12},{12,16},{16,20},{20,24},{24,28},{28,32},{32,36}... | collective-permute-start | bytes 36872 | tf_op jit(solution)/shard_map/ppermute | solution.py:119
  117.7 0.8 collective-permute-done.5
  118.5 0.2 pad_maximum_fusion.3
  118.8 1.5 reshape.53.x_ref
  120.3 25.8 %shard_map.73 = f32[128,8,128]{2,1,0:T(8,128)} custom-call(f32[3,130,8,128]{3,2,1,0:T(8,128)} %reshape.53.x_ref, f32[3,3,8,128]{3,2,1,0:T(8,128)} %reshape.46.taps_ref, f32[16,8,128]{2,1,0:T(8,128)} %bitcast.63, f32[16,8,128]{2,1,0:T(8,128)} %bitcast.62, f32[8,128]{1,0:T(8,128)} %bitcast.70, f32[7,16,8,128]{3,2,1,0:T(8,128)} %get-tuple-element.19.lift_ref, ...), custom_call_target="tpu_custom_call" | custom-call | tf_op jit(solution)/shard_map/pallas_call | solution.py:183
  146.1 1.1 convert_element_type.11
  147.2 0.8 copy.14
  (27 shorter events, 0.8 us)
Async XLA Ops:
  6.5 95.6 %all-gather.2.cloned.1.call-start = ((), (), s32[]{:S(2)}) async-start(), calls=%async_computation | async-start | bytes 13369344 | tf_op jit(solution)/shard_map/all_gather | solution.py:144
  7.3 9.7 %collective-permute-start = (bf16[128,1024]{1,0:T(8,128)(2,1)}, bf16[128,1024]{1,0:T(8,128)(2,1)S(1)}, u32[]{:S(2)}, u32[]{:S(2)}) collective-permute-start(bf16[128,1024]{1,0:T(8,128)(2,1)} %param.7), channel_id=1, source_target_pairs={{0,1},{1,2},{2,3},{3,0},{4,5},{5,6},{6,7},{7,4},{8,9},{9,10},{10,1... | collective-permute-start | bytes 786440 | tf_op jit(solution)/shard_map/ppermute | solution.py:130
  9.0 13.1 %collective-permute-start.2 = (bf16[128,1024]{1,0:T(8,128)(2,1)}, bf16[128,1024]{1,0:T(8,128)(2,1)S(1)}, u32[]{:S(2)}, u32[]{:S(2)}) collective-permute-start(bf16[128,1024]{1,0:T(8,128)(2,1)} %param.7), channel_id=1, source_target_pairs={{0,3},{1,0},{2,1},{3,2},{4,7},{5,4},{6,5},{7,6},{8,11},{9,8},{10,9... | collective-permute-start | bytes 786440 | tf_op jit(solution)/shard_map/ppermute | solution.py:130
  10.6 13.2 %collective-permute-start.1 = (bf16[128,1024]{1,0:T(8,128)(2,1)}, bf16[128,1024]{1,0:T(8,128)(2,1)S(1)}, u32[]{:S(2)}, u32[]{:S(2)}) collective-permute-start(bf16[128,1024]{1,0:T(8,128)(2,1)} %param.7), channel_id=1, source_target_pairs={{0,2},{1,3},{2,0},{3,1},{4,6},{5,7},{6,4},{7,5},{8,10},{9,11},{10,... | collective-permute-start | bytes 786440 | tf_op jit(solution)/shard_map/ppermute | solution.py:130
  24.8 1.7 %copy-start.2 = (f32[3,3,1024]{2,1,0:T(4,128)S(1)}, f32[3,3,1024]{2,1,0:T(4,128)}, u32[]{:S(2)}) copy-start(f32[3,3,1024]{2,1,0:T(4,128)} %param.9) | copy-start | bytes 110596
  24.8 2.3 %copy-start.1 = (f32[16,1024]{1,0:T(8,128)S(1)}, f32[16,1024]{1,0:T(8,128)}, u32[]{:S(2)}) copy-start(f32[16,1024]{1,0:T(8,128)} %param.11) | copy-start | bytes 196612
  24.8 3.0 %copy-start = (f32[16,1024]{1,0:T(8,128)S(1)}, f32[16,1024]{1,0:T(8,128)}, u32[]{:S(2)}) copy-start(f32[16,1024]{1,0:T(8,128)} %param.10) | copy-start | bytes 196612
  24.9 3.6 %copy-start.3 = (f32[7]{0:T(128)S(1)}, f32[7]{0:T(128)}, u32[]{:S(2)}) copy-start(f32[7]{0:T(128)} %constant.48) | copy-start | bytes 88
  24.9 3.6 %copy-start.4 = (f32[7]{0:T(128)S(1)}, f32[7]{0:T(128)}, u32[]{:S(2)}) copy-start(f32[7]{0:T(128)} %constant.47) | copy-start | bytes 88
  26.4 3.2 %collective-permute-start.3 = (bf16[128,2048]{0,1:T(8,128)(2,1)S(1)}, bf16[128,2048]{0,1:T(8,128)(2,1)S(1)}, u32[]{:S(2)}, u32[]{:S(2)}) collective-permute-start(bf16[128,2048]{0,1:T(8,128)(2,1)S(1)} %bitcast.61), channel_id=1, source_target_pairs={{0,4},{4,0},{1,5},{5,1},{2,6},{6,2},{3,7},{7,3},{8,12},{12,8},{9,1... | collective-permute-start | bytes 1572872 | tf_op jit(solution)/shard_map/ppermute | solution.py:123
  105.1 7.1 %copy-start.5 = (bf16[2048,3,1024]{2,0,1:T(8,128)(2,1)S(1)}, bf16[2048,3,1024]{2,0,1:T(8,128)(2,1)}, u32[]{:S(2)}) copy-start(bf16[2048,3,1024]{2,0,1:T(8,128)(2,1)} %all-gather.2.cloned.1.call-done) | copy-start | bytes 37748740
  111.8 3.5 %collective-permute-start.4 = (f32[3,128,1024]{2,1,0:T(8,128)S(1)}, f32[3,128,1024]{2,1,0:T(8,128)S(1)}, u32[]{:S(2)}, u32[]{:S(2)}) collective-permute-start(f32[3,128,1024]{2,1,0:T(8,128)S(1)} %pad_maximum_fusion), channel_id=1, source_target_pairs={{0,4},{4,0},{1,5},{5,1},{2,6},{6,2},{3,7},{7,3},{8,12},{12,8},{9,1... | collective-permute-start | bytes 4718600 | tf_op jit(solution)/shard_map/ppermute | solution.py:123
  115.7 2.9 %collective-permute-start.5 = (bf16[3,2,1024]{2,1,0:T(2,128)(2,1)S(1)}, bf16[3,2,1024]{2,1,0:T(2,128)(2,1)S(1)}, u32[]{:S(2)}, u32[]{:S(2)}) collective-permute-start(bf16[3,2,1024]{2,1,0:T(2,128)(2,1)S(1)} %slice.48), channel_id=1, source_target_pairs={{0,4},{4,8},{8,12},{12,16},{16,20},{20,24},{24,28},{28,32},{32,36}... | collective-permute-start | bytes 36872 | tf_op jit(solution)/shard_map/ppermute | solution.py:119
Sparse Core Ops, SparseCore 0:
  9.5 92.6 all-gather.1

commit v10 on v7

--- a/solution.py
+++ b/solution.py
@@ -105,6 +105,29 @@
         digits.append(digit)
         peers //= digit
     return digits or [2]
+
+
+def matmul_kernel(a_ref, w_ref, o_ref):
+    o_ref[...] = jnp.dot(a_ref[...], w_ref[...], preferred_element_type=jnp.float32)
+
+
+def stream_matmul(a, w, g):
+    m, k = a.shape
+    n = w.shape[2]
+    tn = 512 if n % 512 == 0 else n
+    return pl.pallas_call(
+        matmul_kernel,
+        out_shape=jax.ShapeDtypeStruct((m, n), jnp.float32),
+        grid=(n // tn,),
+        in_specs=[
+            pl.BlockSpec((m, k), lambda j: (0, 0)),
+            pl.BlockSpec((None, k, tn), lambda j: (g, 0, j)),
+        ],
+        out_specs=pl.BlockSpec((m, tn), lambda j: (0, j)),
+        cost_estimate=pl.CostEstimate(
+            flops=2 * m * k * n, transcendentals=0, bytes_accessed=2 * (m * k + k * n) + 4 * m * n
+        ),
+    )(a, w)
 
 
 def vmem_specs(n):
@@ -164,11 +187,15 @@
     (taps, decay, resid, direct, lift, keep), both = lax.optimization_barrier(
         ((taps, decay, resid, direct, lift, keep), both)
     )
-    partial = jnp.stack(
-        [jnp.dot(both, piece[:, g, :], preferred_element_type=jnp.float32) for g in range(3)],
-        axis=0,
-    )
-    sums = partial[:, :rows] + swapped(partial[:, rows:], "core")
+    streams = jnp.transpose(piece, (1, 0, 2))
+    arrived, mine_part = [], []
+    for g in range(3):
+        part = stream_matmul(both, streams, g)
+        arrived.append(swapped(part[rows:], "core"))
+        mine_part.append(part[:rows])
+    arrived = jnp.stack(arrived, axis=0)
+    mine_part = jnp.stack(mine_part, axis=0)
+    sums = mine_part + arrived
     projected = sums.astype(jnp.bfloat16)
     edge_out = shifted(projected[:, rows - 2 :, :], ctx, 1)
     extended = jnp.concatenate([edge_out, projected], axis=1)

time: 157 us -> 159 us (1.013)
  Pallas kernels: 25.8 us -> 38.3 us
  matrix products: 10.4 us -> 0 us
  waiting for transfers between devices: 87.6 us -> 84.7 us
  local copies, waits for them, and re-layouts: 5.59 us -> 7.82 us
    pallas_call x0 -> x3, Pallas kernels: none -> 12.4 us  [stream_matmul(): pl.pallas_call(matmul_kernel, out_shape=jax.ShapeDtypeStruct((m, n), jnp....]
    dot_general x3 -> x0, matrix products: 10.4 us -> none  [per_device(): jnp.dot(both, piece[:, g, :], preferred_element_type=jnp.float32)]
    all_gather x1, waiting for transfers between devices: 72.4 us -> 70.7 us  [per_device(): piece = lax.all_gather(in_weight, 'cx', axis=0, tiled=True)]
    unnamed x14 -> x20, local copies, waits for them, and re-layouts: 2.08 us -> 3.71 us
    ppermute x2 -> x4, waiting for transfers between devices: 3.4 us -> 2.15 us  [swapped(): return lax.ppermute(array, axis, [(0, 1), (1, 0)])]
  transfers between devices with their start and end apart: 7 -> 9, of which waited for: 6 -> 7; matrix products, arithmetic and copies ran while one was open for 4% -> 5% of each run, Pallas kernels for 0% -> 0%
where the time goes in v10:
time: 159 us; the launch traced here: 158 us
  waiting for transfers between devices  84.7 us (53%)
  Pallas kernels  38.3 us (24%)
  between operations  13.6 us (9%)
  starting transfers between devices  8.17 us (5%)
  local copies, waits for them, and re-layouts  7.82 us (5%)
  other arithmetic  5.89 us (4%)
    all_gather x1, waiting for transfers between devices, per_device(): piece = lax.all_gather(in_weight, 'cx', axis=0, tiled=True)  70.7 us
    pallas_call x1, Pallas kernels, per_device(): pl.pallas_call(functools.partial(block_kernel, peers, digits), out_shape=...  25.8 us
    pallas_call x3, Pallas kernels, stream_matmul(): pl.pallas_call(matmul_kernel, out_shape=jax.ShapeDtypeStruct((m, n), jnp....  12.4 us
    ppermute x3, waiting for transfers between devices, gathered_tp(): lax.ppermute(tokens, 'tp', [(i, (i + by) % peers) for i in range(peers)])  10.3 us
    ppermute x3, starting transfers between devices, gathered_tp(): lax.ppermute(tokens, 'tp', [(i, (i + by) % peers) for i in range(peers)])  5.37 us
    unnamed x20, local copies, waits for them, and re-layouts  3.71 us
  transfers between devices with their start and end apart: 9, of which 7 were waited for; matrix products, arithmetic and copies ran while one was open for 5% of the time, Pallas kernels for 0%

profile of v10, /device:TPU:0, one launch (start us, length us, event | category | flops | bytes accessed | tf_op | source)
XLA Modules:
  0.0 158.5 jit_solution(15186131729143331239)
XLA Ops:
  6.5 0.7 all-gather.2.cloned.1.call-update
  7.3 1.7 %collective-permute-start = (bf16[128,1024]{1,0:T(8,128)(2,1)}, bf16[128,1024]{1,0:T(8,128)(2,1)S(1)}, u32[]{:S(2)}, u32[]{:S(2)}) collective-permute-start(bf16[128,1024]{1,0:T(8,128)(2,1)} %param.7), channel_id=1, source_target_pairs={{0,1},{1,2},{2,3},{3,0},{4,5},{5,6},{6,7},{7,4},{8,9},{9,10},{10,1... | collective-permute-start | bytes 786440 | tf_op jit(solution)/shard_map/ppermute | solution.py:153
  9.0 1.6 collective-permute-start.2
  10.6 2.1 %collective-permute-start.1 = (bf16[128,1024]{1,0:T(8,128)(2,1)}, bf16[128,1024]{1,0:T(8,128)(2,1)S(1)}, u32[]{:S(2)}, u32[]{:S(2)}) collective-permute-start(bf16[128,1024]{1,0:T(8,128)(2,1)} %param.7), channel_id=1, source_target_pairs={{0,2},{1,3},{2,0},{3,1},{4,6},{5,7},{6,4},{7,5},{8,10},{9,11},{10,... | collective-permute-start | bytes 786440 | tf_op jit(solution)/shard_map/ppermute | solution.py:153
  12.6 0.7 sort.17
  13.4 3.5 %collective-permute-done = bf16[128,1024]{1,0:T(8,128)(2,1)S(1)} collective-permute-done((bf16[128,1024]{1,0:T(8,128)(2,1)}, bf16[128,1024]{1,0:T(8,128)(2,1)S(1)}, u32[]{:S(2)}, u32[]{:S(2)}) %collective-permute-start) | collective-permute-done | bytes 262176 | tf_op jit(solution)/shard_map/ppermute | solution.py:153
  16.9 5.1 %collective-permute-done.2 = bf16[128,1024]{1,0:T(8,128)(2,1)S(1)} collective-permute-done((bf16[128,1024]{1,0:T(8,128)(2,1)}, bf16[128,1024]{1,0:T(8,128)(2,1)S(1)}, u32[]{:S(2)}, u32[]{:S(2)}) %collective-permute-start.2) | collective-permute-done | bytes 262176 | tf_op jit(solution)/shard_map/ppermute | solution.py:153
  22.0 1.7 %collective-permute-done.1 = bf16[128,1024]{1,0:T(8,128)(2,1)S(1)} collective-permute-done((bf16[128,1024]{1,0:T(8,128)(2,1)}, bf16[128,1024]{1,0:T(8,128)(2,1)S(1)}, u32[]{:S(2)}, u32[]{:S(2)}) %collective-permute-start.1) | collective-permute-done | bytes 262176 | tf_op jit(solution)/shard_map/ppermute | solution.py:153
  23.7 1.1 pad_maximum_fusion
  24.8 0.6 gather_fusion
  25.6 0.7 copy.10
  26.7 0.3 copy-done.5
  27.1 0.6 reshape.46.taps_ref
  27.7 0.6 copy.16
  28.4 0.6 copy.15
  29.0 1.1 multiply_exponential_fusion
  30.4 1.0 pad_maximum_fusion.1.a_ref
  31.4 70.7 %all-gather.2.cloned.1.call-done = bf16[2048,3,1024]{2,0,1:T(8,128)(2,1)} async-done(((bf16[128,3,1024]{2,0,1:T(8,128)(2,1)}), bf16[2048,3,1024]{2,0,1:T(8,128)(2,1)}) %all-gather.2.cloned.1.call-update) | async-done | bytes 12582928 | tf_op jit(solution)/shard_map/all_gather | solution.py:167
  102.2 4.2 %shard_map.75 = f32[256,1024]{1,0:T(8,128)} custom-call(bf16[256,2048]{1,0:T(8,128)(2,1)} %pad_maximum_fusion.1.a_ref, bf16[3,2048,1024]{2,1,0:T(8,128)(2,1)} %bitcast.32), custom_call_target="tpu_custom_call" | custom-call | flops 1073741824 | bytes 6291456 | tf_op jit(solution)/shard_map/pallas_call | solution.py:118
  106.3 4.1 %shard_map.74 = f32[256,1024]{1,0:T(8,128)} custom-call(bf16[256,2048]{1,0:T(8,128)(2,1)} %pad_maximum_fusion.1.a_ref, bf16[3,2048,1024]{2,1,0:T(8,128)(2,1)} %bitcast.33), custom_call_target="tpu_custom_call" | custom-call | flops 1073741824 | bytes 6291456 | tf_op jit(solution)/shard_map/pallas_call | solution.py:118
  110.4 4.2 %shard_map.73 = f32[256,1024]{1,0:T(8,128)} custom-call(bf16[256,2048]{1,0:T(8,128)(2,1)} %pad_maximum_fusion.1.a_ref, bf16[3,2048,1024]{2,1,0:T(8,128)(2,1)} %bitcast.34), custom_call_target="tpu_custom_call" | custom-call | flops 1073741824 | bytes 6291456 | tf_op jit(solution)/shard_map/pallas_call | solution.py:118
  114.8 1.0 copy-done.1
  116.3 0.5 collective-permute-start.4
  116.8 1.4 collective-permute-done.5
  118.2 0.7 collective-permute-done.4
  119.0 0.3 fusion
  119.4 2.0 %collective-permute-start.7 = (bf16[3,2,1024]{2,1,0:T(2,128)(2,1)S(1)}, bf16[3,2,1024]{2,1,0:T(2,128)(2,1)S(1)}, u32[]{:S(2)}, u32[]{:S(2)}) collective-permute-start(bf16[3,2,1024]{2,1,0:T(2,128)(2,1)S(1)} %slice.48), channel_id=1, source_target_pairs={{0,4},{4,8},{8,12},{12,16},{16,20},{20,24},{24,28},{28,32},{32,36}... | collective-permute-start | bytes 36872 | tf_op jit(solution)/shard_map/ppermute | solution.py:142
  121.4 0.8 collective-permute-done.7
  122.5 1.5 reshape.53.x_ref
  124.0 25.8 %shard_map.76 = f32[128,8,128]{2,1,0:T(8,128)} custom-call(f32[3,130,8,128]{3,2,1,0:T(8,128)} %reshape.53.x_ref, f32[3,3,8,128]{3,2,1,0:T(8,128)} %reshape.46.taps_ref, f32[16,8,128]{2,1,0:T(8,128)} %bitcast.43, f32[16,8,128]{2,1,0:T(8,128)} %bitcast.42, f32[8,128]{1,0:T(8,128)} %bitcast.50, f32[7,16,8,128]{3,2,1,0:T(8,128)} %get-tuple-element.19.lift_ref, ...), custom_call_target="tpu_custom_call" | custom-call | tf_op jit(solution)/shard_map/pallas_call | solution.py:205
  149.8 1.1 convert_element_type.11
  150.9 0.8 copy.20
  (36 shorter events, 1.8 us)
Async XLA Ops:
  6.5 95.6 %all-gather.2.cloned.1.call-start = ((), (), s32[]{:S(2)}) async-start(), calls=%async_computation | async-start | bytes 13369344 | tf_op jit(solution)/shard_map/all_gather | solution.py:167
  7.3 9.7 %collective-permute-start = (bf16[128,1024]{1,0:T(8,128)(2,1)}, bf16[128,1024]{1,0:T(8,128)(2,1)S(1)}, u32[]{:S(2)}, u32[]{:S(2)}) collective-permute-start(bf16[128,1024]{1,0:T(8,128)(2,1)} %param.7), channel_id=1, source_target_pairs={{0,1},{1,2},{2,3},{3,0},{4,5},{5,6},{6,7},{7,4},{8,9},{9,10},{10,1... | collective-permute-start | bytes 786440 | tf_op jit(solution)/shard_map/ppermute | solution.py:153
  9.0 13.1 %collective-permute-start.2 = (bf16[128,1024]{1,0:T(8,128)(2,1)}, bf16[128,1024]{1,0:T(8,128)(2,1)S(1)}, u32[]{:S(2)}, u32[]{:S(2)}) collective-permute-start(bf16[128,1024]{1,0:T(8,128)(2,1)} %param.7), channel_id=1, source_target_pairs={{0,3},{1,0},{2,1},{3,2},{4,7},{5,4},{6,5},{7,6},{8,11},{9,8},{10,9... | collective-permute-start | bytes 786440 | tf_op jit(solution)/shard_map/ppermute | solution.py:153
  10.6 13.2 %collective-permute-start.1 = (bf16[128,1024]{1,0:T(8,128)(2,1)}, bf16[128,1024]{1,0:T(8,128)(2,1)S(1)}, u32[]{:S(2)}, u32[]{:S(2)}) collective-permute-start(bf16[128,1024]{1,0:T(8,128)(2,1)} %param.7), channel_id=1, source_target_pairs={{0,2},{1,3},{2,0},{3,1},{4,6},{5,7},{6,4},{7,5},{8,10},{9,11},{10,... | collective-permute-start | bytes 786440 | tf_op jit(solution)/shard_map/ppermute | solution.py:153
  26.3 0.8 copy-start.5
  26.3 1.4 copy-start.4
  26.3 2.0 %copy-start.3 = (f32[16,1024]{1,0:T(8,128)S(1)}, f32[16,1024]{1,0:T(8,128)}, u32[]{:S(2)}) copy-start(f32[16,1024]{1,0:T(8,128)} %param.10) | copy-start | bytes 196612
  26.3 2.7 %copy-start.6 = (f32[7]{0:T(128)S(1)}, f32[7]{0:T(128)}, u32[]{:S(2)}) copy-start(f32[7]{0:T(128)} %constant.48) | copy-start | bytes 88
  26.3 2.7 %copy-start.7 = (f32[7]{0:T(128)S(1)}, f32[7]{0:T(128)}, u32[]{:S(2)}) copy-start(f32[7]{0:T(128)} %constant.47) | copy-start | bytes 88
  26.6 3.7 %collective-permute-start.3 = (bf16[128,2048]{1,0:T(8,128)(2,1)S(1)}, bf16[128,2048]{1,0:T(8,128)(2,1)S(1)}, u32[]{:S(2)}, u32[]{:S(2)}) collective-permute-start(bf16[128,2048]{1,0:T(8,128)(2,1)S(1)} %copy.14), channel_id=1, source_target_pairs={{0,4},{4,0},{1,5},{5,1},{2,6},{6,2},{3,7},{7,3},{8,12},{12,8},{9,1... | collective-permute-start | bytes 1572872 | tf_op jit(solution)/shard_map/ppermute | solution.py:146
  110.4 4.2 %copy-start.2 = (f32[256,1024]{1,0:T(8,128)S(1)}, f32[256,1024]{1,0:T(8,128)}, u32[]{:S(2)}) copy-start(f32[256,1024]{1,0:T(8,128)} %shard_map.75) | copy-start | bytes 3145732
  114.6 1.2 copy-start.1
  114.7 1.5 copy-start
  114.7 2.1 %collective-permute-start.6 = (f32[128,1024]{1,0:T(8,128)S(1)}, f32[128,1024]{1,0:T(8,128)S(1)}, u32[]{:S(2)}, u32[]{:S(2)}) collective-permute-start(f32[128,1024]{1,0:T(8,128)S(1)} %get-tuple-element.25), channel_id=1, source_target_pairs={{0,4},{4,0},{1,5},{5,1},{2,6},{6,2},{3,7},{7,3},{8,12},{12,8},{9,1... | collective-permute-start | bytes 1572872 | tf_op jit(solution)/shard_map/ppermute | solution.py:146
  116.3 2.0 %collective-permute-start.5 = (f32[128,1024]{1,0:T(8,128)S(1)}, f32[128,1024]{1,0:T(8,128)S(1)}, u32[]{:S(2)}, u32[]{:S(2)}) collective-permute-start(f32[128,1024]{1,0:T(8,128)S(1)} %get-tuple-element.23), channel_id=1, source_target_pairs={{0,4},{4,0},{1,5},{5,1},{2,6},{6,2},{3,7},{7,3},{8,12},{12,8},{9,1... | collective-permute-start | bytes 1572872 | tf_op jit(solution)/shard_map/ppermute | solution.py:146
  116.3 2.6 %collective-permute-start.4 = (f32[128,1024]{1,0:T(8,128)S(1)}, f32[128,1024]{1,0:T(8,128)S(1)}, u32[]{:S(2)}, u32[]{:S(2)}) collective-permute-start(f32[128,1024]{1,0:T(8,128)S(1)} %get-tuple-element.21), channel_id=1, source_target_pairs={{0,4},{4,0},{1,5},{5,1},{2,6},{6,2},{3,7},{7,3},{8,12},{12,8},{9,1... | collective-permute-start | bytes 1572872 | tf_op jit(solution)/shard_map/ppermute | solution.py:146
  119.4 2.9 %collective-permute-start.7 = (bf16[3,2,1024]{2,1,0:T(2,128)(2,1)S(1)}, bf16[3,2,1024]{2,1,0:T(2,128)(2,1)S(1)}, u32[]{:S(2)}, u32[]{:S(2)}) collective-permute-start(bf16[3,2,1024]{2,1,0:T(2,128)(2,1)S(1)} %slice.48), channel_id=1, source_target_pairs={{0,4},{4,8},{8,12},{12,16},{16,20},{20,24},{24,28},{28,32},{32,36}... | collective-permute-start | bytes 36872 | tf_op jit(solution)/shard_map/ppermute | solution.py:142
Sparse Core Ops, SparseCore 0:
  9.5 92.6 all-gather.1

commit v11 on v7

--- a/solution.py
+++ b/solution.py
@@ -105,6 +105,39 @@
         digits.append(digit)
         peers //= digit
     return digits or [2]
+
+
+def matmul_kernel(a_ref, w_ref, o_ref):
+    k = pl.program_id(1)
+    tk = w_ref.shape[0]
+
+    @pl.when(k == 0)
+    def _():
+        o_ref[...] = jnp.zeros(o_ref.shape, jnp.float32)
+
+    cols = pl.ds(pl.multiple_of(k * tk, tk), tk)
+    o_ref[...] += jnp.dot(a_ref[:, cols], w_ref[...], preferred_element_type=jnp.float32)
+
+
+def stream_matmul(a, w):
+    m, depth = a.shape
+    streams, _, n = w.shape
+    tk = 512 if depth % 512 == 0 else depth
+    return pl.pallas_call(
+        matmul_kernel,
+        out_shape=jax.ShapeDtypeStruct((streams, m, n), jnp.float32),
+        grid=(streams, depth // tk),
+        in_specs=[
+            pl.BlockSpec((m, depth), lambda g, k: (0, 0)),
+            pl.BlockSpec((None, tk, n), lambda g, k: (g, k, 0)),
+        ],
+        out_specs=pl.BlockSpec((None, m, n), lambda g, k: (g, 0, 0)),
+        cost_estimate=pl.CostEstimate(
+            flops=2 * m * depth * n * streams,
+            transcendentals=0,
+            bytes_accessed=2 * (m * depth + depth * n * streams) + 4 * m * n * streams,
+        ),
+    )(a, w)
 
 
 def vmem_specs(n):
@@ -164,11 +197,10 @@
     (taps, decay, resid, direct, lift, keep), both = lax.optimization_barrier(
         ((taps, decay, resid, direct, lift, keep), both)
     )
-    partial = jnp.stack(
-        [jnp.dot(both, piece[:, g, :], preferred_element_type=jnp.float32) for g in range(3)],
-        axis=0,
-    )
-    sums = partial[:, :rows] + swapped(partial[:, rows:], "core")
+    part = stream_matmul(both, jnp.transpose(piece, (1, 0, 2)))
+    arrived = swapped(part[:, rows:], "core")
+    mine_part = part[:, :rows]
+    sums = mine_part + arrived
     projected = sums.astype(jnp.bfloat16)
     edge_out = shifted(projected[:, rows - 2 :, :], ctx, 1)
     extended = jnp.concatenate([edge_out, projected], axis=1)

time: 157 us -> 161 us (1.025)
  Pallas kernels: 25.8 us -> 38.9 us
  matrix products: 10.4 us -> 0 us
  local copies, waits for them, and re-layouts: 5.59 us -> 7.94 us
  waiting for transfers between devices: 87.6 us -> 85.9 us
    pallas_call x0 -> x1, Pallas kernels: none -> 13.1 us  [stream_matmul(): pl.pallas_call(matmul_kernel, out_shape=jax.ShapeDtypeStruct((streams, m,...]
    dot_general x3 -> x0, matrix products: 10.4 us -> none  [per_device(): jnp.dot(both, piece[:, g, :], preferred_element_type=jnp.float32)]
    all_gather x1, waiting for transfers between devices: 72.4 us -> 70.7 us  [per_device(): piece = lax.all_gather(in_weight, 'cx', axis=0, tiled=True)]
  transfers between devices with their start and end apart: 7 -> 7, of which waited for: 6 -> 6; matrix products, arithmetic and copies ran while one was open for 4% -> 5% of each run, Pallas kernels for 0% -> 0%
where the time goes in v11:
time: 161 us; the launch traced here: 160 us
  waiting for transfers between devices  85.9 us (53%)
  Pallas kernels  38.9 us (24%)
  between operations  13.6 us (8%)
  local copies, waits for them, and re-layouts  7.94 us (5%)
  starting transfers between devices  7.59 us (5%)
  other arithmetic  5.91 us (4%)
    all_gather x1, waiting for transfers between devices, per_device(): piece = lax.all_gather(in_weight, 'cx', axis=0, tiled=True)  70.7 us
    pallas_call x1, Pallas kernels, per_device(): pl.pallas_call(functools.partial(block_kernel, peers, digits), out_shape=...  25.8 us
    pallas_call x1, Pallas kernels, stream_matmul(): pl.pallas_call(matmul_kernel, out_shape=jax.ShapeDtypeStruct((streams, m,...  13.1 us
    ppermute x3, waiting for transfers between devices, gathered_tp(): lax.ppermute(tokens, 'tp', [(i, (i + by) % peers) for i in range(peers)])  10.3 us
    ppermute x3, starting transfers between devices, gathered_tp(): lax.ppermute(tokens, 'tp', [(i, (i + by) % peers) for i in range(peers)])  5.37 us
    ppermute x2, waiting for transfers between devices, swapped(): return lax.ppermute(array, axis, [(0, 1), (1, 0)])  3.4 us
  transfers between devices with their start and end apart: 7, of which 6 were waited for; matrix products, arithmetic and copies ran while one was open for 5% of the time, Pallas kernels for 0%

profile of v11, /device:TPU:0, one launch (start us, length us, event | category | flops | bytes accessed | tf_op | source)
XLA Modules:
  0.0 159.8 jit_solution(11491480247754118435)
XLA Ops:
  6.5 0.7 all-gather.2.cloned.1.call-update
  7.3 1.7 %collective-permute-start = (bf16[128,1024]{1,0:T(8,128)(2,1)}, bf16[128,1024]{1,0:T(8,128)(2,1)S(1)}, u32[]{:S(2)}, u32[]{:S(2)}) collective-permute-start(bf16[128,1024]{1,0:T(8,128)(2,1)} %param.7), channel_id=1, source_target_pairs={{0,1},{1,2},{2,3},{3,0},{4,5},{5,6},{6,7},{7,4},{8,9},{9,10},{10,1... | collective-permute-start | bytes 786440 | tf_op jit(solution)/shard_map/ppermute | solution.py:163
  9.0 1.6 collective-permute-start.2
  10.6 2.1 %collective-permute-start.1 = (bf16[128,1024]{1,0:T(8,128)(2,1)}, bf16[128,1024]{1,0:T(8,128)(2,1)S(1)}, u32[]{:S(2)}, u32[]{:S(2)}) collective-permute-start(bf16[128,1024]{1,0:T(8,128)(2,1)} %param.7), channel_id=1, source_target_pairs={{0,2},{1,3},{2,0},{3,1},{4,6},{5,7},{6,4},{7,5},{8,10},{9,11},{10,... | collective-permute-start | bytes 786440 | tf_op jit(solution)/shard_map/ppermute | solution.py:163
  12.6 0.7 sort.17
  13.4 3.5 %collective-permute-done = bf16[128,1024]{1,0:T(8,128)(2,1)S(1)} collective-permute-done((bf16[128,1024]{1,0:T(8,128)(2,1)}, bf16[128,1024]{1,0:T(8,128)(2,1)S(1)}, u32[]{:S(2)}, u32[]{:S(2)}) %collective-permute-start) | collective-permute-done | bytes 262176 | tf_op jit(solution)/shard_map/ppermute | solution.py:163
  16.9 5.1 %collective-permute-done.2 = bf16[128,1024]{1,0:T(8,128)(2,1)S(1)} collective-permute-done((bf16[128,1024]{1,0:T(8,128)(2,1)}, bf16[128,1024]{1,0:T(8,128)(2,1)S(1)}, u32[]{:S(2)}, u32[]{:S(2)}) %collective-permute-start.2) | collective-permute-done | bytes 262176 | tf_op jit(solution)/shard_map/ppermute | solution.py:163
  22.0 1.7 %collective-permute-done.1 = bf16[128,1024]{1,0:T(8,128)(2,1)S(1)} collective-permute-done((bf16[128,1024]{1,0:T(8,128)(2,1)}, bf16[128,1024]{1,0:T(8,128)(2,1)S(1)}, u32[]{:S(2)}, u32[]{:S(2)}) %collective-permute-start.1) | collective-permute-done | bytes 262176 | tf_op jit(solution)/shard_map/ppermute | solution.py:163
  23.7 1.1 pad_maximum_fusion
  24.8 0.6 gather_fusion
  25.4 0.2 select_bitcast_fusion
  25.6 0.7 copy.10
  26.4 0.2 copy.14
  26.7 0.3 copy-done.3
  27.1 0.6 reshape.46.taps_ref
  27.7 0.6 copy.16
  28.4 0.6 copy.15
  29.0 1.1 multiply_exponential_fusion
  30.2 0.2 copy.13
  30.4 1.0 pad_maximum_fusion.1.a_ref
  31.4 70.7 %all-gather.2.cloned.1.call-done = bf16[2048,3,1024]{2,0,1:T(8,128)(2,1)} async-done(((bf16[128,3,1024]{2,0,1:T(8,128)(2,1)}), bf16[2048,3,1024]{2,0,1:T(8,128)(2,1)}) %all-gather.2.cloned.1.call-update) | async-done | bytes 12582928 | tf_op jit(solution)/shard_map/all_gather | solution.py:177
  102.2 13.1 %shard_map.73 = f32[3,256,1024]{2,1,0:T(8,128)} custom-call(bf16[256,2048]{1,0:T(8,128)(2,1)} %pad_maximum_fusion.1.a_ref, bf16[3,2048,1024]{2,1,0:T(8,128)(2,1)} %bitcast.23), custom_call_target="tpu_custom_call" | custom-call | flops 3221225472 | bytes 16777216 | tf_op jit(solution)/shard_map/pallas_call | solution.py:126
  115.2 1.7 %slice.27 = f32[3,128,1024]{2,1,0:T(8,128)S(1)} slice(f32[3,256,1024]{2,1,0:T(8,128)} %shard_map.73), slice={[0:3], [128:256], [0:1024]} | slice | bytes 3145728 | tf_op jit(solution)/shard_map/slice | solution.py:201
  117.0 3.4 %collective-permute-done.4 = f32[3,128,1024]{2,1,0:T(8,128)S(1)} collective-permute-done((f32[3,128,1024]{2,1,0:T(8,128)S(1)}, f32[3,128,1024]{2,1,0:T(8,128)S(1)}, u32[]{:S(2)}, u32[]{:S(2)}) %collective-permute-start.4) | collective-permute-done | bytes 1572896 | tf_op jit(solution)/shard_map/ppermute | solution.py:156
  120.4 0.3 fusion
  120.7 2.0 %collective-permute-start.5 = (bf16[3,2,1024]{2,1,0:T(2,128)(2,1)S(1)}, bf16[3,2,1024]{2,1,0:T(2,128)(2,1)S(1)}, u32[]{:S(2)}, u32[]{:S(2)}) collective-permute-start(bf16[3,2,1024]{2,1,0:T(2,128)(2,1)S(1)} %slice.28), channel_id=1, source_target_pairs={{0,4},{4,8},{8,12},{12,16},{16,20},{20,24},{24,28},{28,32},{32,36}... | collective-permute-start | bytes 36872 | tf_op jit(solution)/shard_map/ppermute | solution.py:152
  122.8 0.8 collective-permute-done.5
  123.6 0.2 pad_maximum_fusion.2
  123.8 1.5 reshape.53.x_ref
  125.3 25.8 %shard_map.74 = f32[128,8,128]{2,1,0:T(8,128)} custom-call(f32[3,130,8,128]{3,2,1,0:T(8,128)} %reshape.53.x_ref, f32[3,3,8,128]{3,2,1,0:T(8,128)} %reshape.46.taps_ref, f32[16,8,128]{2,1,0:T(8,128)} %bitcast.29, f32[16,8,128]{2,1,0:T(8,128)} %bitcast.28, f32[8,128]{1,0:T(8,128)} %bitcast.36, f32[7,16,8,128]{3,2,1,0:T(8,128)} %get-tuple-element.19.lift_ref, ...), custom_call_target="tpu_custom_call" | custom-call | tf_op jit(solution)/shard_map/pallas_call | solution.py:210
  151.2 1.1 convert_element_type.11
  152.2 0.8 copy.20
  (24 shorter events, 0.4 us)
Async XLA Ops:
  6.5 95.6 %all-gather.2.cloned.1.call-start = ((), (), s32[]{:S(2)}) async-start(), calls=%async_computation | async-start | bytes 13369344 | tf_op jit(solution)/shard_map/all_gather | solution.py:177
  7.3 9.7 %collective-permute-start = (bf16[128,1024]{1,0:T(8,128)(2,1)}, bf16[128,1024]{1,0:T(8,128)(2,1)S(1)}, u32[]{:S(2)}, u32[]{:S(2)}) collective-permute-start(bf16[128,1024]{1,0:T(8,128)(2,1)} %param.7), channel_id=1, source_target_pairs={{0,1},{1,2},{2,3},{3,0},{4,5},{5,6},{6,7},{7,4},{8,9},{9,10},{10,1... | collective-permute-start | bytes 786440 | tf_op jit(solution)/shard_map/ppermute | solution.py:163
  9.0 13.1 %collective-permute-start.2 = (bf16[128,1024]{1,0:T(8,128)(2,1)}, bf16[128,1024]{1,0:T(8,128)(2,1)S(1)}, u32[]{:S(2)}, u32[]{:S(2)}) collective-permute-start(bf16[128,1024]{1,0:T(8,128)(2,1)} %param.7), channel_id=1, source_target_pairs={{0,3},{1,0},{2,1},{3,2},{4,7},{5,4},{6,5},{7,6},{8,11},{9,8},{10,9... | collective-permute-start | bytes 786440 | tf_op jit(solution)/shard_map/ppermute | solution.py:163
  10.6 13.2 %collective-permute-start.1 = (bf16[128,1024]{1,0:T(8,128)(2,1)}, bf16[128,1024]{1,0:T(8,128)(2,1)S(1)}, u32[]{:S(2)}, u32[]{:S(2)}) collective-permute-start(bf16[128,1024]{1,0:T(8,128)(2,1)} %param.7), channel_id=1, source_target_pairs={{0,2},{1,3},{2,0},{3,1},{4,6},{5,7},{6,4},{7,5},{8,10},{9,11},{10,... | collective-permute-start | bytes 786440 | tf_op jit(solution)/shard_map/ppermute | solution.py:163
  26.3 0.8 copy-start.3
  26.3 1.4 copy-start.2
  26.3 2.0 %copy-start.1 = (f32[16,1024]{1,0:T(8,128)S(1)}, f32[16,1024]{1,0:T(8,128)}, u32[]{:S(2)}) copy-start(f32[16,1024]{1,0:T(8,128)} %param.10) | copy-start | bytes 196612
  26.3 2.7 %copy-start.4 = (f32[7]{0:T(128)S(1)}, f32[7]{0:T(128)}, u32[]{:S(2)}) copy-start(f32[7]{0:T(128)} %constant.48) | copy-start | bytes 88
  26.3 2.7 %copy-start.5 = (f32[7]{0:T(128)S(1)}, f32[7]{0:T(128)}, u32[]{:S(2)}) copy-start(f32[7]{0:T(128)} %constant.47) | copy-start | bytes 88
  26.6 3.7 %collective-permute-start.3 = (bf16[128,2048]{1,0:T(8,128)(2,1)S(1)}, bf16[128,2048]{1,0:T(8,128)(2,1)S(1)}, u32[]{:S(2)}, u32[]{:S(2)}) collective-permute-start(bf16[128,2048]{1,0:T(8,128)(2,1)S(1)} %copy.14), channel_id=1, source_target_pairs={{0,4},{4,0},{1,5},{5,1},{2,6},{6,2},{3,7},{7,3},{8,12},{12,8},{9,1... | collective-permute-start | bytes 1572872 | tf_op jit(solution)/shard_map/ppermute | solution.py:156
  115.2 5.2 %copy-start = (f32[3,256,1024]{2,1,0:T(8,128)S(1)}, f32[3,256,1024]{2,1,0:T(8,128)}, u32[]{:S(2)}) copy-start(f32[3,256,1024]{2,1,0:T(8,128)} %shard_map.73) | copy-start | bytes 9437188
  116.9 3.5 %collective-permute-start.4 = (f32[3,128,1024]{2,1,0:T(8,128)S(1)}, f32[3,128,1024]{2,1,0:T(8,128)S(1)}, u32[]{:S(2)}, u32[]{:S(2)}) collective-permute-start(f32[3,128,1024]{2,1,0:T(8,128)S(1)} %slice.27), channel_id=1, source_target_pairs={{0,4},{4,0},{1,5},{5,1},{2,6},{6,2},{3,7},{7,3},{8,12},{12,8},{9,1... | collective-permute-start | bytes 4718600 | tf_op jit(solution)/shard_map/ppermute | solution.py:156
  120.7 2.9 %collective-permute-start.5 = (bf16[3,2,1024]{2,1,0:T(2,128)(2,1)S(1)}, bf16[3,2,1024]{2,1,0:T(2,128)(2,1)S(1)}, u32[]{:S(2)}, u32[]{:S(2)}) collective-permute-start(bf16[3,2,1024]{2,1,0:T(2,128)(2,1)S(1)} %slice.28), channel_id=1, source_target_pairs={{0,4},{4,8},{8,12},{12,16},{16,20},{20,24},{24,28},{28,32},{32,36}... | collective-permute-start | bytes 36872 | tf_op jit(solution)/shard_map/ppermute | solution.py:152
Sparse Core Ops, SparseCore 0:
  9.5 92.6 all-gather.1

commit v12 on v9

--- a/solution.py
+++ b/solution.py
@@ -99,9 +99,10 @@
 
 
 def scan_digits(peers):
-    digits = []
+    digits = [2] if peers % 2 == 0 else []
+    peers //= 2 if digits else 1
     while peers > 1:
-        digit = 4 if peers % 4 == 0 and peers != 8 else 2
+        digit = 4 if peers % 4 == 0 else 2
         digits.append(digit)
         peers //= digit
     return digits or [2]

time: 155 us -> 155 us (level)
  no operation moved by 1% of the time
where the time goes in v12:
time: 155 us; the launch traced here: 154 us
  waiting for transfers between devices  85.1 us (55%)
  Pallas kernels  25 us (16%)
  between operations  13.6 us (9%)
  matrix products  11.7 us (8%)
  starting transfers between devices  7.59 us (5%)
  local copies, waits for them, and re-layouts  5.79 us (4%)
  other arithmetic  5.17 us (3%)
    all_gather x1, waiting for transfers between devices, per_device(): piece = lax.all_gather(in_weight, 'cx', axis=0, tiled=True)  72.4 us
    pallas_call x1, Pallas kernels, per_device(): pl.pallas_call(functools.partial(block_kernel, peers, digits), out_shape=...  25 us
    ppermute x3, waiting for transfers between devices, gathered_tp(): lax.ppermute(tokens, 'tp', [(i, (i + by) % peers) for i in range(peers)])  10.3 us
    dot_general x3, matrix products, per_device(): jnp.dot(both[rows:], piece[:, g, :], preferred_element_type=jnp.float32)  9.45 us
    ppermute x3, starting transfers between devices, gathered_tp(): lax.ppermute(tokens, 'tp', [(i, (i + by) % peers) for i in range(peers)])  5.37 us
  transfers between devices with their start and end apart: 7, of which 6 were waited for; matrix products, arithmetic and copies ran while one was open for 6% of the time, Pallas kernels for 0%

profile of v12, /device:TPU:0, one launch (start us, length us, event | category | flops | bytes accessed | tf_op | source)
XLA Modules:
  0.0 153.9 jit_solution(17824172713702879971)
XLA Ops:
  6.5 0.7 all-gather.2.cloned.1.call-update
  7.3 1.7 %collective-permute-start = (bf16[128,1024]{1,0:T(8,128)(2,1)}, bf16[128,1024]{1,0:T(8,128)(2,1)S(1)}, u32[]{:S(2)}, u32[]{:S(2)}) collective-permute-start(bf16[128,1024]{1,0:T(8,128)(2,1)} %param.7), channel_id=1, source_target_pairs={{0,1},{1,2},{2,3},{3,0},{4,5},{5,6},{6,7},{7,4},{8,9},{9,10},{10,1... | collective-permute-start | bytes 786440 | tf_op jit(solution)/shard_map/ppermute | solution.py:131
  9.0 1.6 %collective-permute-start.2 = (bf16[128,1024]{1,0:T(8,128)(2,1)}, bf16[128,1024]{1,0:T(8,128)(2,1)S(1)}, u32[]{:S(2)}, u32[]{:S(2)}) collective-permute-start(bf16[128,1024]{1,0:T(8,128)(2,1)} %param.7), channel_id=1, source_target_pairs={{0,3},{1,0},{2,1},{3,2},{4,7},{5,4},{6,5},{7,6},{8,11},{9,8},{10,9... | collective-permute-start | bytes 786440 | tf_op jit(solution)/shard_map/ppermute | solution.py:131
  10.6 2.1 %collective-permute-start.1 = (bf16[128,1024]{1,0:T(8,128)(2,1)}, bf16[128,1024]{1,0:T(8,128)(2,1)S(1)}, u32[]{:S(2)}, u32[]{:S(2)}) collective-permute-start(bf16[128,1024]{1,0:T(8,128)(2,1)} %param.7), channel_id=1, source_target_pairs={{0,2},{1,3},{2,0},{3,1},{4,6},{5,7},{6,4},{7,5},{8,10},{9,11},{10,... | collective-permute-start | bytes 786440 | tf_op jit(solution)/shard_map/ppermute | solution.py:131
  12.6 0.7 sort.17
  13.4 3.5 %collective-permute-done = bf16[128,1024]{1,0:T(8,128)(2,1)S(1)} collective-permute-done((bf16[128,1024]{1,0:T(8,128)(2,1)}, bf16[128,1024]{1,0:T(8,128)(2,1)S(1)}, u32[]{:S(2)}, u32[]{:S(2)}) %collective-permute-start) | collective-permute-done | bytes 262176 | tf_op jit(solution)/shard_map/ppermute | solution.py:131
  16.9 5.1 %collective-permute-done.2 = bf16[128,1024]{1,0:T(8,128)(2,1)S(1)} collective-permute-done((bf16[128,1024]{1,0:T(8,128)(2,1)}, bf16[128,1024]{1,0:T(8,128)(2,1)S(1)}, u32[]{:S(2)}, u32[]{:S(2)}) %collective-permute-start.2) | collective-permute-done | bytes 262176 | tf_op jit(solution)/shard_map/ppermute | solution.py:131
  22.0 1.7 %collective-permute-done.1 = bf16[128,1024]{1,0:T(8,128)(2,1)S(1)} collective-permute-done((bf16[128,1024]{1,0:T(8,128)(2,1)}, bf16[128,1024]{1,0:T(8,128)(2,1)S(1)}, u32[]{:S(2)}, u32[]{:S(2)}) %collective-permute-start.1) | collective-permute-done | bytes 262176 | tf_op jit(solution)/shard_map/ppermute | solution.py:131
  23.7 1.1 pad_maximum_fusion.1
  24.9 0.6 gather_fusion
  25.7 0.7 copy.8
  26.5 0.6 reshape.46.taps_ref
  27.2 0.6 copy.10
  27.8 0.6 copy.9
  28.5 1.1 multiply_exponential_fusion
  29.8 72.4 %all-gather.2.cloned.1.call-done = bf16[2048,3,1024]{2,0,1:T(8,128)(2,1)} async-done(((bf16[128,3,1024]{2,0,1:T(8,128)(2,1)}), bf16[2048,3,1024]{2,0,1:T(8,128)(2,1)}) %all-gather.2.cloned.1.call-update) | async-done | bytes 12582928 | tf_op jit(solution)/shard_map/all_gather | solution.py:145
  102.2 2.9 %fusion.10 = f32[1,128,1024]{2,1,0:T(8,128)S(1)} fusion(bf16[2048,3,1024]{2,0,1:T(8,128)(2,1)} %all-gather.2.cloned.1.call-done, bf16[256,2048]{0,1:T(8,128)(2,1)S(1)} %pad_maximum_fusion.2), kind=kOutput, calls=%fused_computation.16 | convolution fusion | flops 536870912 | bytes 5242880 | tf_op jit(solution)/shard_map/dot_general | solution.py:169
  105.1 3.1 %fusion.8 = f32[1,128,1024]{2,1,0:T(8,128)S(1)} fusion(bf16[2048,3,1024]{2,0,1:T(8,128)(2,1)} %all-gather.2.cloned.1.call-done, bf16[256,2048]{0,1:T(8,128)(2,1)S(1)} %pad_maximum_fusion.2), kind=kOutput, calls=%fused_computation.14 | convolution fusion | flops 536870912 | bytes 5242880 | tf_op jit(solution)/shard_map/dot_general | solution.py:169
  108.2 3.5 %fusion.12 = f32[1,128,1024]{2,1,0:T(8,128)S(1)} fusion(bf16[2048,3,1024]{2,0,1:T(8,128)(2,1)} %all-gather.2.cloned.1.call-done, bf16[256,2048]{0,1:T(8,128)(2,1)S(1)} %pad_maximum_fusion.2), kind=kOutput, calls=%fused_computation.18 | convolution fusion | flops 536870912 | bytes 5242880 | tf_op jit(solution)/shard_map/dot_general | solution.py:169
  111.9 0.3 copy-done.5
  112.2 0.7 fusion.9
  112.9 0.8 fusion.7
  113.7 0.8 fusion.11
  114.5 0.8 collective-permute-done.4
  115.3 0.3 fusion.6
  115.7 2.0 %collective-permute-start.5 = (bf16[3,2,1024]{2,1,0:T(2,128)(2,1)S(1)}, bf16[3,2,1024]{2,1,0:T(2,128)(2,1)S(1)}, u32[]{:S(2)}, u32[]{:S(2)}) collective-permute-start(bf16[3,2,1024]{2,1,0:T(2,128)(2,1)S(1)} %slice.48), channel_id=1, source_target_pairs={{0,4},{4,8},{8,12},{12,16},{16,20},{20,24},{24,28},{28,32},{32,36}... | collective-permute-start | bytes 36872 | tf_op jit(solution)/shard_map/ppermute | solution.py:120
  117.7 0.8 collective-permute-done.5
  118.5 0.2 pad_maximum_fusion.3
  118.8 1.5 reshape.53.x_ref
  120.3 25.0 %shard_map.73 = f32[128,8,128]{2,1,0:T(8,128)} custom-call(f32[3,130,8,128]{3,2,1,0:T(8,128)} %reshape.53.x_ref, f32[3,3,8,128]{3,2,1,0:T(8,128)} %reshape.46.taps_ref, f32[16,8,128]{2,1,0:T(8,128)} %bitcast.63, f32[16,8,128]{2,1,0:T(8,128)} %bitcast.62, f32[8,128]{1,0:T(8,128)} %bitcast.70, f32[7,16,8,128]{3,2,1,0:T(8,128)} %get-tuple-element.19.lift_ref, ...), custom_call_target="tpu_custom_call" | custom-call | tf_op jit(solution)/shard_map/pallas_call | solution.py:184
  145.3 1.1 convert_element_type.11
  146.3 0.8 copy.14
  (27 shorter events, 0.8 us)
Async XLA Ops:
  6.5 95.6 %all-gather.2.cloned.1.call-start = ((), (), s32[]{:S(2)}) async-start(), calls=%async_computation | async-start | bytes 13369344 | tf_op jit(solution)/shard_map/all_gather | solution.py:145
  7.3 9.7 %collective-permute-start = (bf16[128,1024]{1,0:T(8,128)(2,1)}, bf16[128,1024]{1,0:T(8,128)(2,1)S(1)}, u32[]{:S(2)}, u32[]{:S(2)}) collective-permute-start(bf16[128,1024]{1,0:T(8,128)(2,1)} %param.7), channel_id=1, source_target_pairs={{0,1},{1,2},{2,3},{3,0},{4,5},{5,6},{6,7},{7,4},{8,9},{9,10},{10,1... | collective-permute-start | bytes 786440 | tf_op jit(solution)/shard_map/ppermute | solution.py:131
  9.0 13.1 %collective-permute-start.2 = (bf16[128,1024]{1,0:T(8,128)(2,1)}, bf16[128,1024]{1,0:T(8,128)(2,1)S(1)}, u32[]{:S(2)}, u32[]{:S(2)}) collective-permute-start(bf16[128,1024]{1,0:T(8,128)(2,1)} %param.7), channel_id=1, source_target_pairs={{0,3},{1,0},{2,1},{3,2},{4,7},{5,4},{6,5},{7,6},{8,11},{9,8},{10,9... | collective-permute-start | bytes 786440 | tf_op jit(solution)/shard_map/ppermute | solution.py:131
  10.6 13.2 %collective-permute-start.1 = (bf16[128,1024]{1,0:T(8,128)(2,1)}, bf16[128,1024]{1,0:T(8,128)(2,1)S(1)}, u32[]{:S(2)}, u32[]{:S(2)}) collective-permute-start(bf16[128,1024]{1,0:T(8,128)(2,1)} %param.7), channel_id=1, source_target_pairs={{0,2},{1,3},{2,0},{3,1},{4,6},{5,7},{6,4},{7,5},{8,10},{9,11},{10,... | collective-permute-start | bytes 786440 | tf_op jit(solution)/shard_map/ppermute | solution.py:131
  24.8 1.7 %copy-start.2 = (f32[3,3,1024]{2,1,0:T(4,128)S(1)}, f32[3,3,1024]{2,1,0:T(4,128)}, u32[]{:S(2)}) copy-start(f32[3,3,1024]{2,1,0:T(4,128)} %param.9) | copy-start | bytes 110596
  24.8 2.3 %copy-start.1 = (f32[16,1024]{1,0:T(8,128)S(1)}, f32[16,1024]{1,0:T(8,128)}, u32[]{:S(2)}) copy-start(f32[16,1024]{1,0:T(8,128)} %param.11) | copy-start | bytes 196612
  24.8 3.0 %copy-start = (f32[16,1024]{1,0:T(8,128)S(1)}, f32[16,1024]{1,0:T(8,128)}, u32[]{:S(2)}) copy-start(f32[16,1024]{1,0:T(8,128)} %param.10) | copy-start | bytes 196612
  24.9 3.6 %copy-start.3 = (f32[7]{0:T(128)S(1)}, f32[7]{0:T(128)}, u32[]{:S(2)}) copy-start(f32[7]{0:T(128)} %constant.48) | copy-start | bytes 88
  24.9 3.6 %copy-start.4 = (f32[7]{0:T(128)S(1)}, f32[7]{0:T(128)}, u32[]{:S(2)}) copy-start(f32[7]{0:T(128)} %constant.47) | copy-start | bytes 88
  26.4 3.2 %collective-permute-start.3 = (bf16[128,2048]{0,1:T(8,128)(2,1)S(1)}, bf16[128,2048]{0,1:T(8,128)(2,1)S(1)}, u32[]{:S(2)}, u32[]{:S(2)}) collective-permute-start(bf16[128,2048]{0,1:T(8,128)(2,1)S(1)} %bitcast.61), channel_id=1, source_target_pairs={{0,4},{4,0},{1,5},{5,1},{2,6},{6,2},{3,7},{7,3},{8,12},{12,8},{9,1... | collective-permute-start | bytes 1572872 | tf_op jit(solution)/shard_map/ppermute | solution.py:124
  105.1 7.1 %copy-start.5 = (bf16[2048,3,1024]{2,0,1:T(8,128)(2,1)S(1)}, bf16[2048,3,1024]{2,0,1:T(8,128)(2,1)}, u32[]{:S(2)}) copy-start(bf16[2048,3,1024]{2,0,1:T(8,128)(2,1)} %all-gather.2.cloned.1.call-done) | copy-start | bytes 37748740
  111.8 3.5 %collective-permute-start.4 = (f32[3,128,1024]{2,1,0:T(8,128)S(1)}, f32[3,128,1024]{2,1,0:T(8,128)S(1)}, u32[]{:S(2)}, u32[]{:S(2)}) collective-permute-start(f32[3,128,1024]{2,1,0:T(8,128)S(1)} %pad_maximum_fusion), channel_id=1, source_target_pairs={{0,4},{4,0},{1,5},{5,1},{2,6},{6,2},{3,7},{7,3},{8,12},{12,8},{9,1... | collective-permute-start | bytes 4718600 | tf_op jit(solution)/shard_map/ppermute | solution.py:124
  115.7 2.9 %collective-permute-start.5 = (bf16[3,2,1024]{2,1,0:T(2,128)(2,1)S(1)}, bf16[3,2,1024]{2,1,0:T(2,128)(2,1)S(1)}, u32[]{:S(2)}, u32[]{:S(2)}) collective-permute-start(bf16[3,2,1024]{2,1,0:T(2,128)(2,1)S(1)} %slice.48), channel_id=1, source_target_pairs={{0,4},{4,8},{8,12},{12,16},{16,20},{20,24},{24,28},{28,32},{32,36}... | collective-permute-start | bytes 36872 | tf_op jit(solution)/shard_map/ppermute | solution.py:120
Sparse Core Ops, SparseCore 0:
  9.5 92.6 all-gather.1

commit v13 on v12

--- a/solution.py
+++ b/solution.py
@@ -177,9 +177,8 @@
     sums = mine_part + arrived
     projected = sums.astype(jnp.bfloat16)
     edge_out = shifted(projected[:, rows - 2 :, :], ctx, 1)
-    extended = jnp.concatenate([edge_out, projected], axis=1)
-    values = lax.optimization_barrier(extended).astype(jnp.float32)
-    x = values.reshape(3, rows + 2, subl, LANES)
+    extended = jnp.concatenate([edge_out, projected], axis=1).reshape(3, rows + 2, subl, LANES)
+    x = lax.optimization_barrier(extended).astype(jnp.float32)
     state_shape = (poles, subl, LANES)
     out = pl.pallas_call(
         functools.partial(block_kernel, peers, digits),

time: 155 us -> 155 us (level)
  no operation moved by 1% of the time
where the time goes in v13:
time: 155 us; the launch traced here: 154 us
  waiting for transfers between devices  85.1 us (55%)
  Pallas kernels  25 us (16%)
  between operations  13.6 us (9%)
  matrix products  11.7 us (8%)
  starting transfers between devices  7.59 us (5%)
  other arithmetic  6.45 us (4%)
  local copies, waits for them, and re-layouts  4.64 us (3%)
    all_gather x1, waiting for transfers between devices, per_device(): piece = lax.all_gather(in_weight, 'cx', axis=0, tiled=True)  72.4 us
    pallas_call x1, Pallas kernels, per_device(): pl.pallas_call(functools.partial(block_kernel, peers, digits), out_shape=...  25 us
    ppermute x3, waiting for transfers between devices, gathered_tp(): lax.ppermute(tokens, 'tp', [(i, (i + by) % peers) for i in range(peers)])  10.3 us
    dot_general x3, matrix products, per_device(): jnp.dot(both[rows:], piece[:, g, :], preferred_element_type=jnp.float32)  9.45 us
    ppermute x3, starting transfers between devices, gathered_tp(): lax.ppermute(tokens, 'tp', [(i, (i + by) % peers) for i in range(peers)])  5.37 us
  transfers between devices with their start and end apart: 7, of which 6 were waited for; matrix products, arithmetic and copies ran while one was open for 6% of the time, Pallas kernels for 0%

profile of v13, /device:TPU:0, one launch (start us, length us, event | category | flops | bytes accessed | tf_op | source)
XLA Modules:
  0.0 154.1 jit_solution(8234727470497772494)
XLA Ops:
  6.5 0.7 all-gather.2.cloned.1.call-update
  7.3 1.7 %collective-permute-start = (bf16[128,1024]{1,0:T(8,128)(2,1)}, bf16[128,1024]{1,0:T(8,128)(2,1)S(1)}, u32[]{:S(2)}, u32[]{:S(2)}) collective-permute-start(bf16[128,1024]{1,0:T(8,128)(2,1)} %param.7), channel_id=1, source_target_pairs={{0,1},{1,2},{2,3},{3,0},{4,5},{5,6},{6,7},{7,4},{8,9},{9,10},{10,1... | collective-permute-start | bytes 786440 | tf_op jit(solution)/shard_map/ppermute | solution.py:131
  9.0 1.6 %collective-permute-start.2 = (bf16[128,1024]{1,0:T(8,128)(2,1)}, bf16[128,1024]{1,0:T(8,128)(2,1)S(1)}, u32[]{:S(2)}, u32[]{:S(2)}) collective-permute-start(bf16[128,1024]{1,0:T(8,128)(2,1)} %param.7), channel_id=1, source_target_pairs={{0,3},{1,0},{2,1},{3,2},{4,7},{5,4},{6,5},{7,6},{8,11},{9,8},{10,9... | collective-permute-start | bytes 786440 | tf_op jit(solution)/shard_map/ppermute | solution.py:131
  10.6 2.1 %collective-permute-start.1 = (bf16[128,1024]{1,0:T(8,128)(2,1)}, bf16[128,1024]{1,0:T(8,128)(2,1)S(1)}, u32[]{:S(2)}, u32[]{:S(2)}) collective-permute-start(bf16[128,1024]{1,0:T(8,128)(2,1)} %param.7), channel_id=1, source_target_pairs={{0,2},{1,3},{2,0},{3,1},{4,6},{5,7},{6,4},{7,5},{8,10},{9,11},{10,... | collective-permute-start | bytes 786440 | tf_op jit(solution)/shard_map/ppermute | solution.py:131
  12.6 0.7 sort.17
  13.4 3.5 %collective-permute-done = bf16[128,1024]{1,0:T(8,128)(2,1)S(1)} collective-permute-done((bf16[128,1024]{1,0:T(8,128)(2,1)}, bf16[128,1024]{1,0:T(8,128)(2,1)S(1)}, u32[]{:S(2)}, u32[]{:S(2)}) %collective-permute-start) | collective-permute-done | bytes 262176 | tf_op jit(solution)/shard_map/ppermute | solution.py:131
  16.9 5.1 %collective-permute-done.2 = bf16[128,1024]{1,0:T(8,128)(2,1)S(1)} collective-permute-done((bf16[128,1024]{1,0:T(8,128)(2,1)}, bf16[128,1024]{1,0:T(8,128)(2,1)S(1)}, u32[]{:S(2)}, u32[]{:S(2)}) %collective-permute-start.2) | collective-permute-done | bytes 262176 | tf_op jit(solution)/shard_map/ppermute | solution.py:131
  22.0 1.7 %collective-permute-done.1 = bf16[128,1024]{1,0:T(8,128)(2,1)S(1)} collective-permute-done((bf16[128,1024]{1,0:T(8,128)(2,1)}, bf16[128,1024]{1,0:T(8,128)(2,1)S(1)}, u32[]{:S(2)}, u32[]{:S(2)}) %collective-permute-start.1) | collective-permute-done | bytes 262176 | tf_op jit(solution)/shard_map/ppermute | solution.py:131
  23.7 1.1 pad_maximum_fusion.1
  24.9 0.6 gather_fusion
  25.7 0.7 copy.8
  26.5 0.6 reshape.44.taps_ref
  27.2 0.6 copy.10
  27.8 0.6 copy.9
  28.5 1.1 multiply_exponential_fusion
  29.8 72.4 %all-gather.2.cloned.1.call-done = bf16[2048,3,1024]{2,0,1:T(8,128)(2,1)} async-done(((bf16[128,3,1024]{2,0,1:T(8,128)(2,1)}), bf16[2048,3,1024]{2,0,1:T(8,128)(2,1)}) %all-gather.2.cloned.1.call-update) | async-done | bytes 12582928 | tf_op jit(solution)/shard_map/all_gather | solution.py:145
  102.2 2.9 %fusion.10 = f32[1,128,1024]{2,1,0:T(8,128)S(1)} fusion(bf16[2048,3,1024]{2,0,1:T(8,128)(2,1)} %all-gather.2.cloned.1.call-done, bf16[256,2048]{0,1:T(8,128)(2,1)S(1)} %pad_maximum_fusion.2), kind=kOutput, calls=%fused_computation.16 | convolution fusion | flops 536870912 | bytes 5242880 | tf_op jit(solution)/shard_map/dot_general | solution.py:169
  105.1 3.1 %fusion.8 = f32[1,128,1024]{2,1,0:T(8,128)S(1)} fusion(bf16[2048,3,1024]{2,0,1:T(8,128)(2,1)} %all-gather.2.cloned.1.call-done, bf16[256,2048]{0,1:T(8,128)(2,1)S(1)} %pad_maximum_fusion.2), kind=kOutput, calls=%fused_computation.14 | convolution fusion | flops 536870912 | bytes 5242880 | tf_op jit(solution)/shard_map/dot_general | solution.py:169
  108.2 3.5 %fusion.12 = f32[1,128,1024]{2,1,0:T(8,128)S(1)} fusion(bf16[2048,3,1024]{2,0,1:T(8,128)(2,1)} %all-gather.2.cloned.1.call-done, bf16[256,2048]{0,1:T(8,128)(2,1)S(1)} %pad_maximum_fusion.2), kind=kOutput, calls=%fused_computation.18 | convolution fusion | flops 536870912 | bytes 5242880 | tf_op jit(solution)/shard_map/dot_general | solution.py:169
  111.9 0.3 copy-done.5
  112.2 0.7 fusion.9
  112.9 0.8 fusion.7
  113.7 0.8 fusion.11
  114.5 0.8 collective-permute-done.4
  115.3 0.3 fusion.6
  115.7 2.0 %collective-permute-start.5 = (bf16[3,2,1024]{2,1,0:T(2,128)(2,1)S(1)}, bf16[3,2,1024]{2,1,0:T(2,128)(2,1)S(1)}, u32[]{:S(2)}, u32[]{:S(2)}) collective-permute-start(bf16[3,2,1024]{2,1,0:T(2,128)(2,1)S(1)} %slice.48), channel_id=1, source_target_pairs={{0,4},{4,8},{8,12},{12,16},{16,20},{20,24},{24,28},{28,32},{32,36}... | collective-permute-start | bytes 36872 | tf_op jit(solution)/shard_map/ppermute | solution.py:120
  117.7 0.8 collective-permute-done.5
  118.8 0.4 reshape.48
  119.1 1.3 convert_element_type.13.x_ref
  120.4 25.0 %shard_map.73 = f32[128,8,128]{2,1,0:T(8,128)} custom-call(f32[3,130,8,128]{3,2,1,0:T(8,128)} %convert_element_type.13.x_ref, f32[3,3,8,128]{3,2,1,0:T(8,128)} %reshape.44.taps_ref, f32[16,8,128]{2,1,0:T(8,128)} %bitcast.63, f32[16,8,128]{2,1,0:T(8,128)} %bitcast.62, f32[8,128]{1,0:T(8,128)} %bitcast.70, f32[7,16,8,128]{3,2,1,0:T(8,128)} %get-tuple-element.19.lift_ref, ...), custom_call_target="tpu_custom_call" | custom-call | tf_op jit(solution)/shard_map/pallas_call | solution.py:183
  145.4 1.1 convert_element_type.14
  146.5 0.8 copy.14
  (28 shorter events, 1.0 us)
Async XLA Ops:
  6.5 95.6 %all-gather.2.cloned.1.call-start = ((), (), s32[]{:S(2)}) async-start(), calls=%async_computation | async-start | bytes 13369344 | tf_op jit(solution)/shard_map/all_gather | solution.py:145
  7.3 9.7 %collective-permute-start = (bf16[128,1024]{1,0:T(8,128)(2,1)}, bf16[128,1024]{1,0:T(8,128)(2,1)S(1)}, u32[]{:S(2)}, u32[]{:S(2)}) collective-permute-start(bf16[128,1024]{1,0:T(8,128)(2,1)} %param.7), channel_id=1, source_target_pairs={{0,1},{1,2},{2,3},{3,0},{4,5},{5,6},{6,7},{7,4},{8,9},{9,10},{10,1... | collective-permute-start | bytes 786440 | tf_op jit(solution)/shard_map/ppermute | solution.py:131
  9.0 13.1 %collective-permute-start.2 = (bf16[128,1024]{1,0:T(8,128)(2,1)}, bf16[128,1024]{1,0:T(8,128)(2,1)S(1)}, u32[]{:S(2)}, u32[]{:S(2)}) collective-permute-start(bf16[128,1024]{1,0:T(8,128)(2,1)} %param.7), channel_id=1, source_target_pairs={{0,3},{1,0},{2,1},{3,2},{4,7},{5,4},{6,5},{7,6},{8,11},{9,8},{10,9... | collective-permute-start | bytes 786440 | tf_op jit(solution)/shard_map/ppermute | solution.py:131
  10.6 13.2 %collective-permute-start.1 = (bf16[128,1024]{1,0:T(8,128)(2,1)}, bf16[128,1024]{1,0:T(8,128)(2,1)S(1)}, u32[]{:S(2)}, u32[]{:S(2)}) collective-permute-start(bf16[128,1024]{1,0:T(8,128)(2,1)} %param.7), channel_id=1, source_target_pairs={{0,2},{1,3},{2,0},{3,1},{4,6},{5,7},{6,4},{7,5},{8,10},{9,11},{10,... | collective-permute-start | bytes 786440 | tf_op jit(solution)/shard_map/ppermute | solution.py:131
  24.8 1.7 %copy-start.2 = (f32[3,3,1024]{2,1,0:T(4,128)S(1)}, f32[3,3,1024]{2,1,0:T(4,128)}, u32[]{:S(2)}) copy-start(f32[3,3,1024]{2,1,0:T(4,128)} %param.9) | copy-start | bytes 110596
  24.8 2.3 %copy-start.1 = (f32[16,1024]{1,0:T(8,128)S(1)}, f32[16,1024]{1,0:T(8,128)}, u32[]{:S(2)}) copy-start(f32[16,1024]{1,0:T(8,128)} %param.11) | copy-start | bytes 196612
  24.8 3.0 %copy-start = (f32[16,1024]{1,0:T(8,128)S(1)}, f32[16,1024]{1,0:T(8,128)}, u32[]{:S(2)}) copy-start(f32[16,1024]{1,0:T(8,128)} %param.10) | copy-start | bytes 196612
  24.9 3.6 %copy-start.3 = (f32[7]{0:T(128)S(1)}, f32[7]{0:T(128)}, u32[]{:S(2)}) copy-start(f32[7]{0:T(128)} %constant.48) | copy-start | bytes 88
  24.9 3.6 %copy-start.4 = (f32[7]{0:T(128)S(1)}, f32[7]{0:T(128)}, u32[]{:S(2)}) copy-start(f32[7]{0:T(128)} %constant.47) | copy-start | bytes 88
  26.4 3.2 %collective-permute-start.3 = (bf16[128,2048]{0,1:T(8,128)(2,1)S(1)}, bf16[128,2048]{0,1:T(8,128)(2,1)S(1)}, u32[]{:S(2)}, u32[]{:S(2)}) collective-permute-start(bf16[128,2048]{0,1:T(8,128)(2,1)S(1)} %bitcast.61), channel_id=1, source_target_pairs={{0,4},{4,0},{1,5},{5,1},{2,6},{6,2},{3,7},{7,3},{8,12},{12,8},{9,1... | collective-permute-start | bytes 1572872 | tf_op jit(solution)/shard_map/ppermute | solution.py:124
  105.1 7.1 %copy-start.5 = (bf16[2048,3,1024]{2,0,1:T(8,128)(2,1)S(1)}, bf16[2048,3,1024]{2,0,1:T(8,128)(2,1)}, u32[]{:S(2)}) copy-start(bf16[2048,3,1024]{2,0,1:T(8,128)(2,1)} %all-gather.2.cloned.1.call-done) | copy-start | bytes 37748740
  111.8 3.5 %collective-permute-start.4 = (f32[3,128,1024]{2,1,0:T(8,128)S(1)}, f32[3,128,1024]{2,1,0:T(8,128)S(1)}, u32[]{:S(2)}, u32[]{:S(2)}) collective-permute-start(f32[3,128,1024]{2,1,0:T(8,128)S(1)} %pad_maximum_fusion), channel_id=1, source_target_pairs={{0,4},{4,0},{1,5},{5,1},{2,6},{6,2},{3,7},{7,3},{8,12},{12,8},{9,1... | collective-permute-start | bytes 4718600 | tf_op jit(solution)/shard_map/ppermute | solution.py:124
  115.7 2.9 %collective-permute-start.5 = (bf16[3,2,1024]{2,1,0:T(2,128)(2,1)S(1)}, bf16[3,2,1024]{2,1,0:T(2,128)(2,1)S(1)}, u32[]{:S(2)}, u32[]{:S(2)}) collective-permute-start(bf16[3,2,1024]{2,1,0:T(2,128)(2,1)S(1)} %slice.48), channel_id=1, source_target_pairs={{0,4},{4,8},{8,12},{12,16},{16,20},{20,24},{24,28},{28,32},{32,36}... | collective-permute-start | bytes 36872 | tf_op jit(solution)/shard_map/ppermute | solution.py:120
Sparse Core Ops, SparseCore 0:
  9.5 92.6 all-gather.1

commit v14 on v13

--- a/solution.py
+++ b/solution.py
@@ -14,9 +14,9 @@
 
 def filtered_at(x_ref, taps_ref, g, t):
     return (
-        taps_ref[0, g] * x_ref[g, t + 2]
-        + taps_ref[1, g] * x_ref[g, t + 1]
-        + taps_ref[2, g] * x_ref[g, t]
+        taps_ref[0, g] * x_ref[g, t + 2].astype(jnp.float32)
+        + taps_ref[1, g] * x_ref[g, t + 1].astype(jnp.float32)
+        + taps_ref[2, g] * x_ref[g, t].astype(jnp.float32)
     )
 
 
@@ -40,7 +40,7 @@
         gated = filtered_at(x_ref, taps_ref, 1, t) * filtered_at(x_ref, taps_ref, 2, t)
         state = decay_ref[...] * state + gated[None]
         convolved = jnp.sum(resid_ref[...] * state, axis=0)
-        out_ref[t] = query * (convolved + skip_ref[...] * gated)
+        out_ref[t] = (query * (convolved + skip_ref[...] * gated)).astype(out_ref.dtype)
         return state
 
     lax.fori_loop(0, rows, step, start_ref[...], unroll=8)
@@ -178,11 +178,11 @@
     projected = sums.astype(jnp.bfloat16)
     edge_out = shifted(projected[:, rows - 2 :, :], ctx, 1)
     extended = jnp.concatenate([edge_out, projected], axis=1).reshape(3, rows + 2, subl, LANES)
-    x = lax.optimization_barrier(extended).astype(jnp.float32)
+    x = lax.optimization_barrier(extended)
     state_shape = (poles, subl, LANES)
     out = pl.pallas_call(
         functools.partial(block_kernel, peers, digits),
-        out_shape=jax.ShapeDtypeStruct((rows, subl, LANES), jnp.float32),
+        out_shape=jax.ShapeDtypeStruct((rows, subl, LANES), jnp.bfloat16),
         in_specs=vmem_specs(7),
         out_specs=pl.BlockSpec(memory_space=pltpu.VMEM),
         scratch_shapes=[
@@ -195,7 +195,7 @@
         ],
         compiler_params=pltpu.CompilerParams(collective_id=0, has_side_effects=True),
     )(x, taps, decay, resid, direct, lift, keep)
-    return out.reshape(rows, chans).astype(jnp.bfloat16)
+    return out.reshape(rows, chans)
 
 
 def solution(mesh):

time: 155 us -> 154 us (level)
  other arithmetic: 6.45 us -> 4.1 us
  local copies, waits for them, and re-layouts: 4.64 us -> 6.49 us
    convert_element_type x2 -> x0, other arithmetic: 2.35 us -> none  [the longest x1 1.28 us: per_device(): x = lax.optimization_barrier(extended).astype(jnp.float32)]
where the time goes in v14:
time: 154 us; the launch traced here: 153 us
  waiting for transfers between devices  85.1 us (55%)
  Pallas kernels  24.8 us (16%)
  between operations  13.6 us (9%)
  matrix products  11.7 us (8%)
  starting transfers between devices  7.59 us (5%)
  local copies, waits for them, and re-layouts  6.49 us (4%)
  other arithmetic  4.1 us (3%)
    all_gather x1, waiting for transfers between devices, per_device(): piece = lax.all_gather(in_weight, 'cx', axis=0, tiled=True)  72.4 us
    pallas_call x1, Pallas kernels, per_device(): pl.pallas_call(functools.partial(block_kernel, peers, digits), out_shape=...  24.8 us
    ppermute x3, waiting for transfers between devices, gathered_tp(): lax.ppermute(tokens, 'tp', [(i, (i + by) % peers) for i in range(peers)])  10.3 us
    dot_general x3, matrix products, per_device(): jnp.dot(both[rows:], piece[:, g, :], preferred_element_type=jnp.float32)  9.45 us
    ppermute x3, starting transfers between devices, gathered_tp(): lax.ppermute(tokens, 'tp', [(i, (i + by) % peers) for i in range(peers)])  5.37 us
    unnamed x16, local copies, waits for them, and re-layouts  3.31 us
  transfers between devices with their start and end apart: 7, of which 6 were waited for; matrix products, arithmetic and copies ran while one was open for 6% of the time, Pallas kernels for 0%

profile of v14, /device:TPU:0, one launch (start us, length us, event | category | flops | bytes accessed | tf_op | source)
XLA Modules:
  0.0 153.4 jit_solution(15474978514730084086)
XLA Ops:
  6.5 0.7 all-gather.2.cloned.1.call-update
  7.3 1.7 %collective-permute-start = (bf16[128,1024]{1,0:T(8,128)(2,1)}, bf16[128,1024]{1,0:T(8,128)(2,1)S(1)}, u32[]{:S(2)}, u32[]{:S(2)}) collective-permute-start(bf16[128,1024]{1,0:T(8,128)(2,1)} %param.7), channel_id=1, source_target_pairs={{0,1},{1,2},{2,3},{3,0},{4,5},{5,6},{6,7},{7,4},{8,9},{9,10},{10,1... | collective-permute-start | bytes 786440 | tf_op jit(solution)/shard_map/ppermute | solution.py:131
  9.0 1.6 %collective-permute-start.2 = (bf16[128,1024]{1,0:T(8,128)(2,1)}, bf16[128,1024]{1,0:T(8,128)(2,1)S(1)}, u32[]{:S(2)}, u32[]{:S(2)}) collective-permute-start(bf16[128,1024]{1,0:T(8,128)(2,1)} %param.7), channel_id=1, source_target_pairs={{0,3},{1,0},{2,1},{3,2},{4,7},{5,4},{6,5},{7,6},{8,11},{9,8},{10,9... | collective-permute-start | bytes 786440 | tf_op jit(solution)/shard_map/ppermute | solution.py:131
  10.6 2.1 %collective-permute-start.1 = (bf16[128,1024]{1,0:T(8,128)(2,1)}, bf16[128,1024]{1,0:T(8,128)(2,1)S(1)}, u32[]{:S(2)}, u32[]{:S(2)}) collective-permute-start(bf16[128,1024]{1,0:T(8,128)(2,1)} %param.7), channel_id=1, source_target_pairs={{0,2},{1,3},{2,0},{3,1},{4,6},{5,7},{6,4},{7,5},{8,10},{9,11},{10,... | collective-permute-start | bytes 786440 | tf_op jit(solution)/shard_map/ppermute | solution.py:131
  12.6 0.7 sort.17
  13.4 3.5 %collective-permute-done = bf16[128,1024]{1,0:T(8,128)(2,1)S(1)} collective-permute-done((bf16[128,1024]{1,0:T(8,128)(2,1)}, bf16[128,1024]{1,0:T(8,128)(2,1)S(1)}, u32[]{:S(2)}, u32[]{:S(2)}) %collective-permute-start) | collective-permute-done | bytes 262176 | tf_op jit(solution)/shard_map/ppermute | solution.py:131
  16.9 5.1 %collective-permute-done.2 = bf16[128,1024]{1,0:T(8,128)(2,1)S(1)} collective-permute-done((bf16[128,1024]{1,0:T(8,128)(2,1)}, bf16[128,1024]{1,0:T(8,128)(2,1)S(1)}, u32[]{:S(2)}, u32[]{:S(2)}) %collective-permute-start.2) | collective-permute-done | bytes 262176 | tf_op jit(solution)/shard_map/ppermute | solution.py:131
  22.0 1.7 %collective-permute-done.1 = bf16[128,1024]{1,0:T(8,128)(2,1)S(1)} collective-permute-done((bf16[128,1024]{1,0:T(8,128)(2,1)}, bf16[128,1024]{1,0:T(8,128)(2,1)S(1)}, u32[]{:S(2)}, u32[]{:S(2)}) %collective-permute-start.1) | collective-permute-done | bytes 262176 | tf_op jit(solution)/shard_map/ppermute | solution.py:131
  23.7 1.1 pad_maximum_fusion.1
  24.9 0.6 gather_fusion
  25.7 0.7 copy.8
  26.5 0.6 reshape.45.taps_ref
  27.2 0.6 copy.10
  27.8 0.6 copy.9
  28.5 1.1 multiply_exponential_fusion
  29.8 72.4 %all-gather.2.cloned.1.call-done = bf16[2048,3,1024]{2,0,1:T(8,128)(2,1)} async-done(((bf16[128,3,1024]{2,0,1:T(8,128)(2,1)}), bf16[2048,3,1024]{2,0,1:T(8,128)(2,1)}) %all-gather.2.cloned.1.call-update) | async-done | bytes 12582928 | tf_op jit(solution)/shard_map/all_gather | solution.py:145
  102.2 2.9 %fusion.10 = f32[1,128,1024]{2,1,0:T(8,128)S(1)} fusion(bf16[2048,3,1024]{2,0,1:T(8,128)(2,1)} %all-gather.2.cloned.1.call-done, bf16[256,2048]{0,1:T(8,128)(2,1)S(1)} %pad_maximum_fusion.2), kind=kOutput, calls=%fused_computation.16 | convolution fusion | flops 536870912 | bytes 5242880 | tf_op jit(solution)/shard_map/dot_general | solution.py:169
  105.1 3.1 %fusion.8 = f32[1,128,1024]{2,1,0:T(8,128)S(1)} fusion(bf16[2048,3,1024]{2,0,1:T(8,128)(2,1)} %all-gather.2.cloned.1.call-done, bf16[256,2048]{0,1:T(8,128)(2,1)S(1)} %pad_maximum_fusion.2), kind=kOutput, calls=%fused_computation.14 | convolution fusion | flops 536870912 | bytes 5242880 | tf_op jit(solution)/shard_map/dot_general | solution.py:169
  108.2 3.5 %fusion.12 = f32[1,128,1024]{2,1,0:T(8,128)S(1)} fusion(bf16[2048,3,1024]{2,0,1:T(8,128)(2,1)} %all-gather.2.cloned.1.call-done, bf16[256,2048]{0,1:T(8,128)(2,1)S(1)} %pad_maximum_fusion.2), kind=kOutput, calls=%fused_computation.18 | convolution fusion | flops 536870912 | bytes 5242880 | tf_op jit(solution)/shard_map/dot_general | solution.py:169
  111.6 0.2 pad_maximum_fusion
  111.9 0.3 copy-done.5
  112.2 0.7 fusion.9
  112.9 0.8 fusion.7
  113.7 0.8 fusion.11
  114.5 0.8 collective-permute-done.4
  115.3 0.3 fusion.6
  115.7 2.0 %collective-permute-start.5 = (bf16[3,2,1024]{2,1,0:T(2,128)(2,1)S(1)}, bf16[3,2,1024]{2,1,0:T(2,128)(2,1)S(1)}, u32[]{:S(2)}, u32[]{:S(2)}) collective-permute-start(bf16[3,2,1024]{2,1,0:T(2,128)(2,1)S(1)} %slice.48), channel_id=1, source_target_pairs={{0,4},{4,8},{8,12},{12,16},{16,20},{20,24},{24,28},{28,32},{32,36}... | collective-permute-start | bytes 36872 | tf_op jit(solution)/shard_map/ppermute | solution.py:120
  117.7 0.8 collective-permute-done.5
  118.5 0.2 pad_maximum_fusion.3
  118.8 1.3 reshape.49.x_ref
  120.0 24.8 %shard_map.73 = bf16[128,8,128]{2,1,0:T(8,128)(2,1)} custom-call(bf16[3,130,8,128]{3,2,1,0:T(8,128)(2,1)} %reshape.49.x_ref, f32[3,3,8,128]{3,2,1,0:T(8,128)} %reshape.45.taps_ref, f32[16,8,128]{2,1,0:T(8,128)} %bitcast.63, f32[16,8,128]{2,1,0:T(8,128)} %bitcast.62, f32[8,128]{1,0:T(8,128)} %bitcast.70, f32[7,16,8,128]{3,2,1,0:T(8,128)} %get-tuple-element.19.lift_ref, ...), custom_call_target="tpu_custom_call" | custom-call | tf_op jit(solution)/shard_map/pallas_call | solution.py:183
  144.8 1.7 %copy.14 = bf16[16,8,8,128]{3,1,2,0:T(8,128)(2,1)} copy(bf16[16,8,8,128]{3,2,1,0:T(8,128)(2,1)} %bitcast.60) | data formatting | bytes 524288
  (26 shorter events, 0.6 us)
Async XLA Ops:
  6.5 95.6 %all-gather.2.cloned.1.call-start = ((), (), s32[]{:S(2)}) async-start(), calls=%async_computation | async-start | bytes 13369344 | tf_op jit(solution)/shard_map/all_gather | solution.py:145
  7.3 9.7 %collective-permute-start = (bf16[128,1024]{1,0:T(8,128)(2,1)}, bf16[128,1024]{1,0:T(8,128)(2,1)S(1)}, u32[]{:S(2)}, u32[]{:S(2)}) collective-permute-start(bf16[128,1024]{1,0:T(8,128)(2,1)} %param.7), channel_id=1, source_target_pairs={{0,1},{1,2},{2,3},{3,0},{4,5},{5,6},{6,7},{7,4},{8,9},{9,10},{10,1... | collective-permute-start | bytes 786440 | tf_op jit(solution)/shard_map/ppermute | solution.py:131
  9.0 13.1 %collective-permute-start.2 = (bf16[128,1024]{1,0:T(8,128)(2,1)}, bf16[128,1024]{1,0:T(8,128)(2,1)S(1)}, u32[]{:S(2)}, u32[]{:S(2)}) collective-permute-start(bf16[128,1024]{1,0:T(8,128)(2,1)} %param.7), channel_id=1, source_target_pairs={{0,3},{1,0},{2,1},{3,2},{4,7},{5,4},{6,5},{7,6},{8,11},{9,8},{10,9... | collective-permute-start | bytes 786440 | tf_op jit(solution)/shard_map/ppermute | solution.py:131
  10.6 13.2 %collective-permute-start.1 = (bf16[128,1024]{1,0:T(8,128)(2,1)}, bf16[128,1024]{1,0:T(8,128)(2,1)S(1)}, u32[]{:S(2)}, u32[]{:S(2)}) collective-permute-start(bf16[128,1024]{1,0:T(8,128)(2,1)} %param.7), channel_id=1, source_target_pairs={{0,2},{1,3},{2,0},{3,1},{4,6},{5,7},{6,4},{7,5},{8,10},{9,11},{10,... | collective-permute-start | bytes 786440 | tf_op jit(solution)/shard_map/ppermute | solution.py:131
  24.8 1.7 %copy-start.2 = (f32[3,3,1024]{2,1,0:T(4,128)S(1)}, f32[3,3,1024]{2,1,0:T(4,128)}, u32[]{:S(2)}) copy-start(f32[3,3,1024]{2,1,0:T(4,128)} %param.9) | copy-start | bytes 110596
  24.8 2.3 %copy-start.1 = (f32[16,1024]{1,0:T(8,128)S(1)}, f32[16,1024]{1,0:T(8,128)}, u32[]{:S(2)}) copy-start(f32[16,1024]{1,0:T(8,128)} %param.11) | copy-start | bytes 196612
  24.8 3.0 %copy-start = (f32[16,1024]{1,0:T(8,128)S(1)}, f32[16,1024]{1,0:T(8,128)}, u32[]{:S(2)}) copy-start(f32[16,1024]{1,0:T(8,128)} %param.10) | copy-start | bytes 196612
  24.9 3.6 %copy-start.3 = (f32[7]{0:T(128)S(1)}, f32[7]{0:T(128)}, u32[]{:S(2)}) copy-start(f32[7]{0:T(128)} %constant.48) | copy-start | bytes 88
  24.9 3.6 %copy-start.4 = (f32[7]{0:T(128)S(1)}, f32[7]{0:T(128)}, u32[]{:S(2)}) copy-start(f32[7]{0:T(128)} %constant.47) | copy-start | bytes 88
  26.4 3.2 %collective-permute-start.3 = (bf16[128,2048]{0,1:T(8,128)(2,1)S(1)}, bf16[128,2048]{0,1:T(8,128)(2,1)S(1)}, u32[]{:S(2)}, u32[]{:S(2)}) collective-permute-start(bf16[128,2048]{0,1:T(8,128)(2,1)S(1)} %bitcast.61), channel_id=1, source_target_pairs={{0,4},{4,0},{1,5},{5,1},{2,6},{6,2},{3,7},{7,3},{8,12},{12,8},{9,1... | collective-permute-start | bytes 1572872 | tf_op jit(solution)/shard_map/ppermute | solution.py:124
  105.1 7.1 %copy-start.5 = (bf16[2048,3,1024]{2,0,1:T(8,128)(2,1)S(1)}, bf16[2048,3,1024]{2,0,1:T(8,128)(2,1)}, u32[]{:S(2)}) copy-start(bf16[2048,3,1024]{2,0,1:T(8,128)(2,1)} %all-gather.2.cloned.1.call-done) | copy-start | bytes 37748740
  111.8 3.5 %collective-permute-start.4 = (f32[3,128,1024]{2,1,0:T(8,128)S(1)}, f32[3,128,1024]{2,1,0:T(8,128)S(1)}, u32[]{:S(2)}, u32[]{:S(2)}) collective-permute-start(f32[3,128,1024]{2,1,0:T(8,128)S(1)} %pad_maximum_fusion), channel_id=1, source_target_pairs={{0,4},{4,0},{1,5},{5,1},{2,6},{6,2},{3,7},{7,3},{8,12},{12,8},{9,1... | collective-permute-start | bytes 4718600 | tf_op jit(solution)/shard_map/ppermute | solution.py:124
  115.7 2.9 %collective-permute-start.5 = (bf16[3,2,1024]{2,1,0:T(2,128)(2,1)S(1)}, bf16[3,2,1024]{2,1,0:T(2,128)(2,1)S(1)}, u32[]{:S(2)}, u32[]{:S(2)}) collective-permute-start(bf16[3,2,1024]{2,1,0:T(2,128)(2,1)S(1)} %slice.48), channel_id=1, source_target_pairs={{0,4},{4,8},{8,12},{12,16},{16,20},{20,24},{24,28},{28,32},{32,36}... | collective-permute-start | bytes 36872 | tf_op jit(solution)/shard_map/ppermute | solution.py:120
Sparse Core Ops, SparseCore 0:
  9.5 92.6 all-gather.1

commit v15 on v14

--- a/solution.py
+++ b/solution.py
@@ -34,16 +34,25 @@
 
 def mixed_kernel(x_ref, taps_ref, decay_ref, resid_ref, skip_ref, start_ref, out_ref):
     rows = x_ref.shape[1] - 2
-
-    def step(t, state):
-        query = filtered_at(x_ref, taps_ref, 0, t)
-        gated = filtered_at(x_ref, taps_ref, 1, t) * filtered_at(x_ref, taps_ref, 2, t)
-        state = decay_ref[...] * state + gated[None]
-        convolved = jnp.sum(resid_ref[...] * state, axis=0)
-        out_ref[t] = (query * (convolved + skip_ref[...] * gated)).astype(out_ref.dtype)
+    run = 16
+    subl = x_ref.shape[2]
+
+    def block(b, state):
+        values = []
+        for i in range(run):
+            t = b * run + i
+            query = filtered_at(x_ref, taps_ref, 0, t)
+            gated = filtered_at(x_ref, taps_ref, 1, t) * filtered_at(x_ref, taps_ref, 2, t)
+            state = decay_ref[...] * state + gated[None]
+            convolved = jnp.sum(resid_ref[...] * state, axis=0)
+            values.append(query * (convolved + skip_ref[...] * gated))
+        tiles = jnp.swapaxes(jnp.stack(values, axis=0), 0, 1)
+        first = pl.multiple_of(b * run, run)
+        for s in range(subl):
+            out_ref[pl.ds(first, run), pl.ds(s * LANES, LANES)] = tiles[s].astype(out_ref.dtype)
         return state
 
-    lax.fori_loop(0, rows, step, start_ref[...], unroll=8)
+    lax.fori_loop(0, rows // run, block, start_ref[...])
 
 
 def block_kernel(
@@ -182,7 +191,7 @@
     state_shape = (poles, subl, LANES)
     out = pl.pallas_call(
         functools.partial(block_kernel, peers, digits),
-        out_shape=jax.ShapeDtypeStruct((rows, subl, LANES), jnp.bfloat16),
+        out_shape=jax.ShapeDtypeStruct((rows, chans), jnp.bfloat16),
         in_specs=vmem_specs(7),
         out_specs=pl.BlockSpec(memory_space=pltpu.VMEM),
         scratch_shapes=[
@@ -195,7 +204,7 @@
         ],
         compiler_params=pltpu.CompilerParams(collective_id=0, has_side_effects=True),
     )(x, taps, decay, resid, direct, lift, keep)
-    return out.reshape(rows, chans)
+    return out
 
 
 def solution(mesh):

time: 154 us -> 154 us (level)
  no operation moved by 1% of the time
where the time goes in v15:
time: 154 us; the launch traced here: 153 us
  waiting for transfers between devices  85.1 us (55%)
  Pallas kernels  24.7 us (16%)
  between operations  13.6 us (9%)
  matrix products  11.7 us (8%)
  starting transfers between devices  7.59 us (5%)
  local copies, waits for them, and re-layouts  6.45 us (4%)
  other arithmetic  4.1 us (3%)
    all_gather x1, waiting for transfers between devices, per_device(): piece = lax.all_gather(in_weight, 'cx', axis=0, tiled=True)  72.4 us
    pallas_call x1, Pallas kernels, per_device(): pl.pallas_call(functools.partial(block_kernel, peers, digits), out_shape=...  24.7 us
    ppermute x3, waiting for transfers between devices, gathered_tp(): lax.ppermute(tokens, 'tp', [(i, (i + by) % peers) for i in range(peers)])  10.3 us
    dot_general x3, matrix products, per_device(): jnp.dot(both[rows:], piece[:, g, :], preferred_element_type=jnp.float32)  9.45 us
    ppermute x3, starting transfers between devices, gathered_tp(): lax.ppermute(tokens, 'tp', [(i, (i + by) % peers) for i in range(peers)])  5.37 us
    unnamed x16, local copies, waits for them, and re-layouts  3.28 us
  transfers between devices with their start and end apart: 7, of which 6 were waited for; matrix products, arithmetic and copies ran while one was open for 6% of the time, Pallas kernels for 0%

profile of v15, /device:TPU:0, one launch (start us, length us, event | category | flops | bytes accessed | tf_op | source)
XLA Modules:
  0.0 153.2 jit_solution(8380290189550567689)
XLA Ops:
  6.5 0.7 all-gather.2.cloned.1.call-update
  7.3 1.7 %collective-permute-start = (bf16[128,1024]{1,0:T(8,128)(2,1)}, bf16[128,1024]{1,0:T(8,128)(2,1)S(1)}, u32[]{:S(2)}, u32[]{:S(2)}) collective-permute-start(bf16[128,1024]{1,0:T(8,128)(2,1)} %param.7), channel_id=1, source_target_pairs={{0,1},{1,2},{2,3},{3,0},{4,5},{5,6},{6,7},{7,4},{8,9},{9,10},{10,1... | collective-permute-start | bytes 786440 | tf_op jit(solution)/shard_map/ppermute | solution.py:140
  9.0 1.6 %collective-permute-start.2 = (bf16[128,1024]{1,0:T(8,128)(2,1)}, bf16[128,1024]{1,0:T(8,128)(2,1)S(1)}, u32[]{:S(2)}, u32[]{:S(2)}) collective-permute-start(bf16[128,1024]{1,0:T(8,128)(2,1)} %param.7), channel_id=1, source_target_pairs={{0,3},{1,0},{2,1},{3,2},{4,7},{5,4},{6,5},{7,6},{8,11},{9,8},{10,9... | collective-permute-start | bytes 786440 | tf_op jit(solution)/shard_map/ppermute | solution.py:140
  10.6 2.1 %collective-permute-start.1 = (bf16[128,1024]{1,0:T(8,128)(2,1)}, bf16[128,1024]{1,0:T(8,128)(2,1)S(1)}, u32[]{:S(2)}, u32[]{:S(2)}) collective-permute-start(bf16[128,1024]{1,0:T(8,128)(2,1)} %param.7), channel_id=1, source_target_pairs={{0,2},{1,3},{2,0},{3,1},{4,6},{5,7},{6,4},{7,5},{8,10},{9,11},{10,... | collective-permute-start | bytes 786440 | tf_op jit(solution)/shard_map/ppermute | solution.py:140
  12.6 0.7 sort.17
  13.4 3.5 %collective-permute-done = bf16[128,1024]{1,0:T(8,128)(2,1)S(1)} collective-permute-done((bf16[128,1024]{1,0:T(8,128)(2,1)}, bf16[128,1024]{1,0:T(8,128)(2,1)S(1)}, u32[]{:S(2)}, u32[]{:S(2)}) %collective-permute-start) | collective-permute-done | bytes 262176 | tf_op jit(solution)/shard_map/ppermute | solution.py:140
  16.9 5.1 %collective-permute-done.2 = bf16[128,1024]{1,0:T(8,128)(2,1)S(1)} collective-permute-done((bf16[128,1024]{1,0:T(8,128)(2,1)}, bf16[128,1024]{1,0:T(8,128)(2,1)S(1)}, u32[]{:S(2)}, u32[]{:S(2)}) %collective-permute-start.2) | collective-permute-done | bytes 262176 | tf_op jit(solution)/shard_map/ppermute | solution.py:140
  22.0 1.7 %collective-permute-done.1 = bf16[128,1024]{1,0:T(8,128)(2,1)S(1)} collective-permute-done((bf16[128,1024]{1,0:T(8,128)(2,1)}, bf16[128,1024]{1,0:T(8,128)(2,1)S(1)}, u32[]{:S(2)}, u32[]{:S(2)}) %collective-permute-start.1) | collective-permute-done | bytes 262176 | tf_op jit(solution)/shard_map/ppermute | solution.py:140
  23.7 1.1 pad_maximum_fusion.1
  24.9 0.6 gather_fusion
  25.7 0.7 copy.8
  26.5 0.6 reshape.42.taps_ref
  27.2 0.6 copy.10
  27.8 0.6 copy.9
  28.5 1.1 multiply_exponential_fusion
  29.8 72.4 %all-gather.2.cloned.1.call-done = bf16[2048,3,1024]{2,0,1:T(8,128)(2,1)} async-done(((bf16[128,3,1024]{2,0,1:T(8,128)(2,1)}), bf16[2048,3,1024]{2,0,1:T(8,128)(2,1)}) %all-gather.2.cloned.1.call-update) | async-done | bytes 12582928 | tf_op jit(solution)/shard_map/all_gather | solution.py:154
  102.2 2.9 %fusion.10 = f32[1,128,1024]{2,1,0:T(8,128)S(1)} fusion(bf16[2048,3,1024]{2,0,1:T(8,128)(2,1)} %all-gather.2.cloned.1.call-done, bf16[256,2048]{0,1:T(8,128)(2,1)S(1)} %pad_maximum_fusion.2), kind=kOutput, calls=%fused_computation.16 | convolution fusion | flops 536870912 | bytes 5242880 | tf_op jit(solution)/shard_map/dot_general | solution.py:178
  105.1 3.1 %fusion.8 = f32[1,128,1024]{2,1,0:T(8,128)S(1)} fusion(bf16[2048,3,1024]{2,0,1:T(8,128)(2,1)} %all-gather.2.cloned.1.call-done, bf16[256,2048]{0,1:T(8,128)(2,1)S(1)} %pad_maximum_fusion.2), kind=kOutput, calls=%fused_computation.14 | convolution fusion | flops 536870912 | bytes 5242880 | tf_op jit(solution)/shard_map/dot_general | solution.py:178
  108.2 3.5 %fusion.12 = f32[1,128,1024]{2,1,0:T(8,128)S(1)} fusion(bf16[2048,3,1024]{2,0,1:T(8,128)(2,1)} %all-gather.2.cloned.1.call-done, bf16[256,2048]{0,1:T(8,128)(2,1)S(1)} %pad_maximum_fusion.2), kind=kOutput, calls=%fused_computation.18 | convolution fusion | flops 536870912 | bytes 5242880 | tf_op jit(solution)/shard_map/dot_general | solution.py:178
  111.6 0.2 pad_maximum_fusion
  111.9 0.3 copy-done.5
  112.2 0.7 fusion.9
  112.9 0.8 fusion.7
  113.7 0.8 fusion.11
  114.5 0.8 collective-permute-done.4
  115.3 0.3 fusion.6
  115.7 2.0 %collective-permute-start.5 = (bf16[3,2,1024]{2,1,0:T(2,128)(2,1)S(1)}, bf16[3,2,1024]{2,1,0:T(2,128)(2,1)S(1)}, u32[]{:S(2)}, u32[]{:S(2)}) collective-permute-start(bf16[3,2,1024]{2,1,0:T(2,128)(2,1)S(1)} %slice.48), channel_id=1, source_target_pairs={{0,4},{4,8},{8,12},{12,16},{16,20},{20,24},{24,28},{28,32},{32,36}... | collective-permute-start | bytes 36872 | tf_op jit(solution)/shard_map/ppermute | solution.py:129
  117.7 0.8 collective-permute-done.5
  118.5 0.2 pad_maximum_fusion.3
  118.8 1.3 reshape.46.x_ref
  120.0 24.7 %shard_map.73 = bf16[128,1024]{1,0:T(8,128)(2,1)} custom-call(bf16[3,130,8,128]{3,2,1,0:T(8,128)(2,1)} %reshape.46.x_ref, f32[3,3,8,128]{3,2,1,0:T(8,128)} %reshape.42.taps_ref, f32[16,8,128]{2,1,0:T(8,128)} %bitcast.58, f32[16,8,128]{2,1,0:T(8,128)} %bitcast.57, f32[8,128]{1,0:T(8,128)} %bitcast.65, f32[7,16,8,128]{3,2,1,0:T(8,128)} %get-tuple-element.19.lift_ref, ...), custom_call_target="tpu_custom_call" | custom-call | tf_op jit(solution)/shard_map/pallas_call | solution.py:192
  144.7 1.7 %copy.13 = bf16[128,1024]{1,0:T(8,128)(2,1)} copy(bf16[128,1024]{1,0:T(8,128)(2,1)} %shard_map.73) | data formatting | bytes 524288
  (26 shorter events, 0.6 us)
Async XLA Ops:
  6.5 95.6 %all-gather.2.cloned.1.call-start = ((), (), s32[]{:S(2)}) async-start(), calls=%async_computation | async-start | bytes 13369344 | tf_op jit(solution)/shard_map/all_gather | solution.py:154
  7.3 9.7 %collective-permute-start = (bf16[128,1024]{1,0:T(8,128)(2,1)}, bf16[128,1024]{1,0:T(8,128)(2,1)S(1)}, u32[]{:S(2)}, u32[]{:S(2)}) collective-permute-start(bf16[128,1024]{1,0:T(8,128)(2,1)} %param.7), channel_id=1, source_target_pairs={{0,1},{1,2},{2,3},{3,0},{4,5},{5,6},{6,7},{7,4},{8,9},{9,10},{10,1... | collective-permute-start | bytes 786440 | tf_op jit(solution)/shard_map/ppermute | solution.py:140
  9.0 13.1 %collective-permute-start.2 = (bf16[128,1024]{1,0:T(8,128)(2,1)}, bf16[128,1024]{1,0:T(8,128)(2,1)S(1)}, u32[]{:S(2)}, u32[]{:S(2)}) collective-permute-start(bf16[128,1024]{1,0:T(8,128)(2,1)} %param.7), channel_id=1, source_target_pairs={{0,3},{1,0},{2,1},{3,2},{4,7},{5,4},{6,5},{7,6},{8,11},{9,8},{10,9... | collective-permute-start | bytes 786440 | tf_op jit(solution)/shard_map/ppermute | solution.py:140
  10.6 13.2 %collective-permute-start.1 = (bf16[128,1024]{1,0:T(8,128)(2,1)}, bf16[128,1024]{1,0:T(8,128)(2,1)S(1)}, u32[]{:S(2)}, u32[]{:S(2)}) collective-permute-start(bf16[128,1024]{1,0:T(8,128)(2,1)} %param.7), channel_id=1, source_target_pairs={{0,2},{1,3},{2,0},{3,1},{4,6},{5,7},{6,4},{7,5},{8,10},{9,11},{10,... | collective-permute-start | bytes 786440 | tf_op jit(solution)/shard_map/ppermute | solution.py:140
  24.8 1.7 %copy-start.2 = (f32[3,3,1024]{2,1,0:T(4,128)S(1)}, f32[3,3,1024]{2,1,0:T(4,128)}, u32[]{:S(2)}) copy-start(f32[3,3,1024]{2,1,0:T(4,128)} %param.9) | copy-start | bytes 110596
  24.8 2.3 %copy-start.1 = (f32[16,1024]{1,0:T(8,128)S(1)}, f32[16,1024]{1,0:T(8,128)}, u32[]{:S(2)}) copy-start(f32[16,1024]{1,0:T(8,128)} %param.11) | copy-start | bytes 196612
  24.8 3.0 %copy-start = (f32[16,1024]{1,0:T(8,128)S(1)}, f32[16,1024]{1,0:T(8,128)}, u32[]{:S(2)}) copy-start(f32[16,1024]{1,0:T(8,128)} %param.10) | copy-start | bytes 196612
  24.9 3.6 %copy-start.3 = (f32[7]{0:T(128)S(1)}, f32[7]{0:T(128)}, u32[]{:S(2)}) copy-start(f32[7]{0:T(128)} %constant.48) | copy-start | bytes 88
  24.9 3.6 %copy-start.4 = (f32[7]{0:T(128)S(1)}, f32[7]{0:T(128)}, u32[]{:S(2)}) copy-start(f32[7]{0:T(128)} %constant.47) | copy-start | bytes 88
  26.4 3.2 %collective-permute-start.3 = (bf16[128,2048]{0,1:T(8,128)(2,1)S(1)}, bf16[128,2048]{0,1:T(8,128)(2,1)S(1)}, u32[]{:S(2)}, u32[]{:S(2)}) collective-permute-start(bf16[128,2048]{0,1:T(8,128)(2,1)S(1)} %bitcast.56), channel_id=1, source_target_pairs={{0,4},{4,0},{1,5},{5,1},{2,6},{6,2},{3,7},{7,3},{8,12},{12,8},{9,1... | collective-permute-start | bytes 1572872 | tf_op jit(solution)/shard_map/ppermute | solution.py:133
  105.1 7.1 %copy-start.5 = (bf16[2048,3,1024]{2,0,1:T(8,128)(2,1)S(1)}, bf16[2048,3,1024]{2,0,1:T(8,128)(2,1)}, u32[]{:S(2)}) copy-start(bf16[2048,3,1024]{2,0,1:T(8,128)(2,1)} %all-gather.2.cloned.1.call-done) | copy-start | bytes 37748740
  111.8 3.5 %collective-permute-start.4 = (f32[3,128,1024]{2,1,0:T(8,128)S(1)}, f32[3,128,1024]{2,1,0:T(8,128)S(1)}, u32[]{:S(2)}, u32[]{:S(2)}) collective-permute-start(f32[3,128,1024]{2,1,0:T(8,128)S(1)} %pad_maximum_fusion), channel_id=1, source_target_pairs={{0,4},{4,0},{1,5},{5,1},{2,6},{6,2},{3,7},{7,3},{8,12},{12,8},{9,1... | collective-permute-start | bytes 4718600 | tf_op jit(solution)/shard_map/ppermute | solution.py:133
  115.7 2.9 %collective-permute-start.5 = (bf16[3,2,1024]{2,1,0:T(2,128)(2,1)S(1)}, bf16[3,2,1024]{2,1,0:T(2,128)(2,1)S(1)}, u32[]{:S(2)}, u32[]{:S(2)}) collective-permute-start(bf16[3,2,1024]{2,1,0:T(2,128)(2,1)S(1)} %slice.48), channel_id=1, source_target_pairs={{0,4},{4,8},{8,12},{12,16},{16,20},{20,24},{24,28},{28,32},{32,36}... | collective-permute-start | bytes 36872 | tf_op jit(solution)/shard_map/ppermute | solution.py:129
Sparse Core Ops, SparseCore 0:
  9.5 92.6 all-gather.1

commit v16 on v15

--- a/solution.py
+++ b/solution.py
@@ -14,9 +14,9 @@
 
 def filtered_at(x_ref, taps_ref, g, t):
     return (
-        taps_ref[0, g] * x_ref[g, t + 2].astype(jnp.float32)
-        + taps_ref[1, g] * x_ref[g, t + 1].astype(jnp.float32)
-        + taps_ref[2, g] * x_ref[g, t].astype(jnp.float32)
+        taps_ref[0, g] * x_ref[g, t + 2]
+        + taps_ref[1, g] * x_ref[g, t + 1]
+        + taps_ref[2, g] * x_ref[g, t]
     )
 
 
@@ -55,9 +55,20 @@
     lax.fori_loop(0, rows // run, block, start_ref[...])
 
 
+def to_positions(proj_ref, edge_ref, x_ref):
+    run = 16
+    subl = x_ref.shape[2]
+    x_ref[:, 0:2] = edge_ref[...].astype(jnp.float32)
+    for g in range(proj_ref.shape[0]):
+        for b in range(proj_ref.shape[1] // run):
+            rows_ = proj_ref[g, b * run : (b + 1) * run, :].astype(jnp.float32)
+            cols = jnp.stack([rows_[:, s * LANES : (s + 1) * LANES] for s in range(subl)], axis=0)
+            x_ref[g, 2 + b * run : 2 + (b + 1) * run] = jnp.swapaxes(cols, 0, 1)
+
+
 def block_kernel(
-    peers, digits, x_ref, taps_ref, decay_ref, resid_ref, skip_ref, lift_ref, keep_ref, out_ref,
-    end_ref, start_ref, held, slots, send_sem, recv_sem,
+    peers, digits, proj_ref, edge_ref, taps_ref, decay_ref, resid_ref, skip_ref, lift_ref, keep_ref,
+    out_ref, x_ref, end_ref, start_ref, held, slots, send_sem, recv_sem,
 ):
     me = lax.axis_index("cx") * 2 + lax.axis_index("core")
     tp = lax.axis_index("tp")
@@ -75,6 +86,7 @@
     for _, by in steps:
         for peer in ((me + by) % peers, (me + peers - by) % peers):
             pl.semaphore_signal(barrier, inc=1, device_id=device(peer), device_id_type=MESH)
+    to_positions(proj_ref, edge_ref, x_ref)
     local_end_kernel(x_ref, taps_ref, decay_ref, end_ref)
     pl.semaphore_wait(barrier, 2 * len(steps))
 
@@ -186,15 +198,16 @@
     sums = mine_part + arrived
     projected = sums.astype(jnp.bfloat16)
     edge_out = shifted(projected[:, rows - 2 :, :], ctx, 1)
-    extended = jnp.concatenate([edge_out, projected], axis=1).reshape(3, rows + 2, subl, LANES)
-    x = lax.optimization_barrier(extended)
+    edge = edge_out.reshape(3, 2, subl, LANES)
+    projected, edge = lax.optimization_barrier((projected, edge))
     state_shape = (poles, subl, LANES)
     out = pl.pallas_call(
         functools.partial(block_kernel, peers, digits),
         out_shape=jax.ShapeDtypeStruct((rows, chans), jnp.bfloat16),
-        in_specs=vmem_specs(7),
+        in_specs=vmem_specs(8),
         out_specs=pl.BlockSpec(memory_space=pltpu.VMEM),
         scratch_shapes=[
+            pltpu.VMEM((3, rows + 2, subl, LANES), jnp.float32),
             pltpu.VMEM(state_shape, jnp.float32),
             pltpu.VMEM(state_shape, jnp.float32),
             pltpu.VMEM((len(digits),) + state_shape, jnp.float32),
@@ -203,7 +216,7 @@
             pltpu.SemaphoreType.DMA((copies,)),
         ],
         compiler_params=pltpu.CompilerParams(collective_id=0, has_side_effects=True),
-    )(x, taps, decay, resid, direct, lift, keep)
+    )(projected, edge, taps, decay, resid, direct, lift, keep)
     return out
 
 

time: 154 us -> 153 us (level)
    unnamed x16 -> x18, local copies, waits for them, and re-layouts: 3.28 us -> 3.28 us
where the time goes in v16:
time: 153 us; the launch traced here: 152 us
  waiting for transfers between devices  85.1 us (56%)
  Pallas kernels  24.7 us (16%)
  between operations  13.6 us (9%)
  matrix products  11.7 us (8%)
  starting transfers between devices  7.59 us (5%)
  local copies, waits for them, and re-layouts  5.82 us (4%)
  other arithmetic  3.89 us (3%)
    all_gather x1, waiting for transfers between devices, per_device(): piece = lax.all_gather(in_weight, 'cx', axis=0, tiled=True)  72.4 us
    pallas_call x1, Pallas kernels, per_device(): pl.pallas_call(functools.partial(block_kernel, peers, digits), out_shape=...  24.7 us
    ppermute x3, waiting for transfers between devices, gathered_tp(): lax.ppermute(tokens, 'tp', [(i, (i + by) % peers) for i in range(peers)])  10.3 us
    dot_general x3, matrix products, per_device(): jnp.dot(both[rows:], piece[:, g, :], preferred_element_type=jnp.float32)  9.45 us
    ppermute x3, starting transfers between devices, gathered_tp(): lax.ppermute(tokens, 'tp', [(i, (i + by) % peers) for i in range(peers)])  5.37 us
    unnamed x18, local copies, waits for them, and re-layouts  3.28 us
  transfers between devices with their start and end apart: 7, of which 6 were waited for; matrix products, arithmetic and copies ran while one was open for 6% of the time, Pallas kernels for 0%

profile of v16, /device:TPU:0, one launch (start us, length us, event | category | flops | bytes accessed | tf_op | source)
XLA Modules:
  0.0 152.4 jit_solution(2975768208993460127)
XLA Ops:
  6.5 0.7 all-gather.2.cloned.1.call-update
  7.3 1.7 %collective-permute-start = (bf16[128,1024]{1,0:T(8,128)(2,1)}, bf16[128,1024]{1,0:T(8,128)(2,1)S(1)}, u32[]{:S(2)}, u32[]{:S(2)}) collective-permute-start(bf16[128,1024]{1,0:T(8,128)(2,1)} %param.7), channel_id=1, source_target_pairs={{0,1},{1,2},{2,3},{3,0},{4,5},{5,6},{6,7},{7,4},{8,9},{9,10},{10,1... | collective-permute-start | bytes 786440 | tf_op jit(solution)/shard_map/ppermute | solution.py:152
  9.0 1.6 %collective-permute-start.2 = (bf16[128,1024]{1,0:T(8,128)(2,1)}, bf16[128,1024]{1,0:T(8,128)(2,1)S(1)}, u32[]{:S(2)}, u32[]{:S(2)}) collective-permute-start(bf16[128,1024]{1,0:T(8,128)(2,1)} %param.7), channel_id=1, source_target_pairs={{0,3},{1,0},{2,1},{3,2},{4,7},{5,4},{6,5},{7,6},{8,11},{9,8},{10,9... | collective-permute-start | bytes 786440 | tf_op jit(solution)/shard_map/ppermute | solution.py:152
  10.6 2.1 %collective-permute-start.1 = (bf16[128,1024]{1,0:T(8,128)(2,1)}, bf16[128,1024]{1,0:T(8,128)(2,1)S(1)}, u32[]{:S(2)}, u32[]{:S(2)}) collective-permute-start(bf16[128,1024]{1,0:T(8,128)(2,1)} %param.7), channel_id=1, source_target_pairs={{0,2},{1,3},{2,0},{3,1},{4,6},{5,7},{6,4},{7,5},{8,10},{9,11},{10,... | collective-permute-start | bytes 786440 | tf_op jit(solution)/shard_map/ppermute | solution.py:152
  12.6 0.7 sort.17
  13.4 3.5 %collective-permute-done = bf16[128,1024]{1,0:T(8,128)(2,1)S(1)} collective-permute-done((bf16[128,1024]{1,0:T(8,128)(2,1)}, bf16[128,1024]{1,0:T(8,128)(2,1)S(1)}, u32[]{:S(2)}, u32[]{:S(2)}) %collective-permute-start) | collective-permute-done | bytes 262176 | tf_op jit(solution)/shard_map/ppermute | solution.py:152
  16.9 5.1 %collective-permute-done.2 = bf16[128,1024]{1,0:T(8,128)(2,1)S(1)} collective-permute-done((bf16[128,1024]{1,0:T(8,128)(2,1)}, bf16[128,1024]{1,0:T(8,128)(2,1)S(1)}, u32[]{:S(2)}, u32[]{:S(2)}) %collective-permute-start.2) | collective-permute-done | bytes 262176 | tf_op jit(solution)/shard_map/ppermute | solution.py:152
  22.0 1.7 %collective-permute-done.1 = bf16[128,1024]{1,0:T(8,128)(2,1)S(1)} collective-permute-done((bf16[128,1024]{1,0:T(8,128)(2,1)}, bf16[128,1024]{1,0:T(8,128)(2,1)S(1)}, u32[]{:S(2)}, u32[]{:S(2)}) %collective-permute-start.1) | collective-permute-done | bytes 262176 | tf_op jit(solution)/shard_map/ppermute | solution.py:152
  23.7 1.1 pad_maximum_fusion.1
  24.9 0.6 gather_fusion
  25.5 0.2 select_bitcast_fusion
  25.7 0.7 copy.8
  26.5 0.6 reshape.42.taps_ref
  27.2 0.6 copy.10
  27.8 0.6 copy.9
  28.5 1.1 multiply_exponential_fusion
  29.8 72.4 %all-gather.2.cloned.1.call-done = bf16[2048,3,1024]{2,0,1:T(8,128)(2,1)} async-done(((bf16[128,3,1024]{2,0,1:T(8,128)(2,1)}), bf16[2048,3,1024]{2,0,1:T(8,128)(2,1)}) %all-gather.2.cloned.1.call-update) | async-done | bytes 12582928 | tf_op jit(solution)/shard_map/all_gather | solution.py:166
  102.2 2.9 %fusion.10 = f32[1,128,1024]{2,1,0:T(8,128)S(1)} fusion(bf16[2048,3,1024]{2,0,1:T(8,128)(2,1)} %all-gather.2.cloned.1.call-done, bf16[256,2048]{0,1:T(8,128)(2,1)S(1)} %pad_maximum_fusion.2), kind=kOutput, calls=%fused_computation.16 | convolution fusion | flops 536870912 | bytes 5242880 | tf_op jit(solution)/shard_map/dot_general | solution.py:190
  105.1 3.1 %fusion.8 = f32[1,128,1024]{2,1,0:T(8,128)S(1)} fusion(bf16[2048,3,1024]{2,0,1:T(8,128)(2,1)} %all-gather.2.cloned.1.call-done, bf16[256,2048]{0,1:T(8,128)(2,1)S(1)} %pad_maximum_fusion.2), kind=kOutput, calls=%fused_computation.14 | convolution fusion | flops 536870912 | bytes 5242880 | tf_op jit(solution)/shard_map/dot_general | solution.py:190
  108.2 3.5 %fusion.12 = f32[1,128,1024]{2,1,0:T(8,128)S(1)} fusion(bf16[2048,3,1024]{2,0,1:T(8,128)(2,1)} %all-gather.2.cloned.1.call-done, bf16[256,2048]{0,1:T(8,128)(2,1)S(1)} %pad_maximum_fusion.2), kind=kOutput, calls=%fused_computation.18 | convolution fusion | flops 536870912 | bytes 5242880 | tf_op jit(solution)/shard_map/dot_general | solution.py:190
  111.6 0.2 pad_maximum_fusion
  111.9 0.3 copy-done.6
  112.2 0.7 fusion.9
  112.9 0.8 fusion.7
  113.7 0.8 fusion.11
  114.5 0.8 collective-permute-done.4
  115.3 0.3 fusion.6.proj_ref
  115.7 2.0 %collective-permute-start.5 = (bf16[3,2,1024]{2,1,0:T(2,128)(2,1)S(1)}, bf16[3,2,1024]{2,1,0:T(2,128)(2,1)S(1)}, u32[]{:S(2)}, u32[]{:S(2)}) collective-permute-start(bf16[3,2,1024]{2,1,0:T(2,128)(2,1)S(1)} %slice.48), channel_id=1, source_target_pairs={{0,4},{4,8},{8,12},{12,16},{16,20},{20,24},{24,28},{28,32},{32,36}... | collective-permute-start | bytes 36872 | tf_op jit(solution)/shard_map/ppermute | solution.py:141
  117.7 0.8 collective-permute-done.5
  118.5 0.6 reshape.46.edge_ref
  119.2 24.7 %shard_map.73 = bf16[128,1024]{1,0:T(8,128)(2,1)} custom-call(bf16[3,128,1024]{2,1,0:T(8,128)(2,1)} %copy-done, bf16[3,2,8,128]{3,2,1,0:T(8,128)(2,1)} %reshape.46.edge_ref, f32[3,3,8,128]{3,2,1,0:T(8,128)} %reshape.42.taps_ref, f32[16,8,128]{2,1,0:T(8,128)} %bitcast.58, f32[16,8,128]{2,1,0:T(8,128)} %bitcast.57, f32[8,128]{1,0:T(8,128)} %bitcast.65, ...), custom_call_target="tpu_custom_call" | custom-call | tf_op jit(solution)/shard_map/pallas_call | solution.py:204
  143.9 1.7 %copy.13 = bf16[128,1024]{1,0:T(8,128)(2,1)} copy(bf16[128,1024]{1,0:T(8,128)(2,1)} %shard_map.73) | data formatting | bytes 524288
  (27 shorter events, 0.5 us)
Async XLA Ops:
  6.5 95.6 %all-gather.2.cloned.1.call-start = ((), (), s32[]{:S(2)}) async-start(), calls=%async_computation | async-start | bytes 13369344 | tf_op jit(solution)/shard_map/all_gather | solution.py:166
  7.3 9.7 %collective-permute-start = (bf16[128,1024]{1,0:T(8,128)(2,1)}, bf16[128,1024]{1,0:T(8,128)(2,1)S(1)}, u32[]{:S(2)}, u32[]{:S(2)}) collective-permute-start(bf16[128,1024]{1,0:T(8,128)(2,1)} %param.7), channel_id=1, source_target_pairs={{0,1},{1,2},{2,3},{3,0},{4,5},{5,6},{6,7},{7,4},{8,9},{9,10},{10,1... | collective-permute-start | bytes 786440 | tf_op jit(solution)/shard_map/ppermute | solution.py:152
  9.0 13.1 %collective-permute-start.2 = (bf16[128,1024]{1,0:T(8,128)(2,1)}, bf16[128,1024]{1,0:T(8,128)(2,1)S(1)}, u32[]{:S(2)}, u32[]{:S(2)}) collective-permute-start(bf16[128,1024]{1,0:T(8,128)(2,1)} %param.7), channel_id=1, source_target_pairs={{0,3},{1,0},{2,1},{3,2},{4,7},{5,4},{6,5},{7,6},{8,11},{9,8},{10,9... | collective-permute-start | bytes 786440 | tf_op jit(solution)/shard_map/ppermute | solution.py:152
  10.6 13.2 %collective-permute-start.1 = (bf16[128,1024]{1,0:T(8,128)(2,1)}, bf16[128,1024]{1,0:T(8,128)(2,1)S(1)}, u32[]{:S(2)}, u32[]{:S(2)}) collective-permute-start(bf16[128,1024]{1,0:T(8,128)(2,1)} %param.7), channel_id=1, source_target_pairs={{0,2},{1,3},{2,0},{3,1},{4,6},{5,7},{6,4},{7,5},{8,10},{9,11},{10,... | collective-permute-start | bytes 786440 | tf_op jit(solution)/shard_map/ppermute | solution.py:152
  24.8 1.7 %copy-start.3 = (f32[3,3,1024]{2,1,0:T(4,128)S(1)}, f32[3,3,1024]{2,1,0:T(4,128)}, u32[]{:S(2)}) copy-start(f32[3,3,1024]{2,1,0:T(4,128)} %param.9) | copy-start | bytes 110596
  24.8 2.3 %copy-start.2 = (f32[16,1024]{1,0:T(8,128)S(1)}, f32[16,1024]{1,0:T(8,128)}, u32[]{:S(2)}) copy-start(f32[16,1024]{1,0:T(8,128)} %param.11) | copy-start | bytes 196612
  24.8 2.9 %copy-start.1 = (f32[16,1024]{1,0:T(8,128)S(1)}, f32[16,1024]{1,0:T(8,128)}, u32[]{:S(2)}) copy-start(f32[16,1024]{1,0:T(8,128)} %param.10) | copy-start | bytes 196612
  24.9 3.6 %copy-start.4 = (f32[7]{0:T(128)S(1)}, f32[7]{0:T(128)}, u32[]{:S(2)}) copy-start(f32[7]{0:T(128)} %constant.48) | copy-start | bytes 88
  24.9 3.6 %copy-start.5 = (f32[7]{0:T(128)S(1)}, f32[7]{0:T(128)}, u32[]{:S(2)}) copy-start(f32[7]{0:T(128)} %constant.47) | copy-start | bytes 88
  26.4 3.2 %collective-permute-start.3 = (bf16[128,2048]{0,1:T(8,128)(2,1)S(1)}, bf16[128,2048]{0,1:T(8,128)(2,1)S(1)}, u32[]{:S(2)}, u32[]{:S(2)}) collective-permute-start(bf16[128,2048]{0,1:T(8,128)(2,1)S(1)} %bitcast.56), channel_id=1, source_target_pairs={{0,4},{4,0},{1,5},{5,1},{2,6},{6,2},{3,7},{7,3},{8,12},{12,8},{9,1... | collective-permute-start | bytes 1572872 | tf_op jit(solution)/shard_map/ppermute | solution.py:145
  105.1 7.1 %copy-start.6 = (bf16[2048,3,1024]{2,0,1:T(8,128)(2,1)S(1)}, bf16[2048,3,1024]{2,0,1:T(8,128)(2,1)}, u32[]{:S(2)}) copy-start(bf16[2048,3,1024]{2,0,1:T(8,128)(2,1)} %all-gather.2.cloned.1.call-done) | copy-start | bytes 37748740
  111.8 3.5 %collective-permute-start.4 = (f32[3,128,1024]{2,1,0:T(8,128)S(1)}, f32[3,128,1024]{2,1,0:T(8,128)S(1)}, u32[]{:S(2)}, u32[]{:S(2)}) collective-permute-start(f32[3,128,1024]{2,1,0:T(8,128)S(1)} %pad_maximum_fusion), channel_id=1, source_target_pairs={{0,4},{4,0},{1,5},{5,1},{2,6},{6,2},{3,7},{7,3},{8,12},{12,8},{9,1... | collective-permute-start | bytes 4718600 | tf_op jit(solution)/shard_map/ppermute | solution.py:145
  115.6 3.5 %copy-start = (bf16[3,128,1024]{2,1,0:T(8,128)(2,1)}, bf16[3,128,1024]{2,1,0:T(8,128)(2,1)S(1)}, u32[]{:S(2)}) copy-start(bf16[3,128,1024]{2,1,0:T(8,128)(2,1)S(1)} %fusion.6.proj_ref) | copy-start | bytes 2359300
  115.7 2.9 %collective-permute-start.5 = (bf16[3,2,1024]{2,1,0:T(2,128)(2,1)S(1)}, bf16[3,2,1024]{2,1,0:T(2,128)(2,1)S(1)}, u32[]{:S(2)}, u32[]{:S(2)}) collective-permute-start(bf16[3,2,1024]{2,1,0:T(2,128)(2,1)S(1)} %slice.48), channel_id=1, source_target_pairs={{0,4},{4,8},{8,12},{12,16},{16,20},{20,24},{24,28},{28,32},{32,36}... | collective-permute-start | bytes 36872 | tf_op jit(solution)/shard_map/ppermute | solution.py:141
Sparse Core Ops, SparseCore 0:
  9.5 92.6 all-gather.1

commit v17 on v16

--- a/solution.py
+++ b/solution.py
@@ -95,28 +95,40 @@
     copies = []
     for r in range(len(digits)):
         mine = [(n, by) for n, (q, by) in enumerate(steps) if q == r]
+        if r + 1 < len(digits):
+            held[r + 1] = held[r]
         for n, by in mine:
             copy = pltpu.make_async_remote_copy(
                 src_ref=held.at[r],
                 dst_ref=slots.at[n],
                 send_sem=send_sem.at[n],
                 recv_sem=recv_sem.at[n],
-                device_id=device((me + by) % peers),
+                device_id=device(jnp.minimum(me + by, peers - 1)),
                 device_id_type=MESH,
             )
-            copy.start()
-            copies.append(copy)
-        grown = held[r]
+
+            @pl.when(me + by < peers)
+            def _():
+                copy.start()
+
+            copies.append((copy, by))
         for n, by in mine:
-            copies[n].wait_recv()
-            got = jnp.where(me >= by, slots[n], 0.0)
-            start_ref[...] += lift_ref[n] * got
-            grown = grown + keep_ref[n] * got
-        if r + 1 < len(digits):
-            held[r + 1] = grown
+            copy = copies[n][0]
+
+            @pl.when(me >= by)
+            def _():
+                copy.wait_recv()
+                got = slots[n]
+                start_ref[...] += lift_ref[n] * got
+                if r + 1 < len(digits):
+                    held[r + 1] = held[r + 1] + keep_ref[n] * got
+
     mixed_kernel(x_ref, taps_ref, decay_ref, resid_ref, skip_ref, start_ref, out_ref)
-    for copy in copies:
-        copy.wait_send()
+    for copy, by in copies:
+
+        @pl.when(me + by < peers)
+        def _():
+            copy.wait_send()
 
 
 def scan_digits(peers):

time: 153 us -> 150 us (0.980)
  the two profiles are of different devices: /device:TPU:0 before, /device:TPU:65 now
where the time goes in v17:
time: 150 us; the launch traced here: 149 us
  waiting for transfers between devices  83.4 us (56%)
  Pallas kernels  22.2 us (15%)
  between operations  13.6 us (9%)
  matrix products  11.7 us (8%)
  starting transfers between devices  8.91 us (6%)
  local copies, waits for them, and re-layouts  5.54 us (4%)
  other arithmetic  3.94 us (3%)
    all_gather x1, waiting for transfers between devices, per_device(): piece = lax.all_gather(in_weight, 'cx', axis=0, tiled=True)  70.8 us
    pallas_call x1, Pallas kernels, per_device(): pl.pallas_call(functools.partial(block_kernel, peers, digits), out_shape=...  22.2 us
    ppermute x3, waiting for transfers between devices, gathered_tp(): lax.ppermute(tokens, 'tp', [(i, (i + by) % peers) for i in range(peers)])  10.3 us
    dot_general x3, matrix products, per_device(): jnp.dot(both[rows:], piece[:, g, :], preferred_element_type=jnp.float32)  9.47 us
    ppermute x3, starting transfers between devices, gathered_tp(): lax.ppermute(tokens, 'tp', [(i, (i + by) % peers) for i in range(peers)])  4.45 us
  transfers between devices with their start and end apart: 7, of which 5 were waited for; matrix products, arithmetic and copies ran while one was open for 6% of the time, Pallas kernels for 0%

profile of v17, /device:TPU:65, one launch (start us, length us, event | category | flops | bytes accessed | tf_op | source)
XLA Modules:
  0.0 149.3 jit_solution(7371966595507246863)
XLA Ops:
  6.5 0.7 all-gather.2.cloned.1.call-update
  7.3 1.4 collective-permute-start
  8.6 1.5 %collective-permute-start.2 = (bf16[128,1024]{1,0:T(8,128)(2,1)}, bf16[128,1024]{1,0:T(8,128)(2,1)S(1)}, u32[]{:S(2)}, u32[]{:S(2)}) collective-permute-start(bf16[128,1024]{1,0:T(8,128)(2,1)} %param.7), channel_id=1, source_target_pairs={{0,3},{1,0},{2,1},{3,2},{4,7},{5,4},{6,5},{7,6},{8,11},{9,8},{10,9... | collective-permute-start | bytes 786440 | tf_op jit(solution)/shard_map/ppermute | solution.py:164
  10.1 1.6 %collective-permute-start.1 = (bf16[128,1024]{1,0:T(8,128)(2,1)}, bf16[128,1024]{1,0:T(8,128)(2,1)S(1)}, u32[]{:S(2)}, u32[]{:S(2)}) collective-permute-start(bf16[128,1024]{1,0:T(8,128)(2,1)} %param.7), channel_id=1, source_target_pairs={{0,2},{1,3},{2,0},{3,1},{4,6},{5,7},{6,4},{7,5},{8,10},{9,11},{10,... | collective-permute-start | bytes 786440 | tf_op jit(solution)/shard_map/ppermute | solution.py:164
  11.7 0.7 sort.17
  12.5 3.6 %collective-permute-done = bf16[128,1024]{1,0:T(8,128)(2,1)S(1)} collective-permute-done((bf16[128,1024]{1,0:T(8,128)(2,1)}, bf16[128,1024]{1,0:T(8,128)(2,1)S(1)}, u32[]{:S(2)}, u32[]{:S(2)}) %collective-permute-start) | collective-permute-done | bytes 262176 | tf_op jit(solution)/shard_map/ppermute | solution.py:164
  16.1 6.7 %collective-permute-done.1 = bf16[128,1024]{1,0:T(8,128)(2,1)S(1)} collective-permute-done((bf16[128,1024]{1,0:T(8,128)(2,1)}, bf16[128,1024]{1,0:T(8,128)(2,1)S(1)}, u32[]{:S(2)}, u32[]{:S(2)}) %collective-permute-start.1) | collective-permute-done | bytes 262176 | tf_op jit(solution)/shard_map/ppermute | solution.py:164
  22.8 1.1 pad_maximum_fusion.1
  24.0 0.6 gather_fusion
  24.6 0.2 select_bitcast_fusion
  24.8 0.7 copy.8
  25.5 1.6 %collective-permute-start.3 = (bf16[128,2048]{0,1:T(8,128)(2,1)S(1)}, bf16[128,2048]{0,1:T(8,128)(2,1)S(1)}, u32[]{:S(2)}, u32[]{:S(2)}) collective-permute-start(bf16[128,2048]{0,1:T(8,128)(2,1)S(1)} %bitcast.56), channel_id=1, source_target_pairs={{0,4},{4,0},{1,5},{5,1},{2,6},{6,2},{3,7},{7,3},{8,12},{12,8},{9,1... | collective-permute-start | bytes 1572872 | tf_op jit(solution)/shard_map/ppermute | solution.py:157
  27.1 0.6 reshape.42.taps_ref
  27.7 0.6 copy.10
  28.4 0.6 copy.9
  29.1 1.1 multiply_exponential_fusion
  30.3 70.8 %all-gather.2.cloned.1.call-done = bf16[2048,3,1024]{2,0,1:T(8,128)(2,1)} async-done(((bf16[128,3,1024]{2,0,1:T(8,128)(2,1)}), bf16[2048,3,1024]{2,0,1:T(8,128)(2,1)}) %all-gather.2.cloned.1.call-update) | async-done | bytes 12582928 | tf_op jit(solution)/shard_map/all_gather | solution.py:178
  101.1 2.9 %fusion.10 = f32[1,128,1024]{2,1,0:T(8,128)S(1)} fusion(bf16[2048,3,1024]{2,0,1:T(8,128)(2,1)} %all-gather.2.cloned.1.call-done, bf16[256,2048]{0,1:T(8,128)(2,1)S(1)} %pad_maximum_fusion.2), kind=kOutput, calls=%fused_computation.16 | convolution fusion | flops 536870912 | bytes 5242880 | tf_op jit(solution)/shard_map/dot_general | solution.py:202
  104.0 3.1 %fusion.8 = f32[1,128,1024]{2,1,0:T(8,128)S(1)} fusion(bf16[2048,3,1024]{2,0,1:T(8,128)(2,1)} %all-gather.2.cloned.1.call-done, bf16[256,2048]{0,1:T(8,128)(2,1)S(1)} %pad_maximum_fusion.2), kind=kOutput, calls=%fused_computation.14 | convolution fusion | flops 536870912 | bytes 5242880 | tf_op jit(solution)/shard_map/dot_general | solution.py:202
  107.1 3.5 %fusion.12 = f32[1,128,1024]{2,1,0:T(8,128)S(1)} fusion(bf16[2048,3,1024]{2,0,1:T(8,128)(2,1)} %all-gather.2.cloned.1.call-done, bf16[256,2048]{0,1:T(8,128)(2,1)S(1)} %pad_maximum_fusion.2), kind=kOutput, calls=%fused_computation.18 | convolution fusion | flops 536870912 | bytes 5242880 | tf_op jit(solution)/shard_map/dot_general | solution.py:202
  110.6 0.2 pad_maximum_fusion
  110.8 0.7 collective-permute-start.4
  111.5 0.7 fusion.9
  112.3 0.8 fusion.7
  113.0 0.8 fusion.11
  113.8 0.8 collective-permute-done.4
  114.5 0.3 fusion.6.proj_ref
  114.9 2.1 %collective-permute-start.5 = (bf16[3,2,1024]{2,1,0:T(2,128)(2,1)S(1)}, bf16[3,2,1024]{2,1,0:T(2,128)(2,1)S(1)}, u32[]{:S(2)}, u32[]{:S(2)}) collective-permute-start(bf16[3,2,1024]{2,1,0:T(2,128)(2,1)S(1)} %slice.48), channel_id=1, source_target_pairs={{0,4},{4,8},{8,12},{12,16},{16,20},{20,24},{24,28},{28,32},{32,36}... | collective-permute-start | bytes 36872 | tf_op jit(solution)/shard_map/ppermute | solution.py:153
  117.1 0.9 collective-permute-done.5
  118.0 0.6 reshape.46.edge_ref
  118.6 22.2 %shard_map.73 = bf16[128,1024]{1,0:T(8,128)(2,1)} custom-call(bf16[3,128,1024]{2,1,0:T(8,128)(2,1)} %copy-done, bf16[3,2,8,128]{3,2,1,0:T(8,128)(2,1)} %reshape.46.edge_ref, f32[3,3,8,128]{3,2,1,0:T(8,128)} %reshape.42.taps_ref, f32[16,8,128]{2,1,0:T(8,128)} %bitcast.58, f32[16,8,128]{2,1,0:T(8,128)} %bitcast.57, f32[8,128]{1,0:T(8,128)} %bitcast.65, ...), custom_call_target="tpu_custom_call" | custom-call | tf_op jit(solution)/shard_map/pallas_call | solution.py:216
  140.8 1.7 %copy.13 = bf16[128,1024]{1,0:T(8,128)(2,1)} copy(bf16[128,1024]{1,0:T(8,128)(2,1)} %shard_map.73) | data formatting | bytes 524288
  (27 shorter events, 0.3 us)
Async XLA Ops:
  6.5 94.5 %all-gather.2.cloned.1.call-start = ((), (), s32[]{:S(2)}) async-start(), calls=%async_computation | async-start | bytes 13369344 | tf_op jit(solution)/shard_map/all_gather | solution.py:178
  7.3 8.8 %collective-permute-start = (bf16[128,1024]{1,0:T(8,128)(2,1)}, bf16[128,1024]{1,0:T(8,128)(2,1)S(1)}, u32[]{:S(2)}, u32[]{:S(2)}) collective-permute-start(bf16[128,1024]{1,0:T(8,128)(2,1)} %param.7), channel_id=1, source_target_pairs={{0,1},{1,2},{2,3},{3,0},{4,5},{5,6},{6,7},{7,4},{8,9},{9,10},{10,1... | collective-permute-start | bytes 786440 | tf_op jit(solution)/shard_map/ppermute | solution.py:164
  8.6 7.4 %collective-permute-start.2 = (bf16[128,1024]{1,0:T(8,128)(2,1)}, bf16[128,1024]{1,0:T(8,128)(2,1)S(1)}, u32[]{:S(2)}, u32[]{:S(2)}) collective-permute-start(bf16[128,1024]{1,0:T(8,128)(2,1)} %param.7), channel_id=1, source_target_pairs={{0,3},{1,0},{2,1},{3,2},{4,7},{5,4},{6,5},{7,6},{8,11},{9,8},{10,9... | collective-permute-start | bytes 786440 | tf_op jit(solution)/shard_map/ppermute | solution.py:164
  10.1 12.6 %collective-permute-start.1 = (bf16[128,1024]{1,0:T(8,128)(2,1)}, bf16[128,1024]{1,0:T(8,128)(2,1)S(1)}, u32[]{:S(2)}, u32[]{:S(2)}) collective-permute-start(bf16[128,1024]{1,0:T(8,128)(2,1)} %param.7), channel_id=1, source_target_pairs={{0,2},{1,3},{2,0},{3,1},{4,6},{5,7},{6,4},{7,5},{8,10},{9,11},{10,... | collective-permute-start | bytes 786440 | tf_op jit(solution)/shard_map/ppermute | solution.py:164
  23.9 3.2 %copy-start.3 = (f32[3,3,1024]{2,1,0:T(4,128)S(1)}, f32[3,3,1024]{2,1,0:T(4,128)}, u32[]{:S(2)}) copy-start(f32[3,3,1024]{2,1,0:T(4,128)} %param.9) | copy-start | bytes 110596
  23.9 3.8 %copy-start.2 = (f32[16,1024]{1,0:T(8,128)S(1)}, f32[16,1024]{1,0:T(8,128)}, u32[]{:S(2)}) copy-start(f32[16,1024]{1,0:T(8,128)} %param.11) | copy-start | bytes 196612
  23.9 4.4 %copy-start.1 = (f32[16,1024]{1,0:T(8,128)S(1)}, f32[16,1024]{1,0:T(8,128)}, u32[]{:S(2)}) copy-start(f32[16,1024]{1,0:T(8,128)} %param.10) | copy-start | bytes 196612
  23.9 5.1 %copy-start.4 = (f32[7]{0:T(128)S(1)}, f32[7]{0:T(128)}, u32[]{:S(2)}) copy-start(f32[7]{0:T(128)} %constant.48) | copy-start | bytes 88
  24.0 5.1 %copy-start.5 = (f32[7]{0:T(128)S(1)}, f32[7]{0:T(128)}, u32[]{:S(2)}) copy-start(f32[7]{0:T(128)} %constant.47) | copy-start | bytes 88
  25.5 4.7 %collective-permute-start.3 = (bf16[128,2048]{0,1:T(8,128)(2,1)S(1)}, bf16[128,2048]{0,1:T(8,128)(2,1)S(1)}, u32[]{:S(2)}, u32[]{:S(2)}) collective-permute-start(bf16[128,2048]{0,1:T(8,128)(2,1)S(1)} %bitcast.56), channel_id=1, source_target_pairs={{0,4},{4,0},{1,5},{5,1},{2,6},{6,2},{3,7},{7,3},{8,12},{12,8},{9,1... | collective-permute-start | bytes 1572872 | tf_op jit(solution)/shard_map/ppermute | solution.py:157
  104.0 7.5 %copy-start.6 = (bf16[2048,3,1024]{2,0,1:T(8,128)(2,1)S(1)}, bf16[2048,3,1024]{2,0,1:T(8,128)(2,1)}, u32[]{:S(2)}) copy-start(bf16[2048,3,1024]{2,0,1:T(8,128)(2,1)} %all-gather.2.cloned.1.call-done) | copy-start | bytes 37748740
  110.8 3.8 %collective-permute-start.4 = (f32[3,128,1024]{2,1,0:T(8,128)S(1)}, f32[3,128,1024]{2,1,0:T(8,128)S(1)}, u32[]{:S(2)}, u32[]{:S(2)}) collective-permute-start(f32[3,128,1024]{2,1,0:T(8,128)S(1)} %pad_maximum_fusion), channel_id=1, source_target_pairs={{0,4},{4,0},{1,5},{5,1},{2,6},{6,2},{3,7},{7,3},{8,12},{12,8},{9,1... | collective-permute-start | bytes 4718600 | tf_op jit(solution)/shard_map/ppermute | solution.py:157
  114.9 3.7 %copy-start = (bf16[3,128,1024]{2,1,0:T(8,128)(2,1)}, bf16[3,128,1024]{2,1,0:T(8,128)(2,1)S(1)}, u32[]{:S(2)}) copy-start(bf16[3,128,1024]{2,1,0:T(8,128)(2,1)S(1)} %fusion.6.proj_ref) | copy-start | bytes 2359300
  114.9 3.1 %collective-permute-start.5 = (bf16[3,2,1024]{2,1,0:T(2,128)(2,1)S(1)}, bf16[3,2,1024]{2,1,0:T(2,128)(2,1)S(1)}, u32[]{:S(2)}, u32[]{:S(2)}) collective-permute-start(bf16[3,2,1024]{2,1,0:T(2,128)(2,1)S(1)} %slice.48), channel_id=1, source_target_pairs={{0,4},{4,8},{8,12},{12,16},{16,20},{20,24},{24,28},{28,32},{32,36}... | collective-permute-start | bytes 36872 | tf_op jit(solution)/shard_map/ppermute | solution.py:153
Sparse Core Ops, SparseCore 0:
  9.5 91.5 all-gather.1
